TPU v7x, 32 devices: a whole 2x2x4 slice. The times are simulated.
32 devices in a mesh: sect: 2 (over core), row: 2 (over y), col: 8 (over z, x).
Axes of the slice: x: 2, y: 2, z: 4, core: 2. Of those that a mesh axis runs over, the one named last changes fastest.
Arguments:
- log_trans: float32 [256, 1024], P('row', 'col'), may hold values from -3 to 3
- corr_len: float32 [2], replicated, may hold values from 1.5 to 3
- taper_width: int32 [2], replicated, may hold values from 1 to 4, as said below
- well_cells: int32 [2, 8], replicated, may hold values from 0 to 262143
- obs_weight: bfloat16 [2, 8, 256, 1024], P('sect', None, 'row', 'col'), may hold values from -0.0048828125 to 0.0048828125
Outputs:
- qh_fields: bfloat16 [2, 8, 256, 1024], P('sect', None, 'row', 'col')
- measure_cov: float32 [16, 16], replicated
Inputs may be any that keep to these rules, and one draw needn't show every extreme that they name: `taper_width`: one of the two widths equals 4.
All inputs are finite; a program needn't handle non-finite values.
Results may differ from a plain program's by a relative error of at most 0.0041.
Values may be sent and summed in bfloat16 or wider, within the bound.
No kernel may reach another device: no remote copies, remote signals or barrier semaphores. Data moves between devices by JAX's collectives and lax.ppermute only.
A program may use at most 64 MiB of HBM per device.

v0:
```python
import jax
import jax.numpy as jnp
from jax import lax
from jax.sharding import PartitionSpec as P

BLOCK = 128
TAPER = 4
SWEEPS = 24


leakage = 0.05


def padded_2(cells, sides, width):
    for axis, dim in sides:
        count = lax.axis_size(axis)
        ends = count - 1
        head = lax.slice_in_dim(cells, 0, width, axis=dim)
        tail = lax.slice_in_dim(cells, cells.shape[dim] - width, cells.shape[dim], axis=dim)
        cells = jnp.concatenate(
            [
                lax.ppermute(tail, axis, [(i, (i + 1) % count) for i in range(ends)]),
                cells,
                lax.ppermute(head, axis, [((i + 1) % count, i) for i in range(ends)]),
            ],
            axis=dim,
        )
    return cells


def passed_along(value, axis, steps):
    count = lax.axis_size(axis)
    initial, last = (max(0, -steps), min(count, count - steps))
    return lax.ppermute(value, axis, [(source, source + steps) for source in range(initial, last)])


def harmonic(left_value, right_value):
    return 2.0 * left_value * right_value / (left_value + right_value)


def covariance_weights(offset_cells, corr_scale, taper_reach):
    distance = jnp.abs(offset_cells).astype(jnp.float32)
    return (
        jnp.exp(-distance / corr_scale) * jnp.maximum(1.0 - distance / taper_reach, 0.0)
    ).astype(jnp.bfloat16)


def interior(values_grid, trim_width):
    return values_grid[..., trim_width:-trim_width, trim_width:-trim_width]


def jacobi_sweep(current, margin, source, face_terms, inside):
    trim_width = 5 - margin
    east_face, west_face, north_face, south_face, diagonal_sum = [
        interior(face_term, trim_width) for face_term in face_terms
    ]
    summed = (
        interior(source, trim_width)
        + east_face * current[:, 1:-1, 2:]
        + west_face * current[:, 1:-1, :-2]
    )
    summed = summed + north_face * current[:, :-2, 1:-1] + south_face * current[:, 2:, 1:-1]
    return jnp.where(interior(inside, trim_width), summed / diagonal_sum, 0.0)


def local(log_trans, corr_len, taper_width, well_cells, obs_weight):
    tile_rows, tile_cols = log_trans.shape
    batch_count, well_count = well_cells.shape
    total_rows = tile_rows * lax.axis_size("row")
    total_cols = tile_cols * lax.axis_size("col")
    row_base = lax.axis_index("row") * tile_rows
    col_base = lax.axis_index("col") * tile_cols
    row_scale = corr_len[0] * (total_rows / 4.0)
    row_reach = (taper_width[0] + TAPER).astype(jnp.float32) * (total_rows / (2.0 * TAPER)) + 1.0
    col_scale = corr_len[1] * BLOCK
    col_reach = (taper_width[1] * BLOCK + 1).astype(jnp.float32)
    widened = padded_2(log_trans, (("row", 0), ("col", 1)), 5)
    conductance = jnp.exp(widened)
    row_global = row_base - 5 + jnp.arange(tile_rows + 10, dtype=jnp.int32)
    col_global = col_base - 5 + jnp.arange(tile_cols + 10, dtype=jnp.int32)
    row_inside = (row_global >= 0) & (row_global < total_rows)
    col_inside = (col_global >= 0) & (col_global < total_cols)
    centre = conductance[1:-1, 1:-1]
    east_face = jnp.where(col_inside[2:][None, :], harmonic(centre, conductance[1:-1, 2:]), centre)
    west_face = jnp.where(
        col_inside[:-2][None, :], harmonic(centre, conductance[1:-1, :-2]), centre
    )
    north_face = jnp.where(
        row_inside[:-2][:, None], harmonic(centre, conductance[:-2, 1:-1]), centre
    )
    south_face = jnp.where(row_inside[2:][:, None], harmonic(centre, conductance[2:, 1:-1]), centre)
    diagonal_sum = east_face + west_face + north_face + south_face + leakage
    face_terms = (east_face, west_face, north_face, south_face, diagonal_sum)
    inside = row_inside[1:-1][:, None] & col_inside[1:-1][None, :]
    own_weight = obs_weight[0]
    state = jnp.zeros((well_count, tile_rows, tile_cols), jnp.float32)
    source = jnp.pad(own_weight.astype(jnp.float32), ((0, 0), (4, 4), (4, 4)))

    def sweep_once(sweep_index, current):
        padded = padded_2(current, (("row", 1), ("col", 2)), 1)
        return jacobi_sweep(padded, 1, source, face_terms, inside)

    state = lax.fori_loop(0, SWEEPS, sweep_once, state)
    adjoint = state.astype(jnp.bfloat16)
    col_local = jnp.arange(tile_cols, dtype=jnp.int32)
    pieces = []
    for offset in range(TAPER, -TAPER - 1, -1):
        if offset == 0:
            pieces.append(adjoint)
        else:
            pieces.append(passed_along(adjoint, "col", offset))
    stacked = jnp.concatenate(pieces, axis=2)
    band_span = stacked.shape[2]
    position = jnp.arange(band_span, dtype=jnp.int32)
    weights = covariance_weights(
        col_local[None, :] + TAPER * tile_cols - position[:, None], col_scale, col_reach
    )
    mixed = jnp.dot(stacked.reshape(-1, band_span), weights, preferred_element_type=jnp.float32)
    mixed = mixed.reshape(adjoint.shape)
    mixed = mixed.astype(jnp.bfloat16)
    row_local = jnp.arange(tile_rows, dtype=jnp.int32)
    segment = lax.all_gather(mixed, "row", axis=1, tiled=True)
    segment_rows = segment.shape[1]
    source_rows = jnp.arange(segment_rows, dtype=jnp.int32)
    weights = covariance_weights(
        row_base + row_local[:, None] - source_rows[None, :], row_scale, row_reach
    )
    qh_fields = jnp.einsum(
        "ik,wkj->wij", weights, segment, preferred_element_type=jnp.float32
    ).astype(jnp.bfloat16)
    all_wells = well_cells.reshape(-1)
    probe_row = all_wells // total_cols
    probe_col = all_wells % total_cols
    hits = (probe_row[:, None, None] == (row_base + row_local)[None, :, None]) & (
        probe_col[:, None, None] == (col_base + col_local)[None, None, :]
    )
    hits = hits.astype(jnp.bfloat16).reshape(all_wells.shape[0], tile_rows * tile_cols)
    sampled = lax.dot_general(
        hits,
        qh_fields.reshape(well_count, tile_rows * tile_cols),
        (((1,), (1,)), ((), ())),
        preferred_element_type=jnp.float32,
    )
    joined = lax.psum(sampled, ("row", "col"))
    measure_cov = lax.all_gather(joined, "sect", axis=1, tiled=True)
    return (qh_fields[None], measure_cov)


def solution(mesh):
    placed = (P("row", "col"), P(), P(), P(), P("sect", None, "row", "col"))
    return jax.shard_map(
        local,
        mesh=mesh,
        in_specs=placed,
        out_specs=(P("sect", None, "row", "col"), P()),
        check_vma=False,
    )
```

profile of v0, /device:TPU:0, one launch (start us, length us, event | category | flops | bytes accessed | tf_op | source)
XLA Modules:
  0.0 814.3 jit_solution(15338494501429233804)
XLA Ops:
  1.5 4.9 collective-permute-start.4
  23.0 698.2 %while.11 = (s32[]{:T(128)}, f32[8,128,128]{1,0,2:T(8,128)S(1)}, pred[136,136]{0,1:T(8,128)(4,1)}, f32[8,136,136]{1,0,2:T(8,128)S(1)}, f32[136,136]{0,1:T(8,128)...) while((s32[]{:T(128)}, f32[8,128,128]{1,0,2:T(8,128)S(1)}, ...), condition=%wide.region_1.2_spmd.clone, body=%wide.region_0.1_spmd.clone.sunk | while | flops 2494531 | bytes 4326991 | solution.py:103
  24.6 4.6 collective-permute-start.1
  29.2 7.9 collective-permute-done
  54.3 4.6 collective-permute-start.1
  58.9 6.6 collective-permute-done
  82.5 4.6 collective-permute-start.1
  87.1 5.2 collective-permute-done
  109.9 4.6 collective-permute-start.1
  114.5 5.2 collective-permute-done
  121.2 4.9 collective-permute-start.2
  137.7 4.6 collective-permute-start.1
  142.3 5.2 collective-permute-done
  149.0 5.4 collective-permute-start.2
  165.9 4.6 collective-permute-start.1
  170.6 5.2 collective-permute-done
  177.3 5.4 collective-permute-start.2
  198.8 5.2 collective-permute-done
  205.6 5.4 collective-permute-start.2
  222.5 4.6 collective-permute-start.1
  227.1 5.2 collective-permute-done
  233.8 5.4 collective-permute-start.2
  255.4 5.2 collective-permute-done
  262.1 5.4 collective-permute-start.2
  279.1 4.6 collective-permute-start.1
  283.7 5.2 collective-permute-done
  290.4 5.4 collective-permute-start.2
  312.0 5.2 collective-permute-done
  318.7 5.4 collective-permute-start.2
  335.6 4.6 collective-permute-start.1
  340.3 5.2 collective-permute-done
  347.0 5.8 collective-permute-start.2
  368.9 6.6 collective-permute-done
  377.3 6.0 collective-permute-start.2
  399.4 8.2 %collective-permute-done = f32[8,1,128]{1,0,2:T(8,128)S(1)} collective-permute-done((f32[8,1,128]{1,0,2:T(8,128)S(1)}, f32[8,1,128]{1,0,2:T(8,128)S(1)}, u32[]{:S(2)}, u32[]{:S(2)}) %collective-permute-start) | collective-permute-done | bytes 4128 | tf_op jit(solution)/shard_map/while/body/eval_jaxpr/ppermute | solution.py:24
  409.4 6.0 collective-permute-start.2
  431.5 9.9 %collective-permute-done = f32[8,1,128]{1,0,2:T(8,128)S(1)} collective-permute-done((f32[8,1,128]{1,0,2:T(8,128)S(1)}, f32[8,1,128]{1,0,2:T(8,128)S(1)}, u32[]{:S(2)}, u32[]{:S(2)}) %collective-permute-start) | collective-permute-done | bytes 4128 | tf_op jit(solution)/shard_map/while/body/eval_jaxpr/ppermute | solution.py:24
  443.3 6.1 collective-permute-start.2
  460.9 4.6 collective-permute-start.1
  465.5 9.9 %collective-permute-done = f32[8,1,128]{1,0,2:T(8,128)S(1)} collective-permute-done((f32[8,1,128]{1,0,2:T(8,128)S(1)}, f32[8,1,128]{1,0,2:T(8,128)S(1)}, u32[]{:S(2)}, u32[]{:S(2)}) %collective-permute-start) | collective-permute-done | bytes 4128 | tf_op jit(solution)/shard_map/while/body/eval_jaxpr/ppermute | solution.py:24
  476.6 5.5 collective-permute-start.2
  498.3 8.4 %collective-permute-done = f32[8,1,128]{1,0,2:T(8,128)S(1)} collective-permute-done((f32[8,1,128]{1,0,2:T(8,128)S(1)}, f32[8,1,128]{1,0,2:T(8,128)S(1)}, u32[]{:S(2)}, u32[]{:S(2)}) %collective-permute-start) | collective-permute-done | bytes 4128 | tf_op jit(solution)/shard_map/while/body/eval_jaxpr/ppermute | solution.py:24
  508.0 4.9 collective-permute-start.2
  529.0 6.8 collective-permute-done
  537.0 4.9 collective-permute-start.2
  558.0 5.2 collective-permute-done
  564.8 5.2 collective-permute-start.2
  586.0 5.2 collective-permute-done
  592.8 5.4 collective-permute-start.2
  614.3 5.2 collective-permute-done
  621.0 5.4 collective-permute-start.2
  638.0 4.6 collective-permute-start.1
  642.6 5.2 collective-permute-done
  649.3 5.4 collective-permute-start.2
  670.9 5.2 collective-permute-done
  677.6 5.4 collective-permute-start.2
  694.6 4.6 collective-permute-start.1
  699.2 5.2 collective-permute-done
  705.9 5.4 collective-permute-start.2
  721.3 7.9 collective-permute-start.8
  753.3 5.4 collective-permute-done.14
  758.7 6.3 collective-permute-done.15
  765.9 7.5 all_gather.6
  774.4 36.6 %psum.7 = f32[16,8]{0,1:T(8,128)S(1)} all-reduce(f32[16,8]{0,1:T(8,128)S(1)} %convolution_bitcast_fusion), channel_id=1, replica_groups=mesh['sect'=2,'row'=2,'col'=8] {'row','col'}, use_global_device_ids=true, to_apply=%region_2.3 | all-reduce | flops 128 | bytes 1024 | tf_op jit(solution)/shard_map/psum | solution.py:144
  (539 shorter events, 423.0 us)
Async XLA Ops:
  1.5 11.3 %collective-permute-start.4 = (f32[5,128]{0,1:T(8,128)S(1)}, f32[5,128]{0,1:T(8,128)S(1)}, u32[]{:S(2)}, u32[]{:S(2)}) collective-permute-start(f32[5,128]{0,1:T(8,128)S(1)} %copy.11), channel_id=1, source_target_pairs={{0,8},{1,9},{2,10},{3,11},{4,12},{5,13},{6,14},{7,15},{16,24},{17,... | collective-permute-start | bytes 7688 | tf_op jit(solution)/shard_map/ppermute | solution.py:22
  23.3 13.8 %collective-permute-start = (f32[8,1,128]{1,0,2:T(8,128)S(1)}, f32[8,1,128]{1,0,2:T(8,128)S(1)}, u32[]{:S(2)}, u32[]{:S(2)}) collective-permute-start(f32[8,1,128]{1,0,2:T(8,128)S(1)} %get-tuple-element.189), channel_id=1, source_target_pairs={{8,0},{9,1},{10,2},{11,3},{12,4},{13,5},{14,6},{15,7},{24,16},{25,... | collective-permute-start | bytes 12296 | tf_op jit(solution)/shard_map/while/body/eval_jaxpr/ppermute | solution.py:24
  24.6 13.8 %collective-permute-start.1 = (f32[8,1,128]{1,0,2:T(8,128)S(1)}, f32[8,1,128]{1,0,2:T(8,128)S(1)}, u32[]{:S(2)}, u32[]{:S(2)}) collective-permute-start(f32[8,1,128]{1,0,2:T(8,128)S(1)} %get-tuple-element.190), channel_id=1, source_target_pairs={{0,8},{1,9},{2,10},{3,11},{4,12},{5,13},{6,14},{7,15},{16,24},{17,... | collective-permute-start | bytes 12296 | tf_op jit(solution)/shard_map/while/body/eval_jaxpr/ppermute | solution.py:22
  38.4 11.5 %collective-permute-start.2 = (f32[8,130,1]{1,0,2:T(8,128)S(1)}, f32[8,130,1]{1,0,2:T(8,128)S(1)}, u32[]{:S(2)}, u32[]{:S(2)}) collective-permute-start(f32[8,130,1]{1,0,2:T(8,128)S(1)} %get-tuple-element.191), channel_id=1, source_target_pairs={{0,1},{1,2},{2,3},{3,4},{4,5},{5,6},{6,7},{8,9},{9,10},{10,11},{11... | collective-permute-start | bytes 12488 | tf_op jit(solution)/shard_map/while/body/eval_jaxpr/ppermute | solution.py:22
  53.0 12.5 %collective-permute-start = (f32[8,1,128]{1,0,2:T(8,128)S(1)}, f32[8,1,128]{1,0,2:T(8,128)S(1)}, u32[]{:S(2)}, u32[]{:S(2)}) collective-permute-start(f32[8,1,128]{1,0,2:T(8,128)S(1)} %get-tuple-element.189), channel_id=1, source_target_pairs={{8,0},{9,1},{10,2},{11,3},{12,4},{13,5},{14,6},{15,7},{24,16},{25,... | collective-permute-start | bytes 12296 | tf_op jit(solution)/shard_map/while/body/eval_jaxpr/ppermute | solution.py:24
  54.3 12.4 %collective-permute-start.1 = (f32[8,1,128]{1,0,2:T(8,128)S(1)}, f32[8,1,128]{1,0,2:T(8,128)S(1)}, u32[]{:S(2)}, u32[]{:S(2)}) collective-permute-start(f32[8,1,128]{1,0,2:T(8,128)S(1)} %get-tuple-element.190), channel_id=1, source_target_pairs={{0,8},{1,9},{2,10},{3,11},{4,12},{5,13},{6,14},{7,15},{16,24},{17,... | collective-permute-start | bytes 12296 | tf_op jit(solution)/shard_map/while/body/eval_jaxpr/ppermute | solution.py:22
  66.7 11.4 %collective-permute-start.2 = (f32[8,130,1]{1,0,2:T(8,128)S(1)}, f32[8,130,1]{1,0,2:T(8,128)S(1)}, u32[]{:S(2)}, u32[]{:S(2)}) collective-permute-start(f32[8,130,1]{1,0,2:T(8,128)S(1)} %get-tuple-element.191), channel_id=1, source_target_pairs={{0,1},{1,2},{2,3},{3,4},{4,5},{5,6},{6,7},{8,9},{9,10},{10,11},{11... | collective-permute-start | bytes 12488 | tf_op jit(solution)/shard_map/while/body/eval_jaxpr/ppermute | solution.py:22
  81.2 11.1 %collective-permute-start = (f32[8,1,128]{1,0,2:T(8,128)S(1)}, f32[8,1,128]{1,0,2:T(8,128)S(1)}, u32[]{:S(2)}, u32[]{:S(2)}) collective-permute-start(f32[8,1,128]{1,0,2:T(8,128)S(1)} %get-tuple-element.189), channel_id=1, source_target_pairs={{8,0},{9,1},{10,2},{11,3},{12,4},{13,5},{14,6},{15,7},{24,16},{25,... | collective-permute-start | bytes 12296 | tf_op jit(solution)/shard_map/while/body/eval_jaxpr/ppermute | solution.py:24
  82.5 11.3 %collective-permute-start.1 = (f32[8,1,128]{1,0,2:T(8,128)S(1)}, f32[8,1,128]{1,0,2:T(8,128)S(1)}, u32[]{:S(2)}, u32[]{:S(2)}) collective-permute-start(f32[8,1,128]{1,0,2:T(8,128)S(1)} %get-tuple-element.190), channel_id=1, source_target_pairs={{0,8},{1,9},{2,10},{3,11},{4,12},{5,13},{6,14},{7,15},{16,24},{17,... | collective-permute-start | bytes 12296 | tf_op jit(solution)/shard_map/while/body/eval_jaxpr/ppermute | solution.py:22
  93.8 11.7 %collective-permute-start.2 = (f32[8,130,1]{1,0,2:T(8,128)S(1)}, f32[8,130,1]{1,0,2:T(8,128)S(1)}, u32[]{:S(2)}, u32[]{:S(2)}) collective-permute-start(f32[8,130,1]{1,0,2:T(8,128)S(1)} %get-tuple-element.191), channel_id=1, source_target_pairs={{0,1},{1,2},{2,3},{3,4},{4,5},{5,6},{6,7},{8,9},{9,10},{10,11},{11... | collective-permute-start | bytes 12488 | tf_op jit(solution)/shard_map/while/body/eval_jaxpr/ppermute | solution.py:22
  108.6 11.1 %collective-permute-start = (f32[8,1,128]{1,0,2:T(8,128)S(1)}, f32[8,1,128]{1,0,2:T(8,128)S(1)}, u32[]{:S(2)}, u32[]{:S(2)}) collective-permute-start(f32[8,1,128]{1,0,2:T(8,128)S(1)} %get-tuple-element.189), channel_id=1, source_target_pairs={{8,0},{9,1},{10,2},{11,3},{12,4},{13,5},{14,6},{15,7},{24,16},{25,... | collective-permute-start | bytes 12296 | tf_op jit(solution)/shard_map/while/body/eval_jaxpr/ppermute | solution.py:24
  109.9 11.3 %collective-permute-start.1 = (f32[8,1,128]{1,0,2:T(8,128)S(1)}, f32[8,1,128]{1,0,2:T(8,128)S(1)}, u32[]{:S(2)}, u32[]{:S(2)}) collective-permute-start(f32[8,1,128]{1,0,2:T(8,128)S(1)} %get-tuple-element.190), channel_id=1, source_target_pairs={{0,8},{1,9},{2,10},{3,11},{4,12},{5,13},{6,14},{7,15},{16,24},{17,... | collective-permute-start | bytes 12296 | tf_op jit(solution)/shard_map/while/body/eval_jaxpr/ppermute | solution.py:22
  121.2 12.1 %collective-permute-start.2 = (f32[8,130,1]{1,0,2:T(8,128)S(1)}, f32[8,130,1]{1,0,2:T(8,128)S(1)}, u32[]{:S(2)}, u32[]{:S(2)}) collective-permute-start(f32[8,130,1]{1,0,2:T(8,128)S(1)} %get-tuple-element.191), channel_id=1, source_target_pairs={{0,1},{1,2},{2,3},{3,4},{4,5},{5,6},{6,7},{8,9},{9,10},{10,11},{11... | collective-permute-start | bytes 12488 | tf_op jit(solution)/shard_map/while/body/eval_jaxpr/ppermute | solution.py:22
  137.7 11.3 %collective-permute-start.1 = (f32[8,1,128]{1,0,2:T(8,128)S(1)}, f32[8,1,128]{1,0,2:T(8,128)S(1)}, u32[]{:S(2)}, u32[]{:S(2)}) collective-permute-start(f32[8,1,128]{1,0,2:T(8,128)S(1)} %get-tuple-element.190), channel_id=1, source_target_pairs={{0,8},{1,9},{2,10},{3,11},{4,12},{5,13},{6,14},{7,15},{16,24},{17,... | collective-permute-start | bytes 12296 | tf_op jit(solution)/shard_map/while/body/eval_jaxpr/ppermute | solution.py:22
  149.0 12.6 %collective-permute-start.2 = (f32[8,130,1]{1,0,2:T(8,128)S(1)}, f32[8,130,1]{1,0,2:T(8,128)S(1)}, u32[]{:S(2)}, u32[]{:S(2)}) collective-permute-start(f32[8,130,1]{1,0,2:T(8,128)S(1)} %get-tuple-element.191), channel_id=1, source_target_pairs={{0,1},{1,2},{2,3},{3,4},{4,5},{5,6},{6,7},{8,9},{9,10},{10,11},{11... | collective-permute-start | bytes 12488 | tf_op jit(solution)/shard_map/while/body/eval_jaxpr/ppermute | solution.py:22
  165.9 11.3 %collective-permute-start.1 = (f32[8,1,128]{1,0,2:T(8,128)S(1)}, f32[8,1,128]{1,0,2:T(8,128)S(1)}, u32[]{:S(2)}, u32[]{:S(2)}) collective-permute-start(f32[8,1,128]{1,0,2:T(8,128)S(1)} %get-tuple-element.190), channel_id=1, source_target_pairs={{0,8},{1,9},{2,10},{3,11},{4,12},{5,13},{6,14},{7,15},{16,24},{17,... | collective-permute-start | bytes 12296 | tf_op jit(solution)/shard_map/while/body/eval_jaxpr/ppermute | solution.py:22
  177.3 12.6 %collective-permute-start.2 = (f32[8,130,1]{1,0,2:T(8,128)S(1)}, f32[8,130,1]{1,0,2:T(8,128)S(1)}, u32[]{:S(2)}, u32[]{:S(2)}) collective-permute-start(f32[8,130,1]{1,0,2:T(8,128)S(1)} %get-tuple-element.191), channel_id=1, source_target_pairs={{0,1},{1,2},{2,3},{3,4},{4,5},{5,6},{6,7},{8,9},{9,10},{10,11},{11... | collective-permute-start | bytes 12488 | tf_op jit(solution)/shard_map/while/body/eval_jaxpr/ppermute | solution.py:22
  194.2 11.3 %collective-permute-start.1 = (f32[8,1,128]{1,0,2:T(8,128)S(1)}, f32[8,1,128]{1,0,2:T(8,128)S(1)}, u32[]{:S(2)}, u32[]{:S(2)}) collective-permute-start(f32[8,1,128]{1,0,2:T(8,128)S(1)} %get-tuple-element.190), channel_id=1, source_target_pairs={{0,8},{1,9},{2,10},{3,11},{4,12},{5,13},{6,14},{7,15},{16,24},{17,... | collective-permute-start | bytes 12296 | tf_op jit(solution)/shard_map/while/body/eval_jaxpr/ppermute | solution.py:22
  205.6 12.6 %collective-permute-start.2 = (f32[8,130,1]{1,0,2:T(8,128)S(1)}, f32[8,130,1]{1,0,2:T(8,128)S(1)}, u32[]{:S(2)}, u32[]{:S(2)}) collective-permute-start(f32[8,130,1]{1,0,2:T(8,128)S(1)} %get-tuple-element.191), channel_id=1, source_target_pairs={{0,1},{1,2},{2,3},{3,4},{4,5},{5,6},{6,7},{8,9},{9,10},{10,11},{11... | collective-permute-start | bytes 12488 | tf_op jit(solution)/shard_map/while/body/eval_jaxpr/ppermute | solution.py:22
  222.5 11.3 %collective-permute-start.1 = (f32[8,1,128]{1,0,2:T(8,128)S(1)}, f32[8,1,128]{1,0,2:T(8,128)S(1)}, u32[]{:S(2)}, u32[]{:S(2)}) collective-permute-start(f32[8,1,128]{1,0,2:T(8,128)S(1)} %get-tuple-element.190), channel_id=1, source_target_pairs={{0,8},{1,9},{2,10},{3,11},{4,12},{5,13},{6,14},{7,15},{16,24},{17,... | collective-permute-start | bytes 12296 | tf_op jit(solution)/shard_map/while/body/eval_jaxpr/ppermute | solution.py:22
  233.8 12.6 %collective-permute-start.2 = (f32[8,130,1]{1,0,2:T(8,128)S(1)}, f32[8,130,1]{1,0,2:T(8,128)S(1)}, u32[]{:S(2)}, u32[]{:S(2)}) collective-permute-start(f32[8,130,1]{1,0,2:T(8,128)S(1)} %get-tuple-element.191), channel_id=1, source_target_pairs={{0,1},{1,2},{2,3},{3,4},{4,5},{5,6},{6,7},{8,9},{9,10},{10,11},{11... | collective-permute-start | bytes 12488 | tf_op jit(solution)/shard_map/while/body/eval_jaxpr/ppermute | solution.py:22
  250.8 11.3 %collective-permute-start.1 = (f32[8,1,128]{1,0,2:T(8,128)S(1)}, f32[8,1,128]{1,0,2:T(8,128)S(1)}, u32[]{:S(2)}, u32[]{:S(2)}) collective-permute-start(f32[8,1,128]{1,0,2:T(8,128)S(1)} %get-tuple-element.190), channel_id=1, source_target_pairs={{0,8},{1,9},{2,10},{3,11},{4,12},{5,13},{6,14},{7,15},{16,24},{17,... | collective-permute-start | bytes 12296 | tf_op jit(solution)/shard_map/while/body/eval_jaxpr/ppermute | solution.py:22
  262.1 12.6 %collective-permute-start.2 = (f32[8,130,1]{1,0,2:T(8,128)S(1)}, f32[8,130,1]{1,0,2:T(8,128)S(1)}, u32[]{:S(2)}, u32[]{:S(2)}) collective-permute-start(f32[8,130,1]{1,0,2:T(8,128)S(1)} %get-tuple-element.191), channel_id=1, source_target_pairs={{0,1},{1,2},{2,3},{3,4},{4,5},{5,6},{6,7},{8,9},{9,10},{10,11},{11... | collective-permute-start | bytes 12488 | tf_op jit(solution)/shard_map/while/body/eval_jaxpr/ppermute | solution.py:22
  279.1 11.3 %collective-permute-start.1 = (f32[8,1,128]{1,0,2:T(8,128)S(1)}, f32[8,1,128]{1,0,2:T(8,128)S(1)}, u32[]{:S(2)}, u32[]{:S(2)}) collective-permute-start(f32[8,1,128]{1,0,2:T(8,128)S(1)} %get-tuple-element.190), channel_id=1, source_target_pairs={{0,8},{1,9},{2,10},{3,11},{4,12},{5,13},{6,14},{7,15},{16,24},{17,... | collective-permute-start | bytes 12296 | tf_op jit(solution)/shard_map/while/body/eval_jaxpr/ppermute | solution.py:22
  290.4 12.6 %collective-permute-start.2 = (f32[8,130,1]{1,0,2:T(8,128)S(1)}, f32[8,130,1]{1,0,2:T(8,128)S(1)}, u32[]{:S(2)}, u32[]{:S(2)}) collective-permute-start(f32[8,130,1]{1,0,2:T(8,128)S(1)} %get-tuple-element.191), channel_id=1, source_target_pairs={{0,1},{1,2},{2,3},{3,4},{4,5},{5,6},{6,7},{8,9},{9,10},{10,11},{11... | collective-permute-start | bytes 12488 | tf_op jit(solution)/shard_map/while/body/eval_jaxpr/ppermute | solution.py:22
  307.4 11.3 %collective-permute-start.1 = (f32[8,1,128]{1,0,2:T(8,128)S(1)}, f32[8,1,128]{1,0,2:T(8,128)S(1)}, u32[]{:S(2)}, u32[]{:S(2)}) collective-permute-start(f32[8,1,128]{1,0,2:T(8,128)S(1)} %get-tuple-element.190), channel_id=1, source_target_pairs={{0,8},{1,9},{2,10},{3,11},{4,12},{5,13},{6,14},{7,15},{16,24},{17,... | collective-permute-start | bytes 12296 | tf_op jit(solution)/shard_map/while/body/eval_jaxpr/ppermute | solution.py:22
  318.7 12.6 %collective-permute-start.2 = (f32[8,130,1]{1,0,2:T(8,128)S(1)}, f32[8,130,1]{1,0,2:T(8,128)S(1)}, u32[]{:S(2)}, u32[]{:S(2)}) collective-permute-start(f32[8,130,1]{1,0,2:T(8,128)S(1)} %get-tuple-element.191), channel_id=1, source_target_pairs={{0,1},{1,2},{2,3},{3,4},{4,5},{5,6},{6,7},{8,9},{9,10},{10,11},{11... | collective-permute-start | bytes 12488 | tf_op jit(solution)/shard_map/while/body/eval_jaxpr/ppermute | solution.py:22
  335.6 11.3 %collective-permute-start.1 = (f32[8,1,128]{1,0,2:T(8,128)S(1)}, f32[8,1,128]{1,0,2:T(8,128)S(1)}, u32[]{:S(2)}, u32[]{:S(2)}) collective-permute-start(f32[8,1,128]{1,0,2:T(8,128)S(1)} %get-tuple-element.190), channel_id=1, source_target_pairs={{0,8},{1,9},{2,10},{3,11},{4,12},{5,13},{6,14},{7,15},{16,24},{17,... | collective-permute-start | bytes 12296 | tf_op jit(solution)/shard_map/while/body/eval_jaxpr/ppermute | solution.py:22
  347.0 12.9 %collective-permute-start.2 = (f32[8,130,1]{1,0,2:T(8,128)S(1)}, f32[8,130,1]{1,0,2:T(8,128)S(1)}, u32[]{:S(2)}, u32[]{:S(2)}) collective-permute-start(f32[8,130,1]{1,0,2:T(8,128)S(1)} %get-tuple-element.191), channel_id=1, source_target_pairs={{0,1},{1,2},{2,3},{3,4},{4,5},{5,6},{6,7},{8,9},{9,10},{10,11},{11... | collective-permute-start | bytes 12488 | tf_op jit(solution)/shard_map/while/body/eval_jaxpr/ppermute | solution.py:22
  363.0 12.5 %collective-permute-start = (f32[8,1,128]{1,0,2:T(8,128)S(1)}, f32[8,1,128]{1,0,2:T(8,128)S(1)}, u32[]{:S(2)}, u32[]{:S(2)}) collective-permute-start(f32[8,1,128]{1,0,2:T(8,128)S(1)} %get-tuple-element.189), channel_id=1, source_target_pairs={{8,0},{9,1},{10,2},{11,3},{12,4},{13,5},{14,6},{15,7},{24,16},{25,... | collective-permute-start | bytes 12296 | tf_op jit(solution)/shard_map/while/body/eval_jaxpr/ppermute | solution.py:24
  364.3 12.9 %collective-permute-start.1 = (f32[8,1,128]{1,0,2:T(8,128)S(1)}, f32[8,1,128]{1,0,2:T(8,128)S(1)}, u32[]{:S(2)}, u32[]{:S(2)}) collective-permute-start(f32[8,1,128]{1,0,2:T(8,128)S(1)} %get-tuple-element.190), channel_id=1, source_target_pairs={{0,8},{1,9},{2,10},{3,11},{4,12},{5,13},{6,14},{7,15},{16,24},{17,... | collective-permute-start | bytes 12296 | tf_op jit(solution)/shard_map/while/body/eval_jaxpr/ppermute | solution.py:22
  377.3 13.1 %collective-permute-start.2 = (f32[8,130,1]{1,0,2:T(8,128)S(1)}, f32[8,130,1]{1,0,2:T(8,128)S(1)}, u32[]{:S(2)}, u32[]{:S(2)}) collective-permute-start(f32[8,130,1]{1,0,2:T(8,128)S(1)} %get-tuple-element.191), channel_id=1, source_target_pairs={{0,1},{1,2},{2,3},{3,4},{4,5},{5,6},{6,7},{8,9},{9,10},{10,11},{11... | collective-permute-start | bytes 12488 | tf_op jit(solution)/shard_map/while/body/eval_jaxpr/ppermute | solution.py:22
  393.5 14.1 %collective-permute-start = (f32[8,1,128]{1,0,2:T(8,128)S(1)}, f32[8,1,128]{1,0,2:T(8,128)S(1)}, u32[]{:S(2)}, u32[]{:S(2)}) collective-permute-start(f32[8,1,128]{1,0,2:T(8,128)S(1)} %get-tuple-element.189), channel_id=1, source_target_pairs={{8,0},{9,1},{10,2},{11,3},{12,4},{13,5},{14,6},{15,7},{24,16},{25,... | collective-permute-start | bytes 12296 | tf_op jit(solution)/shard_map/while/body/eval_jaxpr/ppermute | solution.py:24
  394.8 14.6 %collective-permute-start.1 = (f32[8,1,128]{1,0,2:T(8,128)S(1)}, f32[8,1,128]{1,0,2:T(8,128)S(1)}, u32[]{:S(2)}, u32[]{:S(2)}) collective-permute-start(f32[8,1,128]{1,0,2:T(8,128)S(1)} %get-tuple-element.190), channel_id=1, source_target_pairs={{0,8},{1,9},{2,10},{3,11},{4,12},{5,13},{6,14},{7,15},{16,24},{17,... | collective-permute-start | bytes 12296 | tf_op jit(solution)/shard_map/while/body/eval_jaxpr/ppermute | solution.py:22
  409.4 13.1 %collective-permute-start.2 = (f32[8,130,1]{1,0,2:T(8,128)S(1)}, f32[8,130,1]{1,0,2:T(8,128)S(1)}, u32[]{:S(2)}, u32[]{:S(2)}) collective-permute-start(f32[8,130,1]{1,0,2:T(8,128)S(1)} %get-tuple-element.191), channel_id=1, source_target_pairs={{0,1},{1,2},{2,3},{3,4},{4,5},{5,6},{6,7},{8,9},{9,10},{10,11},{11... | collective-permute-start | bytes 12488 | tf_op jit(solution)/shard_map/while/body/eval_jaxpr/ppermute | solution.py:22
  425.6 15.8 %collective-permute-start = (f32[8,1,128]{1,0,2:T(8,128)S(1)}, f32[8,1,128]{1,0,2:T(8,128)S(1)}, u32[]{:S(2)}, u32[]{:S(2)}) collective-permute-start(f32[8,1,128]{1,0,2:T(8,128)S(1)} %get-tuple-element.189), channel_id=1, source_target_pairs={{8,0},{9,1},{10,2},{11,3},{12,4},{13,5},{14,6},{15,7},{24,16},{25,... | collective-permute-start | bytes 12296 | tf_op jit(solution)/shard_map/while/body/eval_jaxpr/ppermute | solution.py:24
  426.9 16.3 %collective-permute-start.1 = (f32[8,1,128]{1,0,2:T(8,128)S(1)}, f32[8,1,128]{1,0,2:T(8,128)S(1)}, u32[]{:S(2)}, u32[]{:S(2)}) collective-permute-start(f32[8,1,128]{1,0,2:T(8,128)S(1)} %get-tuple-element.190), channel_id=1, source_target_pairs={{0,8},{1,9},{2,10},{3,11},{4,12},{5,13},{6,14},{7,15},{16,24},{17,... | collective-permute-start | bytes 12296 | tf_op jit(solution)/shard_map/while/body/eval_jaxpr/ppermute | solution.py:22
  443.3 13.2 %collective-permute-start.2 = (f32[8,130,1]{1,0,2:T(8,128)S(1)}, f32[8,130,1]{1,0,2:T(8,128)S(1)}, u32[]{:S(2)}, u32[]{:S(2)}) collective-permute-start(f32[8,130,1]{1,0,2:T(8,128)S(1)} %get-tuple-element.191), channel_id=1, source_target_pairs={{0,1},{1,2},{2,3},{3,4},{4,5},{5,6},{6,7},{8,9},{9,10},{10,11},{11... | collective-permute-start | bytes 12488 | tf_op jit(solution)/shard_map/while/body/eval_jaxpr/ppermute | solution.py:22
  459.6 15.8 %collective-permute-start = (f32[8,1,128]{1,0,2:T(8,128)S(1)}, f32[8,1,128]{1,0,2:T(8,128)S(1)}, u32[]{:S(2)}, u32[]{:S(2)}) collective-permute-start(f32[8,1,128]{1,0,2:T(8,128)S(1)} %get-tuple-element.189), channel_id=1, source_target_pairs={{8,0},{9,1},{10,2},{11,3},{12,4},{13,5},{14,6},{15,7},{24,16},{25,... | collective-permute-start | bytes 12296 | tf_op jit(solution)/shard_map/while/body/eval_jaxpr/ppermute | solution.py:24
  460.9 15.7 %collective-permute-start.1 = (f32[8,1,128]{1,0,2:T(8,128)S(1)}, f32[8,1,128]{1,0,2:T(8,128)S(1)}, u32[]{:S(2)}, u32[]{:S(2)}) collective-permute-start(f32[8,1,128]{1,0,2:T(8,128)S(1)} %get-tuple-element.190), channel_id=1, source_target_pairs={{0,8},{1,9},{2,10},{3,11},{4,12},{5,13},{6,14},{7,15},{16,24},{17,... | collective-permute-start | bytes 12296 | tf_op jit(solution)/shard_map/while/body/eval_jaxpr/ppermute | solution.py:22
  476.6 12.6 %collective-permute-start.2 = (f32[8,130,1]{1,0,2:T(8,128)S(1)}, f32[8,130,1]{1,0,2:T(8,128)S(1)}, u32[]{:S(2)}, u32[]{:S(2)}) collective-permute-start(f32[8,130,1]{1,0,2:T(8,128)S(1)} %get-tuple-element.191), channel_id=1, source_target_pairs={{0,1},{1,2},{2,3},{3,4},{4,5},{5,6},{6,7},{8,9},{9,10},{10,11},{11... | collective-permute-start | bytes 12488 | tf_op jit(solution)/shard_map/while/body/eval_jaxpr/ppermute | solution.py:22
  492.4 14.4 %collective-permute-start = (f32[8,1,128]{1,0,2:T(8,128)S(1)}, f32[8,1,128]{1,0,2:T(8,128)S(1)}, u32[]{:S(2)}, u32[]{:S(2)}) collective-permute-start(f32[8,1,128]{1,0,2:T(8,128)S(1)} %get-tuple-element.189), channel_id=1, source_target_pairs={{8,0},{9,1},{10,2},{11,3},{12,4},{13,5},{14,6},{15,7},{24,16},{25,... | collective-permute-start | bytes 12296 | tf_op jit(solution)/shard_map/while/body/eval_jaxpr/ppermute | solution.py:24
  493.6 14.3 %collective-permute-start.1 = (f32[8,1,128]{1,0,2:T(8,128)S(1)}, f32[8,1,128]{1,0,2:T(8,128)S(1)}, u32[]{:S(2)}, u32[]{:S(2)}) collective-permute-start(f32[8,1,128]{1,0,2:T(8,128)S(1)} %get-tuple-element.190), channel_id=1, source_target_pairs={{0,8},{1,9},{2,10},{3,11},{4,12},{5,13},{6,14},{7,15},{16,24},{17,... | collective-permute-start | bytes 12296 | tf_op jit(solution)/shard_map/while/body/eval_jaxpr/ppermute | solution.py:22
  508.0 12.0 %collective-permute-start.2 = (f32[8,130,1]{1,0,2:T(8,128)S(1)}, f32[8,130,1]{1,0,2:T(8,128)S(1)}, u32[]{:S(2)}, u32[]{:S(2)}) collective-permute-start(f32[8,130,1]{1,0,2:T(8,128)S(1)} %get-tuple-element.191), channel_id=1, source_target_pairs={{0,1},{1,2},{2,3},{3,4},{4,5},{5,6},{6,7},{8,9},{9,10},{10,11},{11... | collective-permute-start | bytes 12488 | tf_op jit(solution)/shard_map/while/body/eval_jaxpr/ppermute | solution.py:22
  523.1 12.7 %collective-permute-start = (f32[8,1,128]{1,0,2:T(8,128)S(1)}, f32[8,1,128]{1,0,2:T(8,128)S(1)}, u32[]{:S(2)}, u32[]{:S(2)}) collective-permute-start(f32[8,1,128]{1,0,2:T(8,128)S(1)} %get-tuple-element.189), channel_id=1, source_target_pairs={{8,0},{9,1},{10,2},{11,3},{12,4},{13,5},{14,6},{15,7},{24,16},{25,... | collective-permute-start | bytes 12296 | tf_op jit(solution)/shard_map/while/body/eval_jaxpr/ppermute | solution.py:24
  524.4 12.6 %collective-permute-start.1 = (f32[8,1,128]{1,0,2:T(8,128)S(1)}, f32[8,1,128]{1,0,2:T(8,128)S(1)}, u32[]{:S(2)}, u32[]{:S(2)}) collective-permute-start(f32[8,1,128]{1,0,2:T(8,128)S(1)} %get-tuple-element.190), channel_id=1, source_target_pairs={{0,8},{1,9},{2,10},{3,11},{4,12},{5,13},{6,14},{7,15},{16,24},{17,... | collective-permute-start | bytes 12296 | tf_op jit(solution)/shard_map/while/body/eval_jaxpr/ppermute | solution.py:22
  537.0 12.0 %collective-permute-start.2 = (f32[8,130,1]{1,0,2:T(8,128)S(1)}, f32[8,130,1]{1,0,2:T(8,128)S(1)}, u32[]{:S(2)}, u32[]{:S(2)}) collective-permute-start(f32[8,130,1]{1,0,2:T(8,128)S(1)} %get-tuple-element.191), channel_id=1, source_target_pairs={{0,1},{1,2},{2,3},{3,4},{4,5},{5,6},{6,7},{8,9},{9,10},{10,11},{11... | collective-permute-start | bytes 12488 | tf_op jit(solution)/shard_map/while/body/eval_jaxpr/ppermute | solution.py:22
  553.4 11.3 %collective-permute-start.1 = (f32[8,1,128]{1,0,2:T(8,128)S(1)}, f32[8,1,128]{1,0,2:T(8,128)S(1)}, u32[]{:S(2)}, u32[]{:S(2)}) collective-permute-start(f32[8,1,128]{1,0,2:T(8,128)S(1)} %get-tuple-element.190), channel_id=1, source_target_pairs={{0,8},{1,9},{2,10},{3,11},{4,12},{5,13},{6,14},{7,15},{16,24},{17,... | collective-permute-start | bytes 12296 | tf_op jit(solution)/shard_map/while/body/eval_jaxpr/ppermute | solution.py:22
  564.8 12.3 %collective-permute-start.2 = (f32[8,130,1]{1,0,2:T(8,128)S(1)}, f32[8,130,1]{1,0,2:T(8,128)S(1)}, u32[]{:S(2)}, u32[]{:S(2)}) collective-permute-start(f32[8,130,1]{1,0,2:T(8,128)S(1)} %get-tuple-element.191), channel_id=1, source_target_pairs={{0,1},{1,2},{2,3},{3,4},{4,5},{5,6},{6,7},{8,9},{9,10},{10,11},{11... | collective-permute-start | bytes 12488 | tf_op jit(solution)/shard_map/while/body/eval_jaxpr/ppermute | solution.py:22
  581.4 11.3 %collective-permute-start.1 = (f32[8,1,128]{1,0,2:T(8,128)S(1)}, f32[8,1,128]{1,0,2:T(8,128)S(1)}, u32[]{:S(2)}, u32[]{:S(2)}) collective-permute-start(f32[8,1,128]{1,0,2:T(8,128)S(1)} %get-tuple-element.190), channel_id=1, source_target_pairs={{0,8},{1,9},{2,10},{3,11},{4,12},{5,13},{6,14},{7,15},{16,24},{17,... | collective-permute-start | bytes 12296 | tf_op jit(solution)/shard_map/while/body/eval_jaxpr/ppermute | solution.py:22
  592.8 12.6 %collective-permute-start.2 = (f32[8,130,1]{1,0,2:T(8,128)S(1)}, f32[8,130,1]{1,0,2:T(8,128)S(1)}, u32[]{:S(2)}, u32[]{:S(2)}) collective-permute-start(f32[8,130,1]{1,0,2:T(8,128)S(1)} %get-tuple-element.191), channel_id=1, source_target_pairs={{0,1},{1,2},{2,3},{3,4},{4,5},{5,6},{6,7},{8,9},{9,10},{10,11},{11... | collective-permute-start | bytes 12488 | tf_op jit(solution)/shard_map/while/body/eval_jaxpr/ppermute | solution.py:22
  609.7 11.3 %collective-permute-start.1 = (f32[8,1,128]{1,0,2:T(8,128)S(1)}, f32[8,1,128]{1,0,2:T(8,128)S(1)}, u32[]{:S(2)}, u32[]{:S(2)}) collective-permute-start(f32[8,1,128]{1,0,2:T(8,128)S(1)} %get-tuple-element.190), channel_id=1, source_target_pairs={{0,8},{1,9},{2,10},{3,11},{4,12},{5,13},{6,14},{7,15},{16,24},{17,... | collective-permute-start | bytes 12296 | tf_op jit(solution)/shard_map/while/body/eval_jaxpr/ppermute | solution.py:22
  621.0 12.6 %collective-permute-start.2 = (f32[8,130,1]{1,0,2:T(8,128)S(1)}, f32[8,130,1]{1,0,2:T(8,128)S(1)}, u32[]{:S(2)}, u32[]{:S(2)}) collective-permute-start(f32[8,130,1]{1,0,2:T(8,128)S(1)} %get-tuple-element.191), channel_id=1, source_target_pairs={{0,1},{1,2},{2,3},{3,4},{4,5},{5,6},{6,7},{8,9},{9,10},{10,11},{11... | collective-permute-start | bytes 12488 | tf_op jit(solution)/shard_map/while/body/eval_jaxpr/ppermute | solution.py:22
  638.0 11.3 %collective-permute-start.1 = (f32[8,1,128]{1,0,2:T(8,128)S(1)}, f32[8,1,128]{1,0,2:T(8,128)S(1)}, u32[]{:S(2)}, u32[]{:S(2)}) collective-permute-start(f32[8,1,128]{1,0,2:T(8,128)S(1)} %get-tuple-element.190), channel_id=1, source_target_pairs={{0,8},{1,9},{2,10},{3,11},{4,12},{5,13},{6,14},{7,15},{16,24},{17,... | collective-permute-start | bytes 12296 | tf_op jit(solution)/shard_map/while/body/eval_jaxpr/ppermute | solution.py:22
  649.3 12.6 %collective-permute-start.2 = (f32[8,130,1]{1,0,2:T(8,128)S(1)}, f32[8,130,1]{1,0,2:T(8,128)S(1)}, u32[]{:S(2)}, u32[]{:S(2)}) collective-permute-start(f32[8,130,1]{1,0,2:T(8,128)S(1)} %get-tuple-element.191), channel_id=1, source_target_pairs={{0,1},{1,2},{2,3},{3,4},{4,5},{5,6},{6,7},{8,9},{9,10},{10,11},{11... | collective-permute-start | bytes 12488 | tf_op jit(solution)/shard_map/while/body/eval_jaxpr/ppermute | solution.py:22
  666.3 11.3 %collective-permute-start.1 = (f32[8,1,128]{1,0,2:T(8,128)S(1)}, f32[8,1,128]{1,0,2:T(8,128)S(1)}, u32[]{:S(2)}, u32[]{:S(2)}) collective-permute-start(f32[8,1,128]{1,0,2:T(8,128)S(1)} %get-tuple-element.190), channel_id=1, source_target_pairs={{0,8},{1,9},{2,10},{3,11},{4,12},{5,13},{6,14},{7,15},{16,24},{17,... | collective-permute-start | bytes 12296 | tf_op jit(solution)/shard_map/while/body/eval_jaxpr/ppermute | solution.py:22
  677.6 12.6 %collective-permute-start.2 = (f32[8,130,1]{1,0,2:T(8,128)S(1)}, f32[8,130,1]{1,0,2:T(8,128)S(1)}, u32[]{:S(2)}, u32[]{:S(2)}) collective-permute-start(f32[8,130,1]{1,0,2:T(8,128)S(1)} %get-tuple-element.191), channel_id=1, source_target_pairs={{0,1},{1,2},{2,3},{3,4},{4,5},{5,6},{6,7},{8,9},{9,10},{10,11},{11... | collective-permute-start | bytes 12488 | tf_op jit(solution)/shard_map/while/body/eval_jaxpr/ppermute | solution.py:22
  694.6 11.3 %collective-permute-start.1 = (f32[8,1,128]{1,0,2:T(8,128)S(1)}, f32[8,1,128]{1,0,2:T(8,128)S(1)}, u32[]{:S(2)}, u32[]{:S(2)}) collective-permute-start(f32[8,1,128]{1,0,2:T(8,128)S(1)} %get-tuple-element.190), channel_id=1, source_target_pairs={{0,8},{1,9},{2,10},{3,11},{4,12},{5,13},{6,14},{7,15},{16,24},{17,... | collective-permute-start | bytes 12296 | tf_op jit(solution)/shard_map/while/body/eval_jaxpr/ppermute | solution.py:22
  705.9 12.6 %collective-permute-start.2 = (f32[8,130,1]{1,0,2:T(8,128)S(1)}, f32[8,130,1]{1,0,2:T(8,128)S(1)}, u32[]{:S(2)}, u32[]{:S(2)}) collective-permute-start(f32[8,130,1]{1,0,2:T(8,128)S(1)} %get-tuple-element.191), channel_id=1, source_target_pairs={{0,1},{1,2},{2,3},{3,4},{4,5},{5,6},{6,7},{8,9},{9,10},{10,11},{11... | collective-permute-start | bytes 12488 | tf_op jit(solution)/shard_map/while/body/eval_jaxpr/ppermute | solution.py:22
  721.3 22.6 %collective-permute-start.8 = (bf16[8,128,128]{1,0,2:T(8,128)(2,1)S(1)}, bf16[8,128,128]{1,0,2:T(8,128)(2,1)S(1)}, u32[]{:S(2)}, u32[]{:S(2)}) collective-permute-start(bf16[8,128,128]{1,0,2:T(8,128)(2,1)S(1)} %convert_element_type.44), channel_id=1, source_target_pairs={{0,4},{1,5},{2,6},{3,7},{8,12},{9,13},{10,14},{11,15},{16,20},{17,... | collective-permute-start | bytes 786440 | tf_op jit(solution)/shard_map/ppermute | solution.py:34
  730.6 14.7 %collective-permute-start.9 = (bf16[8,128,128]{1,0,2:T(8,128)(2,1)S(1)}, bf16[8,128,128]{1,0,2:T(8,128)(2,1)S(1)}, u32[]{:S(2)}, u32[]{:S(2)}) collective-permute-start(bf16[8,128,128]{1,0,2:T(8,128)(2,1)S(1)} %convert_element_type.44), channel_id=1, source_target_pairs={{0,3},{1,4},{2,5},{3,6},{4,7},{8,11},{9,12},{10,13},{11,14},{12,15... | collective-permute-start | bytes 786440 | tf_op jit(solution)/shard_map/ppermute | solution.py:34
  734.0 12.7 %collective-permute-start.10 = (bf16[8,128,128]{1,0,2:T(8,128)(2,1)S(1)}, bf16[8,128,128]{1,0,2:T(8,128)(2,1)S(1)}, u32[]{:S(2)}, u32[]{:S(2)}) collective-permute-start(bf16[8,128,128]{1,0,2:T(8,128)(2,1)S(1)} %convert_element_type.44), channel_id=1, source_target_pairs={{0,2},{1,3},{2,4},{3,5},{4,6},{5,7},{8,10},{9,11},{10,12},{11,13},... | collective-permute-start | bytes 786440 | tf_op jit(solution)/shard_map/ppermute | solution.py:34
  745.3 13.4 %collective-permute-start.14 = (bf16[8,128,128]{1,0,2:T(8,128)(2,1)S(1)}, bf16[8,128,128]{1,0,2:T(8,128)(2,1)S(1)}, u32[]{:S(2)}, u32[]{:S(2)}) collective-permute-start(bf16[8,128,128]{1,0,2:T(8,128)(2,1)S(1)} %convert_element_type.44), channel_id=1, source_target_pairs={{3,0},{4,1},{5,2},{6,3},{7,4},{11,8},{12,9},{13,10},{14,11},{15,12... | collective-permute-start | bytes 786440 | tf_op jit(solution)/shard_map/ppermute | solution.py:34
  746.6 18.4 %collective-permute-start.15 = (bf16[8,128,128]{1,0,2:T(8,128)(2,1)S(1)}, bf16[8,128,128]{1,0,2:T(8,128)(2,1)S(1)}, u32[]{:S(2)}, u32[]{:S(2)}) collective-permute-start(bf16[8,128,128]{1,0,2:T(8,128)(2,1)S(1)} %convert_element_type.44), channel_id=1, source_target_pairs={{4,0},{5,1},{6,2},{7,3},{12,8},{13,9},{14,10},{15,11},{20,16},{21,... | collective-permute-start | bytes 786440 | tf_op jit(solution)/shard_map/ppermute | solution.py:34
  (96 other events, 425.5 us)
where the time goes:
time: 822 us; the launch traced here: 814 us
  starting transfers between devices  332 us (40%)
  waiting for transfers between devices  203 us (25%)
  local copies, waits for them, and re-layouts  181 us (22%)
  blocking collectives  45.8 us (6%)
  other arithmetic  44.6 us (5%)
    ppermute x50, starting transfers between devices, padded_2(): lax.ppermute(tail, axis, [(i, (i + 1) % count) for i in range(ends)])  246 us
    ppermute x50, waiting for transfers between devices, padded_2(): lax.ppermute(head, axis, [((i + 1) % count, i) for i in range(ends)])  151 us
    slice x144, local copies, waits for them, and re-layouts, interior(): return values_grid[..., trim_width:-trim_width, trim_width:-trim_width]  139 us
    ppermute x50, starting transfers between devices, padded_2(): lax.ppermute(head, axis, [((i + 1) % count, i) for i in range(ends)])  64.5 us
    select_n x24, other arithmetic, jacobi_sweep(): return jnp.where(interior(inside, trim_width), summed / diagonal_sum, 0.0)  38.2 us
    psum x1, blocking collectives, local(): joined = lax.psum(sampled, ('row', 'col'))  36.6 us
    ppermute x50, waiting for transfers between devices, padded_2(): lax.ppermute(tail, axis, [(i, (i + 1) % count) for i in range(ends)])  35.3 us
    while x96, local copies, waits for them, and re-layouts  28.1 us
  transfers between devices with their start and end apart: 108, of which 53 were waited for; matrix products, arithmetic and copies ran while one was open for 18% of the time, Pallas kernels for 0%

commit v1 on v0

v1 whole, which is shorter than its diff:
```python
import functools

import jax
import jax.numpy as jnp
from jax import lax
from jax.experimental import pallas as pl
from jax.experimental.pallas import tpu as pltpu
from jax.sharding import PartitionSpec as P

BLOCK = 128
TAPER = 4
SWEEPS = 24
HALO = 24
LANES = 128
STRIP = 32

leakage = 0.05
F32, BF16 = jnp.float32, jnp.bfloat16


def iota(shape, dim):
    return lax.broadcasted_iota(jnp.int32, shape, dim)


def one_hot(mask):
    return jnp.where(mask, 1.0, 0.0).astype(BF16)


def dot(a, b):
    return jnp.dot(a, b, preferred_element_type=F32)


def harmonic(a, b):
    return 2.0 * a * b / (a + b)


def factor(offset, scale, reach):
    distance = jnp.abs(offset).astype(F32)
    return jnp.exp(-distance / scale) * jnp.maximum(1.0 - distance / reach, 0.0)


def scales(corr_ref, taper_ref, total_rows):
    row_scale = corr_ref[0] * (total_rows / 4.0)
    row_reach = (taper_ref[0] + TAPER).astype(F32) * (total_rows / (2.0 * TAPER)) + 1.0
    col_scale = corr_ref[1] * BLOCK
    col_reach = (taper_ref[1] * BLOCK + 1).astype(F32)
    return row_scale, row_reach, col_scale, col_reach


def pack_kernel(swapped, place_ref, *refs):
    if swapped:
        obs_ref, recv_ref, lt_ref, lt_recv_ref, full_ref, split_ref, a_ref, b_ref = refs
    else:
        obs_ref, lt_ref, full_ref, split_ref, a_ref, b_ref = refs
    wells, rows, _ = full_ref.shape
    if swapped:
        half = rows // 2
        mine = pl.multiple_of(place_ref[0] * half, half)
        other = pl.multiple_of(half - mine, half)
        first = place_ref[0] * wells
        for w in range(wells):
            full_ref[w, pl.ds(mine, half), :] = obs_ref[first + w]
            full_ref[w, pl.ds(other, half), :] = recv_ref[w]
        parts = [(lt_ref[...], pl.ds(mine, half)), (lt_recv_ref[...], pl.ds(other, half))]
    else:
        full_ref[...] = obs_ref[...]
        parts = [(lt_ref[...], pl.ds(0, rows))]
    for value, where in parts:
        for i in range(3):
            piece = value.astype(BF16)
            split_ref[i, where, :] = piece
            value = value - piece.astype(F32)
    even = lax.rem(place_ref[1], 2) == 0
    src, dst = iota((LANES, LANES), 0), iota((LANES, LANES), 1)
    tail = LANES - HALO
    start_a = jnp.where(even, tail, 0)
    for out_ref, start in ((a_ref, start_a), (b_ref, tail - start_a)):
        for group, (ref, count) in enumerate(((full_ref, wells), (split_ref, 3))):
            total = jnp.zeros((rows, LANES), F32)
            for i in range(count):
                k = dst - STRIP * i
                pick = one_hot((src == k + start) & (k >= 0) & (k < HALO))
                total = total + dot(ref[i], pick)
            out_ref[:, group * LANES : (group + 1) * LANES] = total.astype(BF16)


def pair_swap(value, wells, outer):
    groups = 8 // wells
    group = iota(value.shape, 0) // wells
    up = pltpu.roll(value, wells, 0)
    if groups == 2:
        return up
    down = pltpu.roll(value, 8 - wells, 0)
    return jnp.where((group % 2 == 0) == (not outer), down, up)


def update(previous, current, following, coefs, source):
    result = []
    even, odd = current
    sides = ((odd, pltpu.roll(odd, 1, 1)), (pltpu.roll(even, LANES - 1, 1), even))
    for p in range(2):
        ce, cw, co, ci = coefs[4 * p : 4 * p + 4]
        east, west = sides[p]
        result.append(
            (source[p] + ce * east) + (cw * west + co * previous[p]) + ci * following[p]
        )
    return result


def sweep_kernel(total_cols, place_ref, corr_ref, taper_ref, cells_ref,
                 full_ref, split_ref, a_ref, b_ref, adj_ref, mom_ref,
                 nat_ref, x_ref, s_ref, c_ref):
    wells, rows, _ = full_ref.shape
    groups = 8 // wells
    seg = rows // groups
    col = place_ref[1]
    even = lax.rem(col, 2) == 0
    src, dst = iota((LANES, 2 * LANES), 0), iota((LANES, 2 * LANES), 1)
    window = 2 * (dst % LANES) + dst // LANES
    own_pick = one_hot(window == src + HALO)
    right = LANES + HALO
    base_a = jnp.where(even, right, 0)
    picks = []
    for i in range(max(wells, 3)):
        k = src - STRIP * i
        live = (k >= 0) & (k < HALO)
        picks.append(tuple(
            one_hot((window == k + base) & live) for base in (base_a, right - base_a)
        ))

    def widened(ref, i, group):
        lanes = slice(group * LANES, (group + 1) * LANES)
        return (
            dot(ref[i], own_pick)
            + dot(a_ref[:, lanes], picks[i][0])
            + dot(b_ref[:, lanes], picks[i][1])
        )

    planes = [widened(split_ref, i, 1) for i in range(3)]
    nat_ref[0:8, :] = jnp.zeros((8, 2 * LANES), F32)
    nat_ref[rows + 8 : rows + 16, :] = jnp.zeros((8, 2 * LANES), F32)
    nat_ref[8 : rows + 8, :] = planes[0] + planes[1] + planes[2]
    planes = [plane.astype(BF16) for plane in planes]
    fields = [widened(full_ref, w, 0) for w in range(wells)]

    lane = iota((seg, LANES), 1)
    step = iota((seg, LANES), 0)
    t_pick, r_pick = iota((seg + 16, rows), 0), iota((seg + 16, rows), 1)
    t_flip, r_flip = iota((seg, rows), 0), iota((seg, rows), 1)
    for g in range(groups):
        if g % 2 == 0:
            logs = nat_ref[g * seg : g * seg + seg + 16, :]
        else:
            pick = one_hot(r_pick == (g + 1) * seg - 1 - (t_pick - 8))
            logs = dot(pick, planes[0]) + dot(pick, planes[1]) + dot(pick, planes[2])
            flip = one_hot(r_flip == (g + 1) * seg - 1 - t_flip)
        cond = jnp.exp(logs)
        sides = [cond[:, :LANES], cond[:, LANES:]]
        centre = [side[8 : seg + 8] for side in sides]
        east = (centre[1], pltpu.roll(centre[0], LANES - 1, 1))
        west = (pltpu.roll(centre[1], 1, 1), centre[0])
        edge = (step == 0) if g in (0, groups - 1) else None
        inverse = []
        for p in range(2):
            column = col * LANES - HALO + 2 * lane + p
            inside = (column >= 0) & (column < total_cols) & (lane < (LANES + 2 * HALO) // 2)
            has_east, has_west = column < total_cols - 1, column > 0
            mid = centre[p]
            fe = jnp.where(has_east, harmonic(mid, east[p]), mid)
            fw = jnp.where(has_west, harmonic(mid, west[p]), mid)
            fo = harmonic(mid, sides[p][7 : seg + 7])
            if edge is not None:
                fo = jnp.where(edge, mid, fo)
            fi = harmonic(mid, sides[p][9 : seg + 9])
            inv = jnp.where(inside, 1.0 / (fe + fw + fo + fi + leakage), 0.0)
            inverse.append(inv)
            outer = fo * inv
            if edge is not None:
                outer = jnp.where(edge, 0.0, outer)
            coefs = (
                jnp.where(has_east, fe * inv, 0.0),
                jnp.where(has_west, fw * inv, 0.0),
                outer,
                fi * inv,
            )
            for d, coef in enumerate(coefs):
                for t in range(0, seg, 8):
                    for w in range(wells):
                        at = ((t * 2 + p) * 4 + d) * 8 + g * wells + w
                        c_ref[pl.ds(at, 8, stride=64), :] = coef[t : t + 8]
        for w in range(wells):
            if g % 2 == 0:
                field = fields[w][g * seg : (g + 1) * seg]
            else:
                field = dot(flip, fields[w].astype(BF16))
            for p in range(2):
                value = field[:, p * LANES : (p + 1) * LANES] * inverse[p]
                for t in range(0, seg, 8):
                    at = (t * 2 + p) * 8 + g * wells + w
                    s_ref[pl.ds(at, 8, stride=16), :] = value[t : t + 8]

    def load(ref, t, count=2):
        at = pl.multiple_of(t * (count * 8), count * 8)
        return [ref[pl.ds(at + 8 * i, 8), :] for i in range(count)]

    def save(t, value):
        at = pl.multiple_of(t * 16, 16)
        for p in range(2):
            x_ref[pl.ds(at + 8 * p, 8), :] = value[p]

    unroll = 8

    def march(first_pass):
        def rows_of(t0, carry, first_block):
            x0, x1, y0, y1, coefs1, source1 = carry
            for i in range(unroll):
                t = t0 + i
                coefs2 = load(c_ref, t, 8)
                source2 = load(s_ref, t)
                if first_pass:
                    y2 = source2
                else:
                    x2 = load(x_ref, t + 2)
                    y2 = update(x0, x1, x2, coefs2, source2)
                    x0, x1 = x1, x2
                if first_block and i == 0:
                    y0 = [pair_swap(v, wells, True) for v in y2]
                    y0, y1 = y0, y2
                else:
                    save(t, update(y0, y1, y2, coefs1, source1))
                    y0, y1 = y1, y2
                coefs1, source1 = coefs2, source2
            return x0, x1, y0, y1, coefs1, source1

        blank = [jnp.zeros((8, LANES), F32)] * 2
        if first_pass:
            x0 = x1 = blank
        else:
            x1 = load(x_ref, 1)
            x0 = [pair_swap(v, wells, True) for v in x1]
            last = load(x_ref, seg)
            save(seg + 1, [pair_swap(v, wells, False) for v in last])
        carry = rows_of(0, (x0, x1, blank, blank, None, None), True)
        carry = lax.fori_loop(
            1, seg // unroll, lambda b, c: rows_of(b * unroll, c, False), carry
        )
        _, _, y0, y1, coefs1, source1 = carry
        y2 = [pair_swap(v, wells, False) for v in y1]
        save(seg, update(y0, y1, y2, coefs1, source1))

    march(True)

    def more(_, carry):
        march(False)
        return carry

    lax.fori_loop(0, SWEEPS // 2 - 1, more, 0)

    row_scale, row_reach, col_scale, col_reach = scales(corr_ref, taper_ref, rows)
    order = one_hot(
        2 * (iota((2 * LANES, LANES), 0) % LANES) + iota((2 * LANES, LANES), 0) // LANES
        == iota((2 * LANES, LANES), 1) + HALO
    )
    reverse = one_hot(iota((seg, seg), 0) == seg - 1 - iota((seg, seg), 1))
    kind, c = iota((8, LANES), 0), iota((8, LANES), 1)
    reach = jnp.where(kind % 4 < 2, LANES - c, c + 1).astype(F32)
    basis = jnp.exp(-reach / col_scale) * jnp.where(kind % 2 == 0, 1.0, reach / LANES)
    high = basis.astype(BF16)
    basis = jnp.where(kind < 4, high.astype(F32), basis - high.astype(F32)).astype(BF16)
    m_lane = iota((1, LANES), 1)
    cell = jnp.full((1, LANES), -1, jnp.int32)
    batches, per_batch = cells_ref.shape
    for b in range(batches):
        for n in range(per_batch):
            cell = jnp.where(m_lane == b * per_batch + n, cells_ref[b, n], cell)
    cell_row, cell_col = lax.div(cell, total_cols), lax.rem(cell, total_cols)
    row_weight = factor(cell_row - iota((rows, LANES), 0), row_scale, row_reach)
    row_weight = row_weight.astype(BF16).astype(F32)
    col_weight = factor(
        cell_col - (col * LANES + iota((LANES, LANES), 0)), col_scale, col_reach
    ).astype(BF16)
    mom_ref[...] = jnp.zeros(mom_ref.shape, F32)
    for w in range(wells):
        for g in range(groups):
            tiles = []
            for t in range(0, seg, 8):
                at = (t + 1) * 16 + g * wells + w
                tiles.append(jnp.concatenate(
                    [x_ref[pl.ds(at + 8 * p, 8, stride=16), :] for p in range(2)], axis=1
                ))
            value = dot(jnp.concatenate(tiles, axis=0).astype(BF16), order)
            if g % 2 == 1:
                value = dot(reverse, value.astype(BF16))
            adj_ref[w, g * seg : (g + 1) * seg, :] = value.astype(BF16)
        adjoint = adj_ref[w]
        both = lax.dot_general(
            basis, adjoint, (((1,), (1,)), ((), ())), preferred_element_type=F32
        )
        mom_ref[0:4, w * rows : (w + 1) * rows] = both[0:4] + both[4:8]
        sampled = jnp.sum(dot(adjoint, col_weight) * row_weight, axis=0, keepdims=True)
        mom_ref[4:5, w * rows : w * rows + LANES] = sampled


def mix_kernel(offsets, swapped, tiles, place_ref, corr_ref, taper_ref, adj_ref, mom_ref, *refs):
    tile_refs = refs[:tiles]
    out_refs = refs[tiles:]
    wells, rows, _ = adj_ref.shape
    col, taper = place_ref[1], taper_ref[1]
    row_scale, row_reach, col_scale, col_reach = scales(corr_ref, taper_ref, rows)
    ones = jnp.ones((1, LANES), F32)
    scale_v, reach_v = ones * col_scale, ones * col_reach
    sums = [jnp.zeros((1, wells * rows), F32) for _ in range(4)]
    for index, offset in enumerate(offsets):
        if offset == 0:
            continue
        away = lax.bitwise_xor(col, offset) - col
        for side, k in ((0, -away), (1, away)):
            live = (k >= 1) & (k < taper)
            gap = jnp.maximum(k - 1, 0).astype(F32)
            gain = jnp.where(live, 1.0, 0.0) * jnp.exp(-gap * LANES / scale_v)
            gain = gain[:, :1]
            zero = mom_ref[index, 2 * side : 2 * side + 1, :]
            one = mom_ref[index, 2 * side + 1 : 2 * side + 2, :]
            sums[2 * side] = sums[2 * side] + gain * zero
            sums[2 * side + 1] = sums[2 * side + 1] + gain * (gap * zero + one)
    stacked = jnp.concatenate(sums * 4, axis=0)
    kind = iota((16, wells * rows), 0)
    high = stacked.astype(BF16).astype(F32)
    stacked = jnp.where((kind >= 4) & (kind < 8), stacked - high, high).astype(BF16)
    kind, c = iota((16, LANES), 0), iota((16, LANES), 1)
    near = jnp.where(kind % 4 < 2, c, LANES - 1 - c).astype(F32)
    spread = jnp.exp(-near / col_scale) * jnp.where(
        kind % 2 == 0, 1.0 - near / col_reach, -LANES / col_reach
    )
    high = spread.astype(BF16).astype(F32)
    spread = jnp.where(kind < 8, high, jnp.where(kind < 12, spread - high, 0.0)).astype(BF16)
    src, dst = iota((LANES, LANES), 0), iota((LANES, LANES), 1)
    matrices = [factor(dst - src, col_scale, col_reach).astype(BF16)]
    even = lax.rem(lax.div(col, taper), 2) == 0
    shift = jnp.where(even, taper, -taper) * LANES
    for i in range(tiles):
        matrices.append(
            factor(dst - src - (shift if i == 0 else -shift), col_scale, col_reach).astype(BF16)
        )
    row_mix = factor(
        iota((rows, rows), 0) - iota((rows, rows), 1), row_scale, row_reach
    ).astype(BF16)
    for w in range(wells):
        mixed = lax.dot_general(
            stacked[:, w * rows : (w + 1) * rows], spread,
            (((0,), (0,)), ((), ())), preferred_element_type=F32,
        )
        mixed = mixed + dot(adj_ref[w], matrices[0])
        for ref, matrix in zip(tile_refs, matrices[1:]):
            mixed = mixed + dot(ref[w], matrix)
        field = dot(row_mix, mixed.astype(BF16)).astype(BF16)
        if swapped:
            half = rows // 2
            keep = place_ref[0] == 0
            out_refs[0][w] = jnp.where(keep, field[:half], field[half:])
            out_refs[1][w] = jnp.where(keep, field[half:], field[:half])
        else:
            out_refs[0][w] = field


VMEM = pl.BlockSpec(memory_space=pltpu.VMEM)
SMEM = pl.BlockSpec(memory_space=pltpu.SMEM)


def call(kernel, smem, vmem, outs, scratch=(), flops=1):
    return pl.pallas_call(
        kernel,
        in_specs=[SMEM] * len(smem) + [VMEM] * len(vmem),
        out_specs=[VMEM] * len(outs),
        out_shape=[jax.ShapeDtypeStruct(shape, dtype) for shape, dtype in outs],
        scratch_shapes=list(scratch),
        compiler_params=pltpu.CompilerParams(vmem_limit_bytes=48 * 2**20),
        cost_estimate=pl.CostEstimate(flops=flops, bytes_accessed=2**20, transcendentals=0),
    )(*smem, *vmem)


def pairs_at(count, distance, odd):
    pairs = []
    for i in range(count - distance):
        if (i // distance) % 2 == odd:
            pairs += [(i, i + distance), (i + distance, i)]
    return pairs


def exchanged(value, axis):
    return lax.ppermute(value, axis, [(0, 1), (1, 0)])


def local(log_trans, corr_len, taper_width, well_cells, obs_weight):
    tile_rows, tile_cols = log_trans.shape
    row_count, col_count = lax.axis_size("row"), lax.axis_size("col")
    total_rows, total_cols = tile_rows * row_count, tile_cols * col_count
    well_count = well_cells.shape[1]
    wells = well_count // row_count
    row, col = lax.axis_index("row"), lax.axis_index("col")
    place = jnp.stack([row, col]).astype(jnp.int32)
    own = obs_weight[0]
    swapped = row_count == 2
    tile = (wells, total_rows, tile_cols)

    if swapped:
        other_logs = exchanged(log_trans, "row")
        sent = lax.dynamic_slice_in_dim(own, (1 - row) * wells, wells, axis=0)
        operands = (own, exchanged(sent, "row"), log_trans, other_logs)
    else:
        operands = (
            lax.all_to_all(own, "row", 0, 1, tiled=True),
            lax.all_gather(log_trans, "row", axis=0, tiled=True),
        )
    strip = ((total_rows, 2 * LANES), BF16)
    full, split, strip_a, strip_b = call(
        functools.partial(pack_kernel, swapped), (place,), operands,
        [(tile, BF16), ((3,) + tile[1:], BF16), strip, strip],
    )
    strip_a = lax.ppermute(strip_a, "col", pairs_at(col_count, 1, 0))
    strip_b = lax.ppermute(strip_b, "col", pairs_at(col_count, 1, 1))

    seg = total_rows * wells // 8
    adjoint, moments = call(
        functools.partial(sweep_kernel, total_cols),
        (place, corr_len, taper_width, well_cells), (full, split, strip_a, strip_b),
        [(tile, BF16), ((8, wells * total_rows), F32)],
        [
            pltpu.VMEM((total_rows + 16, 2 * LANES), F32),
            pltpu.VMEM(((seg + 2) * 16, LANES), F32),
            pltpu.VMEM((seg * 16, LANES), F32),
            pltpu.VMEM((seg * 64, LANES), F32),
        ],
    )

    def finish(distance, adjoint, moments):
        tiles = []
        for odd in range(2):
            pairs = pairs_at(col_count, distance, odd)
            if pairs:
                tiles.append(lax.ppermute(adjoint, "col", pairs))
        gathered, offsets = moments[None], [0]
        step = col_count // 2
        while step:
            moved = lax.ppermute(gathered, "col", [(i, i ^ step) for i in range(col_count)])
            gathered = jnp.concatenate([gathered, moved], axis=0)
            offsets = offsets + [offset ^ step for offset in offsets]
            step //= 2
        samples = [gathered[i, 4] for i in range(col_count)]
        while len(samples) > 1:
            samples = [a + b for a, b in zip(samples[::2], samples[1::2])]
        samples = samples[0].reshape(wells, total_rows)[:, : 2 * well_count]
        samples = lax.all_gather(samples, "row", axis=0, tiled=True)
        samples = lax.all_gather(samples, "sect", axis=0, tiled=True)
        half = ((wells, tile_rows, tile_cols), BF16)
        fields = call(
            functools.partial(mix_kernel, tuple(offsets), swapped, len(tiles)),
            (place, corr_len, taper_width), (adjoint, gathered, *tiles),
            [half, half] if swapped else [(tile, BF16)],
        )
        return tuple(fields) + (samples.T,)

    branches = [functools.partial(finish, distance) for distance in range(1, TAPER + 1)]
    *fields, measure_cov = lax.switch(taper_width[1] - 1, branches, adjoint, moments)
    if swapped:
        kept, sent = fields
        other = exchanged(sent, "row")
        low = row == 0
        qh_fields = jnp.concatenate(
            [jnp.where(low, kept, other), jnp.where(low, other, kept)], axis=0
        )
    else:
        qh_fields = lax.all_to_all(fields[0], "row", 1, 0, tiled=True)
    return (qh_fields[None], measure_cov)


def solution(mesh):
    placed = (P("row", "col"), P(), P(), P(), P("sect", None, "row", "col"))
    return jax.shard_map(
        local,
        mesh=mesh,
        in_specs=placed,
        out_specs=(P("sect", None, "row", "col"), P()),
        check_vma=False,
    )
```

time: 822 us -> 86.9 us (0.11)
  starting transfers between devices: 332 us -> 18.9 us
  waiting for transfers between devices: 203 us -> 17.9 us
  local copies, waits for them, and re-layouts: 181 us -> 3.17 us
  other arithmetic: 44.6 us -> 0.9 us
  blocking collectives: 45.8 us -> 6.12 us
  Pallas kernels: 0 us -> 38.2 us
    ppermute x108 -> x9, starting transfers between devices: 332 us -> 18.9 us  [the longest x3 9.01 us: finish(): lax.ppermute(gathered, 'col', [(i, i ^ step) for i in range(col_count)])]
    ppermute x108 -> x9, waiting for transfers between devices: 203 us -> 17.9 us  [the longest x3 8.89 us: exchanged(): return lax.ppermute(value, axis, [(0, 1), (1, 0)])]
    slice x174 -> x1, local copies, waits for them, and re-layouts: 148 us -> 0.58 us  [local(): taper_width[1] - 1]
    pallas_call x0 -> x3, Pallas kernels: none -> 38.2 us  [call(): pl.pallas_call(kernel, in_specs=[SMEM] * len(smem) + [VMEM] * len(vmem),...]
    select_n x25 -> x1, other arithmetic: 38.2 us -> 0.02 us  [local(): jnp.where(low, kept, other)]
    psum x1 -> x0, blocking collectives: 36.6 us -> none  [local(): joined = lax.psum(sampled, ('row', 'col'))]
    while x96 -> x0, local copies, waits for them, and re-layouts: 28.1 us -> none
  transfers between devices with their start and end apart: 108 -> 9, of which waited for: 53 -> 6; matrix products, arithmetic and copies ran while one was open for 18% -> 1% of each run, Pallas kernels for 0% -> 0%
where the time goes in v1:
time: 86.9 us; the launch traced here: 86.6 us
  Pallas kernels  38.2 us (44%)
  starting transfers between devices  18.9 us (22%)
  waiting for transfers between devices  17.9 us (21%)
  blocking collectives  6.12 us (7%)
  local copies, waits for them, and re-layouts  3.17 us (4%)
  between operations  1.37 us (2%)
  other arithmetic  0.9 us (1%)
    pallas_call x3, Pallas kernels, call(): pl.pallas_call(kernel, in_specs=[SMEM] * len(smem) + [VMEM] * len(vmem),...  38.2 us
    ppermute x3, starting transfers between devices, finish(): lax.ppermute(gathered, 'col', [(i, i ^ step) for i in range(col_count)])  9.01 us
    ppermute x3, waiting for transfers between devices, exchanged(): return lax.ppermute(value, axis, [(0, 1), (1, 0)])  8.89 us
    ppermute x3, waiting for transfers between devices, finish(): lax.ppermute(gathered, 'col', [(i, i ^ step) for i in range(col_count)])  7.61 us
    ppermute x3, starting transfers between devices, exchanged(): return lax.ppermute(value, axis, [(0, 1), (1, 0)])  4.64 us
    all_gather x1, blocking collectives, finish(): samples = lax.all_gather(samples, 'row', axis=0, tiled=True)  4.34 us
    ppermute x1, starting transfers between devices, finish(): tiles.append(lax.ppermute(adjoint, 'col', pairs))  2.84 us
    all_gather x1, blocking collectives, finish(): samples = lax.all_gather(samples, 'sect', axis=0, tiled=True)  1.78 us
  transfers between devices with their start and end apart: 9, of which 6 were waited for; matrix products, arithmetic and copies ran while one was open for 1% of the time, Pallas kernels for 0%

profile of v1, /device:TPU:0, one launch (start us, length us, event | category | flops | bytes accessed | tf_op | source)
XLA Modules:
  0.0 86.6 jit_solution(9052455204994762574)
XLA Ops:
  0.6 0.0 copy-start
  0.6 1.0 %dynamic-slice_bitcast_fusion = bf16[4,128,128]{2,1,0:T(8,128)(2,1)S(1)} fusion(bf16[1,8,128,128]{3,2,1,0:T(8,128)(2,1)} %param.13, s32[]{:T(128)S(6)} %select_n.16), kind=kLoop, calls=%fused_computation.49 | loop fusion | bytes 262148 | tf_op jit(solution)/shard_map/dynamic_slice | solution.py:408
  1.6 3.0 %collective-permute-start.19 = (bf16[4,128,128]{2,1,0:T(8,128)(2,1)S(1)}, bf16[4,128,128]{2,1,0:T(8,128)(2,1)S(1)}, u32[]{:S(2)}, u32[]{:S(2)}) collective-permute-start(bf16[4,128,128]{2,1,0:T(8,128)(2,1)S(1)} %dynamic-slice_bitcast_fusion), channel_id=1, source_target_pairs={{0,8},{8,0},{1,9},{9,1},{2,10},{10,2},{3,11},{11,3},{4,12},{12,4},... | collective-permute-start | bytes 393224 | tf_op jit(solution)/shard_map/ppermute | solution.py:391
  4.7 0.1 collective-permute-start.20
  4.7 0.1 pad_add_fusion.place_ref
  4.8 4.7 %collective-permute-done.20.refs_3_ = f32[128,128]{1,0:T(8,128)S(1)} collective-permute-done((f32[128,128]{1,0:T(8,128)}, f32[128,128]{1,0:T(8,128)S(1)}, u32[]{:S(2)}, u32[]{:S(2)}) %collective-permute-start.20) | collective-permute-done | bytes 65568 | tf_op jit(solution)/shard_map/ppermute | solution.py:391
  9.6 0.0 collective-permute-done.19.refs_1_
  9.6 0.0 copy-done
  9.6 0.0 copy-start.1
  9.6 0.8 copy-done.1
  10.4 0.9 %shard_map.68 = (bf16[4,256,128]{2,1,0:T(8,128)(2,1)S(1)}, bf16[3,256,128]{2,1,0:T(8,128)(2,1)S(1)}, bf16[256,256]{1,0:T(8,128)(2,1)S(1)}, bf16[256,256]{1,0:T(8,128)(2,1)S(1)}) custom-call(s32[2]{0:T(128)S(1)} %pad_add_fusion.place_ref, bf16[8,128,128]{2,1,0:T(8,128)(2,1)S(1)} %bitcast.28, bf16[4,128,128]{2,1,0:T(8,128)(2,1)S(1)} %collective-permute-done.19.refs_1_, ...), custom_call_target="tpu_custom_call" | custom-call | flops 1 | bytes 1048576 | tf_op jit(solution)/shard_map/pallas_call | solution.py:371
  11.4 0.0 copy-start.3
  11.4 1.8 %collective-permute-start.21 = (bf16[256,256]{1,0:T(8,128)(2,1)S(1)}, bf16[256,256]{1,0:T(8,128)(2,1)S(1)}, u32[]{:S(2)}, u32[]{:S(2)}) collective-permute-start(bf16[256,256]{1,0:T(8,128)(2,1)S(1)} %get-tuple-element.81), channel_id=1, source_target_pairs={{0,1},{1,0},{2,3},{3,2},{4,5},{5,4},{6,7},{7,6},{8,9},{9,8},{10,11... | collective-permute-start | bytes 393224 | tf_op jit(solution)/shard_map/ppermute | solution.py:420
  13.1 0.7 collective-permute-start.22
  13.8 0.0 copy-done.3
  13.8 0.6 slice.111
  15.1 1.3 %collective-permute-done.21.a_ref = bf16[256,256]{1,0:T(8,128)(2,1)S(1)} collective-permute-done((bf16[256,256]{1,0:T(8,128)(2,1)S(1)}, bf16[256,256]{1,0:T(8,128)(2,1)S(1)}, u32[]{:S(2)}, u32[]{:S(2)}) %collective-permute-start.21) | collective-permute-done | bytes 131104 | tf_op jit(solution)/shard_map/ppermute | solution.py:420
  16.4 0.0 collective-permute-done.22.b_ref
  16.4 0.0 copy-start.2
  16.4 0.0 copy-start.4
  16.4 0.7 copy-done.2
  17.1 0.0 copy-done.4
  17.1 35.3 %shard_map.69 = (bf16[4,256,128]{2,1,0:T(8,128)(2,1)S(1)}, f32[8,1024]{1,0:T(8,128)S(1)}) custom-call(s32[2]{0:T(128)S(1)} %pad_add_fusion.place_ref, f32[2]{0:T(128)S(1)} %copy-done.4, s32[2]{0:T(128)S(1)} %copy-done.3, s32[2,8]{1,0:T(2,128)S(1)} %copy-done.2, bf16[4,256,128]{2,1,0:T(8,128)(2,1)S(1)} %get-tuple-element.79.full_ref, ...), custom_call_target="tpu_custom_call" | custom-call | flops 1 | bytes 1048576 | tf_op jit(solution)/shard_map/pallas_call | solution.py:371
  52.4 27.7 %conditional.1 = (bf16[4,128,128]{2,1,0:T(8,128)(2,1)S(1)}, bf16[4,128,128]{2,1,0:T(8,128)(2,1)S(1)}, f32[16,16]{1,0:T(8,128)S(1)}) conditional(s32[]{:T(128)} %bitcast.16, (f32[8,1024]{1,0:T(8,128)S(1)}, bf16[4,256,128]{2,1,0:T(8,128)(2,1)S(1)}, s32[2]{0:T(128)S(1)}, f32[2]{0:T(128)S(1)}, s32[2]{0:T(128)S(1)}) %tuple.41, ...), branch_computations={%region_0.0_spmd, %region_1.0_spmd, %region_2.0_spmd, %region_3.0_... | conditional | flops 285697 | bytes 5030880 | solution.py:464
  52.5 7.1 %collective-permute-start.15 = (f32[1,8,1024]{2,1,0:T(8,128)S(1)}, f32[1,8,1024]{2,1,0:T(8,128)S(1)}, u32[]{:S(2)}, u32[]{:S(2)}) collective-permute-start(f32[1,8,1024]{2,1,0:T(8,128)S(1)} %bitcast.44), channel_id=1, source_target_pairs={{0,4},{1,5},{2,6},{3,7},{4,0},{5,1},{6,2},{7,3},{8,12},{9,13},{10,... | collective-permute-start | bytes 98312 | tf_op jit(solution)/shard_map/cond/branch_3_fun/ppermute | solution.py:445
  59.6 2.0 %collective-permute-done.15 = f32[1,8,1024]{2,1,0:T(8,128)S(1)} collective-permute-done((f32[1,8,1024]{2,1,0:T(8,128)S(1)}, f32[1,8,1024]{2,1,0:T(8,128)S(1)}, u32[]{:S(2)}, u32[]{:S(2)}) %collective-permute-start.15) | collective-permute-done | bytes 32800 | tf_op jit(solution)/shard_map/cond/branch_3_fun/ppermute | solution.py:445
  61.6 1.8 %collective-permute-start.16 = (f32[2,8,1024]{2,1,0:T(8,128)S(1)}, f32[2,8,1024]{2,1,0:T(8,128)S(1)}, u32[]{:S(2)}, u32[]{:S(2)}) collective-permute-start(f32[2,8,1024]{2,1,0:T(8,128)S(1)} %pad_maximum_fusion.11), channel_id=1, source_target_pairs={{0,2},{1,3},{2,0},{3,1},{4,6},{5,7},{6,4},{7,5},{8,10},{9,11},{10,... | collective-permute-start | bytes 196616 | tf_op jit(solution)/shard_map/cond/branch_3_fun/ppermute | solution.py:445
  63.4 3.5 %collective-permute-done.16 = f32[2,8,1024]{2,1,0:T(8,128)S(1)} collective-permute-done((f32[2,8,1024]{2,1,0:T(8,128)S(1)}, f32[2,8,1024]{2,1,0:T(8,128)S(1)}, u32[]{:S(2)}, u32[]{:S(2)}) %collective-permute-start.16) | collective-permute-done | bytes 65568 | tf_op jit(solution)/shard_map/cond/branch_3_fun/ppermute | solution.py:445
  66.9 0.1 collective-permute-start.17
  67.0 2.8 %collective-permute-start.18 = (bf16[4,256,128]{2,1,0:T(8,128)(2,1)S(1)}, bf16[4,256,128]{2,1,0:T(8,128)(2,1)S(1)}, u32[]{:S(2)}, u32[]{:S(2)}) collective-permute-start(bf16[4,256,128]{2,1,0:T(8,128)(2,1)S(1)} %get-tuple-element.64.adj_ref), channel_id=1, source_target_pairs={{0,4},{4,0},{1,5},{5,1},{2,6},{6,2},{3,7},{7,3},{8,12},{12,8},{9,1... | collective-permute-start | bytes 786440 | tf_op jit(solution)/shard_map/cond/branch_3_fun/ppermute | solution.py:441
  69.8 2.1 %collective-permute-done.17 = f32[4,8,1024]{2,1,0:T(8,128)S(1)} collective-permute-done((f32[4,8,1024]{2,1,0:T(8,128)S(1)}, f32[4,8,1024]{2,1,0:T(8,128)S(1)}, u32[]{:S(2)}, u32[]{:S(2)}) %collective-permute-start.17) | collective-permute-done | bytes 131104 | tf_op jit(solution)/shard_map/cond/branch_3_fun/ppermute | solution.py:445
  72.0 4.3 %all-gather.3 = f32[2,4,16]{2,1,0:T(4,128)S(1)} all-gather(f32[1,4,16]{2,1,0:T(4,128)S(1)} %slice_bitcast_fusion.3), channel_id=1, replica_groups=mesh['sect'=2,'row'=2,'col'=8] {'row'}, dimensions={0}, use_global_device_ids=true | all-gather | bytes 768 | tf_op jit(solution)/shard_map/cond/branch_3_fun/all_gather | solution.py:453
  76.4 1.8 %all_gather.23 = f32[16,16]{1,0:T(8,128)S(1)} all-gather(f32[8,16]{1,0:T(8,128)S(1)} %bitcast.56), channel_id=1, replica_groups=mesh['sect'=2,'row'=2,'col'=8] {'sect'}, dimensions={0}, use_global_device_ids=true | all-gather | bytes 1536 | tf_op jit(solution)/shard_map/cond/branch_3_fun/all_gather | solution.py:454
  78.1 0.1 copy.12
  78.2 0.0 collective-permute-done.18.refs_0_
  78.2 1.9 %branch_3_fun.1 = (bf16[4,128,128]{2,1,0:T(8,128)(2,1)S(1)}, bf16[4,128,128]{2,1,0:T(8,128)(2,1)S(1)}) custom-call(s32[2]{0:T(128)S(1)} %get-tuple-element.61.place_ref, f32[2]{0:T(128)S(1)} %get-tuple-element.62.corr_ref, s32[2]{0:T(128)S(1)} %get-tuple-element.63.taper_ref, bf16[4,256,128]{2,1,0:T(8,128)(2,1)S(1)} %get-tuple-element.64.adj_ref, ...), custom_call_target="tpu_custom_call" | custom-call | flops 1 | bytes 1048576 | tf_op jit(solution)/shard_map/cond/branch_3_fun/pallas_call | solution.py:371
  80.2 0.0 copy-start.5
  80.2 1.5 %collective-permute-start.23 = (bf16[4,128,128]{2,1,0:T(8,128)(2,1)S(1)}, bf16[4,128,128]{2,1,0:T(8,128)(2,1)S(1)}, u32[]{:S(2)}, u32[]{:S(2)}) collective-permute-start(bf16[4,128,128]{2,1,0:T(8,128)(2,1)S(1)} %get-tuple-element.86), channel_id=1, source_target_pairs={{0,8},{8,0},{1,9},{9,1},{2,10},{10,2},{3,11},{11,3},{4,12},{12,4},... | collective-permute-start | bytes 393224 | tf_op jit(solution)/shard_map/ppermute | solution.py:391
  81.7 4.1 %collective-permute-done.23 = bf16[4,128,128]{2,1,0:T(8,128)(2,1)S(1)} collective-permute-done((bf16[4,128,128]{2,1,0:T(8,128)(2,1)S(1)}, bf16[4,128,128]{2,1,0:T(8,128)(2,1)S(1)}, u32[]{:S(2)}, u32[]{:S(2)}) %collective-permute-start.23) | collective-permute-done | bytes 131104 | tf_op jit(solution)/shard_map/ppermute | solution.py:391
  85.9 0.0 copy-done.5
  85.9 0.7 maximum_bitcast_fusion
  (7 shorter events, 0.1 us)
Async XLA Ops:
  0.6 8.9 %copy-start = (bf16[1,8,128,128]{3,2,1,0:T(8,128)(2,1)S(1)}, bf16[1,8,128,128]{3,2,1,0:T(8,128)(2,1)}, u32[]{:S(2)}) copy-start(bf16[1,8,128,128]{3,2,1,0:T(8,128)(2,1)} %param.13) | copy-start | bytes 786436
  1.6 7.9 %collective-permute-start.19 = (bf16[4,128,128]{2,1,0:T(8,128)(2,1)S(1)}, bf16[4,128,128]{2,1,0:T(8,128)(2,1)S(1)}, u32[]{:S(2)}, u32[]{:S(2)}) collective-permute-start(bf16[4,128,128]{2,1,0:T(8,128)(2,1)S(1)} %dynamic-slice_bitcast_fusion), channel_id=1, source_target_pairs={{0,8},{8,0},{1,9},{9,1},{2,10},{10,2},{3,11},{11,3},{4,12},{12,4},... | collective-permute-start | bytes 393224 | tf_op jit(solution)/shard_map/ppermute | solution.py:391
  4.7 4.9 %collective-permute-start.20 = (f32[128,128]{1,0:T(8,128)}, f32[128,128]{1,0:T(8,128)S(1)}, u32[]{:S(2)}, u32[]{:S(2)}) collective-permute-start(f32[128,128]{1,0:T(8,128)} %refs_2_.1), channel_id=1, source_target_pairs={{0,8},{8,0},{1,9},{9,1},{2,10},{10,2},{3,11},{11,3},{4,12},{12,4},... | collective-permute-start | bytes 196616 | tf_op jit(solution)/shard_map/ppermute | solution.py:391
  9.6 0.8 copy-start.1
  11.4 2.5 %copy-start.3 = (s32[2]{0:T(128)S(1)}, s32[2]{0:T(128)}, u32[]{:S(2)}) copy-start(s32[2]{0:T(128)} %taper_ref.1) | copy-start | bytes 28
  11.4 5.0 %collective-permute-start.21 = (bf16[256,256]{1,0:T(8,128)(2,1)S(1)}, bf16[256,256]{1,0:T(8,128)(2,1)S(1)}, u32[]{:S(2)}, u32[]{:S(2)}) collective-permute-start(bf16[256,256]{1,0:T(8,128)(2,1)S(1)} %get-tuple-element.81), channel_id=1, source_target_pairs={{0,1},{1,0},{2,3},{3,2},{4,5},{5,4},{6,7},{7,6},{8,9},{9,8},{10,11... | collective-permute-start | bytes 393224 | tf_op jit(solution)/shard_map/ppermute | solution.py:420
  13.1 3.3 %collective-permute-start.22 = (bf16[256,256]{1,0:T(8,128)(2,1)S(1)}, bf16[256,256]{1,0:T(8,128)(2,1)S(1)}, u32[]{:S(2)}, u32[]{:S(2)}) collective-permute-start(bf16[256,256]{1,0:T(8,128)(2,1)S(1)} %get-tuple-element.82), channel_id=1, source_target_pairs={{1,2},{2,1},{3,4},{4,3},{5,6},{6,5},{9,10},{10,9},{11,12},{12,11},... | collective-permute-start | bytes 393224 | tf_op jit(solution)/shard_map/ppermute | solution.py:421
  16.4 0.7 copy-start.2
  16.4 0.7 copy-start.4
  52.5 9.1 %collective-permute-start.15 = (f32[1,8,1024]{2,1,0:T(8,128)S(1)}, f32[1,8,1024]{2,1,0:T(8,128)S(1)}, u32[]{:S(2)}, u32[]{:S(2)}) collective-permute-start(f32[1,8,1024]{2,1,0:T(8,128)S(1)} %bitcast.44), channel_id=1, source_target_pairs={{0,4},{1,5},{2,6},{3,7},{4,0},{5,1},{6,2},{7,3},{8,12},{9,13},{10,... | collective-permute-start | bytes 98312 | tf_op jit(solution)/shard_map/cond/branch_3_fun/ppermute | solution.py:445
  61.6 5.3 %collective-permute-start.16 = (f32[2,8,1024]{2,1,0:T(8,128)S(1)}, f32[2,8,1024]{2,1,0:T(8,128)S(1)}, u32[]{:S(2)}, u32[]{:S(2)}) collective-permute-start(f32[2,8,1024]{2,1,0:T(8,128)S(1)} %pad_maximum_fusion.11), channel_id=1, source_target_pairs={{0,2},{1,3},{2,0},{3,1},{4,6},{5,7},{6,4},{7,5},{8,10},{9,11},{10,... | collective-permute-start | bytes 196616 | tf_op jit(solution)/shard_map/cond/branch_3_fun/ppermute | solution.py:445
  66.9 5.0 %collective-permute-start.17 = (f32[4,8,1024]{2,1,0:T(8,128)S(1)}, f32[4,8,1024]{2,1,0:T(8,128)S(1)}, u32[]{:S(2)}, u32[]{:S(2)}) collective-permute-start(f32[4,8,1024]{2,1,0:T(8,128)S(1)} %pad_maximum_fusion.10), channel_id=1, source_target_pairs={{0,1},{1,0},{2,3},{3,2},{4,5},{5,4},{6,7},{7,6},{8,9},{9,8},{10,11... | collective-permute-start | bytes 393224 | tf_op jit(solution)/shard_map/cond/branch_3_fun/ppermute | solution.py:445
  67.0 11.2 %collective-permute-start.18 = (bf16[4,256,128]{2,1,0:T(8,128)(2,1)S(1)}, bf16[4,256,128]{2,1,0:T(8,128)(2,1)S(1)}, u32[]{:S(2)}, u32[]{:S(2)}) collective-permute-start(bf16[4,256,128]{2,1,0:T(8,128)(2,1)S(1)} %get-tuple-element.64.adj_ref), channel_id=1, source_target_pairs={{0,4},{4,0},{1,5},{5,1},{2,6},{6,2},{3,7},{7,3},{8,12},{12,8},{9,1... | collective-permute-start | bytes 786440 | tf_op jit(solution)/shard_map/cond/branch_3_fun/ppermute | solution.py:441
  80.2 5.7 %copy-start.5 = (f32[16,16]{1,0:T(8,128)}, f32[16,16]{1,0:T(8,128)S(1)}, u32[]{:S(2)}) copy-start(f32[16,16]{1,0:T(8,128)S(1)} %get-tuple-element.92) | copy-start | bytes 3076
  80.2 5.7 %collective-permute-start.23 = (bf16[4,128,128]{2,1,0:T(8,128)(2,1)S(1)}, bf16[4,128,128]{2,1,0:T(8,128)(2,1)S(1)}, u32[]{:S(2)}, u32[]{:S(2)}) collective-permute-start(bf16[4,128,128]{2,1,0:T(8,128)(2,1)S(1)} %get-tuple-element.86), channel_id=1, source_target_pairs={{0,8},{8,0},{1,9},{9,1},{2,10},{10,2},{3,11},{11,3},{4,12},{12,4},... | collective-permute-start | bytes 393224 | tf_op jit(solution)/shard_map/ppermute | solution.py:391

commit v2 on v1

--- a/solution.py
+++ b/solution.py
@@ -13,6 +13,7 @@
 HALO = 24
 LANES = 128
 STRIP = 32
+UNROLL = 64
 
 leakage = 0.05
 F32, BF16 = jnp.float32, jnp.bfloat16
@@ -109,7 +110,7 @@
 
 def sweep_kernel(total_cols, place_ref, corr_ref, taper_ref, cells_ref,
                  full_ref, split_ref, a_ref, b_ref, adj_ref, mom_ref,
-                 nat_ref, x_ref, s_ref, c_ref):
+                 nat_ref, xa_ref, xb_ref, s_ref, c_ref):
     wells, rows, _ = full_ref.shape
     groups = 8 // wells
     seg = rows // groups
@@ -203,55 +204,32 @@
         at = pl.multiple_of(t * (count * 8), count * 8)
         return [ref[pl.ds(at + 8 * i, 8), :] for i in range(count)]
 
-    def save(t, value):
+    def save(ref, t, value):
         at = pl.multiple_of(t * 16, 16)
         for p in range(2):
-            x_ref[pl.ds(at + 8 * p, 8), :] = value[p]
-
-    unroll = 8
-
-    def march(first_pass):
-        def rows_of(t0, carry, first_block):
-            x0, x1, y0, y1, coefs1, source1 = carry
-            for i in range(unroll):
-                t = t0 + i
-                coefs2 = load(c_ref, t, 8)
-                source2 = load(s_ref, t)
-                if first_pass:
-                    y2 = source2
-                else:
-                    x2 = load(x_ref, t + 2)
-                    y2 = update(x0, x1, x2, coefs2, source2)
-                    x0, x1 = x1, x2
-                if first_block and i == 0:
-                    y0 = [pair_swap(v, wells, True) for v in y2]
-                    y0, y1 = y0, y2
-                else:
-                    save(t, update(y0, y1, y2, coefs1, source1))
-                    y0, y1 = y1, y2
-                coefs1, source1 = coefs2, source2
-            return x0, x1, y0, y1, coefs1, source1
-
-        blank = [jnp.zeros((8, LANES), F32)] * 2
-        if first_pass:
-            x0 = x1 = blank
-        else:
-            x1 = load(x_ref, 1)
-            x0 = [pair_swap(v, wells, True) for v in x1]
-            last = load(x_ref, seg)
-            save(seg + 1, [pair_swap(v, wells, False) for v in last])
-        carry = rows_of(0, (x0, x1, blank, blank, None, None), True)
-        carry = lax.fori_loop(
-            1, seg // unroll, lambda b, c: rows_of(b * unroll, c, False), carry
-        )
-        _, _, y0, y1, coefs1, source1 = carry
-        y2 = [pair_swap(v, wells, False) for v in y1]
-        save(seg, update(y0, y1, y2, coefs1, source1))
-
-    march(True)
+            ref[pl.ds(at + 8 * p, 8), :] = value[p]
+
+    def march(from_ref, to_ref):
+        x1 = load(from_ref, 0)
+        x0 = [pair_swap(v, wells, True) for v in x1]
+        save(from_ref, seg, [pair_swap(v, wells, False) for v in load(from_ref, seg - 1)])
+
+        def rows_of(block, carry):
+            x0, x1 = carry
+            for i in range(UNROLL):
+                t = block * UNROLL + i
+                x2 = load(from_ref, t + 1)
+                save(to_ref, t, update(x0, x1, x2, load(c_ref, t, 8), load(s_ref, t)))
+                x0, x1 = x1, x2
+            return x0, x1
+
+        lax.fori_loop(0, seg // UNROLL, rows_of, (x0, x1))
+
+    march(s_ref, xa_ref)
 
     def more(_, carry):
-        march(False)
+        march(xa_ref, xb_ref)
+        march(xb_ref, xa_ref)
         return carry
 
     lax.fori_loop(0, SWEEPS // 2 - 1, more, 0)
@@ -284,9 +262,9 @@
         for g in range(groups):
             tiles = []
             for t in range(0, seg, 8):
-                at = (t + 1) * 16 + g * wells + w
+                at = t * 16 + g * wells + w
                 tiles.append(jnp.concatenate(
-                    [x_ref[pl.ds(at + 8 * p, 8, stride=16), :] for p in range(2)], axis=1
+                    [xa_ref[pl.ds(at + 8 * p, 8, stride=16), :] for p in range(2)], axis=1
                 ))
             value = dot(jnp.concatenate(tiles, axis=0).astype(BF16), order)
             if g % 2 == 1:
@@ -428,7 +406,8 @@
         [
             pltpu.VMEM((total_rows + 16, 2 * LANES), F32),
             pltpu.VMEM(((seg + 2) * 16, LANES), F32),
-            pltpu.VMEM((seg * 16, LANES), F32),
+            pltpu.VMEM(((seg + 2) * 16, LANES), F32),
+            pltpu.VMEM(((seg + 2) * 16, LANES), F32),
             pltpu.VMEM((seg * 64, LANES), F32),
         ],
     )
@@ -446,32 +425,37 @@
             gathered = jnp.concatenate([gathered, moved], axis=0)
             offsets = offsets + [offset ^ step for offset in offsets]
             step //= 2
-        samples = [gathered[i, 4] for i in range(col_count)]
-        while len(samples) > 1:
-            samples = [a + b for a, b in zip(samples[::2], samples[1::2])]
-        samples = samples[0].reshape(wells, total_rows)[:, : 2 * well_count]
-        samples = lax.all_gather(samples, "row", axis=0, tiled=True)
-        samples = lax.all_gather(samples, "sect", axis=0, tiled=True)
         half = ((wells, tile_rows, tile_cols), BF16)
         fields = call(
             functools.partial(mix_kernel, tuple(offsets), swapped, len(tiles)),
             (place, corr_len, taper_width), (adjoint, gathered, *tiles),
             [half, half] if swapped else [(tile, BF16)],
         )
-        return tuple(fields) + (samples.T,)
+        samples, *fields = lax.optimization_barrier((gathered[:, 4], *fields))
+        if swapped:
+            kept, sent = fields
+            other = exchanged(sent, "row")
+        samples = [samples[i] for i in range(col_count)]
+        while len(samples) > 1:
+            samples = [a + b for a, b in zip(samples[::2], samples[1::2])]
+        samples = samples[0].reshape(wells, total_rows)[:, : 2 * well_count]
+        if swapped:
+            theirs = exchanged(samples, "row")
+            low = row == 0
+            samples = jnp.concatenate(
+                [jnp.where(low, samples, theirs), jnp.where(low, theirs, samples)], axis=0
+            )
+            qh_fields = jnp.concatenate(
+                [jnp.where(low, kept, other), jnp.where(low, other, kept)], axis=0
+            )
+        else:
+            samples = lax.all_gather(samples, "row", axis=0, tiled=True)
+            qh_fields = lax.all_to_all(fields[0], "row", 1, 0, tiled=True)
+        samples = lax.all_gather(samples, "sect", axis=0, tiled=True)
+        return qh_fields[None], samples.T
 
     branches = [functools.partial(finish, distance) for distance in range(1, TAPER + 1)]
-    *fields, measure_cov = lax.switch(taper_width[1] - 1, branches, adjoint, moments)
-    if swapped:
-        kept, sent = fields
-        other = exchanged(sent, "row")
-        low = row == 0
-        qh_fields = jnp.concatenate(
-            [jnp.where(low, kept, other), jnp.where(low, other, kept)], axis=0
-        )
-    else:
-        qh_fields = lax.all_to_all(fields[0], "row", 1, 0, tiled=True)
-    return (qh_fields[None], measure_cov)
+    return lax.switch(taper_width[1] - 1, branches, adjoint, moments)
 
 
 def solution(mesh):

time: 86.9 us -> 64.4 us (0.74)
  Pallas kernels: 38.2 us -> 18.7 us
  blocking collectives: 6.12 us -> 1.79 us
  starting transfers between devices: 18.9 us -> 19.8 us
    pallas_call x3, Pallas kernels: 38.2 us -> 18.7 us  [call(): pl.pallas_call(kernel, in_specs=[SMEM] * len(smem) + [VMEM] * len(vmem),...]
    all_gather x1 -> x0, blocking collectives: 4.34 us -> none  [finish(): samples = lax.all_gather(samples, 'row', axis=0, tiled=True)]
    ppermute x1, waiting for transfers between devices: 0.01 us -> 2.98 us  [finish(): tiles.append(lax.ppermute(adjoint, 'col', pairs))]
    ppermute x3 -> x4, waiting for transfers between devices: 8.89 us -> 6.73 us  [exchanged(): return lax.ppermute(value, axis, [(0, 1), (1, 0)])]
    ppermute x3 -> x4, starting transfers between devices: 4.64 us -> 5.2 us  [exchanged(): return lax.ppermute(value, axis, [(0, 1), (1, 0)])]
  transfers between devices with their start and end apart: 9 -> 10, of which waited for: 6 -> 7; matrix products, arithmetic and copies ran while one was open for 1% -> 2% of each run, Pallas kernels for 0% -> 0%
where the time goes in v2:
time: 64.4 us; the launch traced here: 64.2 us
  starting transfers between devices  19.8 us (31%)
  Pallas kernels  18.7 us (29%)
  waiting for transfers between devices  17.8 us (28%)
  local copies, waits for them, and re-layouts  3.8 us (6%)
  blocking collectives  1.79 us (3%)
  between operations  1.34 us (2%)
  other arithmetic  0.91 us (1%)
    pallas_call x3, Pallas kernels, call(): pl.pallas_call(kernel, in_specs=[SMEM] * len(smem) + [VMEM] * len(vmem),...  18.7 us
    ppermute x3, starting transfers between devices, finish(): lax.ppermute(gathered, 'col', [(i, i ^ step) for i in range(col_count)])  9.21 us
    ppermute x3, waiting for transfers between devices, finish(): lax.ppermute(gathered, 'col', [(i, i ^ step) for i in range(col_count)])  6.77 us
    ppermute x4, waiting for transfers between devices, exchanged(): return lax.ppermute(value, axis, [(0, 1), (1, 0)])  6.73 us
    ppermute x4, starting transfers between devices, exchanged(): return lax.ppermute(value, axis, [(0, 1), (1, 0)])  5.2 us
    ppermute x1, waiting for transfers between devices, finish(): tiles.append(lax.ppermute(adjoint, 'col', pairs))  2.98 us
    ppermute x1, starting transfers between devices, finish(): tiles.append(lax.ppermute(adjoint, 'col', pairs))  2.91 us
    all_gather x1, blocking collectives, finish(): samples = lax.all_gather(samples, 'sect', axis=0, tiled=True)  1.79 us
  transfers between devices with their start and end apart: 10, of which 7 were waited for; matrix products, arithmetic and copies ran while one was open for 2% of the time, Pallas kernels for 0%

profile of v2, /device:TPU:0, one launch (start us, length us, event | category | flops | bytes accessed | tf_op | source)
XLA Modules:
  0.0 64.2 jit_solution(12447034794856327632)
XLA Ops:
  0.6 0.0 copy-start
  0.6 1.0 %dynamic-slice_bitcast_fusion = bf16[4,128,128]{2,1,0:T(8,128)(2,1)S(1)} fusion(bf16[1,8,128,128]{3,2,1,0:T(8,128)(2,1)} %param.13, s32[]{:T(128)S(6)} %select_n.87), kind=kLoop, calls=%fused_computation.44 | loop fusion | bytes 262148 | tf_op jit(solution)/shard_map/dynamic_slice | solution.py:386
  1.6 3.0 %collective-permute-start.27 = (bf16[4,128,128]{2,1,0:T(8,128)(2,1)S(1)}, bf16[4,128,128]{2,1,0:T(8,128)(2,1)S(1)}, u32[]{:S(2)}, u32[]{:S(2)}) collective-permute-start(bf16[4,128,128]{2,1,0:T(8,128)(2,1)S(1)} %dynamic-slice_bitcast_fusion), channel_id=1, source_target_pairs={{0,8},{8,0},{1,9},{9,1},{2,10},{10,2},{3,11},{11,3},{4,12},{12,4},... | collective-permute-start | bytes 393224 | tf_op jit(solution)/shard_map/ppermute | solution.py:369
  4.7 0.1 collective-permute-start.28
  4.7 0.1 pad_add_fusion.place_ref
  4.8 4.7 %collective-permute-done.28.refs_3_ = f32[128,128]{1,0:T(8,128)S(1)} collective-permute-done((f32[128,128]{1,0:T(8,128)}, f32[128,128]{1,0:T(8,128)S(1)}, u32[]{:S(2)}, u32[]{:S(2)}) %collective-permute-start.28) | collective-permute-done | bytes 65568 | tf_op jit(solution)/shard_map/ppermute | solution.py:369
  9.6 0.0 collective-permute-done.27.refs_1_
  9.6 0.0 copy-done
  9.6 0.0 copy-start.1
  9.6 0.8 %copy-done.1 = f32[128,128]{1,0:T(8,128)S(1)} copy-done((f32[128,128]{1,0:T(8,128)S(1)}, f32[128,128]{1,0:T(8,128)}, u32[]{:S(2)}) %copy-start.1) | copy-done | bytes 65560
  10.4 0.9 %shard_map.76 = (bf16[4,256,128]{2,1,0:T(8,128)(2,1)S(1)}, bf16[3,256,128]{2,1,0:T(8,128)(2,1)S(1)}, bf16[256,256]{1,0:T(8,128)(2,1)S(1)}, bf16[256,256]{1,0:T(8,128)(2,1)S(1)}) custom-call(s32[2]{0:T(128)S(1)} %pad_add_fusion.place_ref, bf16[8,128,128]{2,1,0:T(8,128)(2,1)S(1)} %bitcast.34, bf16[4,128,128]{2,1,0:T(8,128)(2,1)S(1)} %collective-permute-done.27.refs_1_, ...), custom_call_target="tpu_custom_call" | custom-call | flops 1 | bytes 1048576 | tf_op jit(solution)/shard_map/pallas_call | solution.py:349
  11.4 0.0 copy-start.3
  11.4 1.8 %collective-permute-start.29 = (bf16[256,256]{1,0:T(8,128)(2,1)S(1)}, bf16[256,256]{1,0:T(8,128)(2,1)S(1)}, u32[]{:S(2)}, u32[]{:S(2)}) collective-permute-start(bf16[256,256]{1,0:T(8,128)(2,1)S(1)} %get-tuple-element.102), channel_id=1, source_target_pairs={{0,1},{1,0},{2,3},{3,2},{4,5},{5,4},{6,7},{7,6},{8,9},{9,8},{10,11... | collective-permute-start | bytes 393224 | tf_op jit(solution)/shard_map/ppermute | solution.py:398
  13.1 0.7 %collective-permute-start.30 = (bf16[256,256]{1,0:T(8,128)(2,1)S(1)}, bf16[256,256]{1,0:T(8,128)(2,1)S(1)}, u32[]{:S(2)}, u32[]{:S(2)}) collective-permute-start(bf16[256,256]{1,0:T(8,128)(2,1)S(1)} %get-tuple-element.103), channel_id=1, source_target_pairs={{1,2},{2,1},{3,4},{4,3},{5,6},{6,5},{9,10},{10,9},{11,12},{12,11},... | collective-permute-start | bytes 393224 | tf_op jit(solution)/shard_map/ppermute | solution.py:399
  13.8 0.0 copy-done.3
  13.8 0.6 slice.123
  15.1 1.3 %collective-permute-done.29.a_ref = bf16[256,256]{1,0:T(8,128)(2,1)S(1)} collective-permute-done((bf16[256,256]{1,0:T(8,128)(2,1)S(1)}, bf16[256,256]{1,0:T(8,128)(2,1)S(1)}, u32[]{:S(2)}, u32[]{:S(2)}) %collective-permute-start.29) | collective-permute-done | bytes 131104 | tf_op jit(solution)/shard_map/ppermute | solution.py:398
  16.4 0.0 collective-permute-done.30.b_ref
  16.4 0.0 copy-start.2
  16.4 0.0 copy-start.4
  16.4 0.7 %copy-done.2 = s32[2,8]{1,0:T(2,128)S(1)} copy-done((s32[2,8]{1,0:T(2,128)S(1)}, s32[2,8]{1,0:T(2,128)}, u32[]{:S(2)}) %copy-start.2) | copy-done | bytes 88
  17.1 0.0 copy-done.4
  17.1 15.8 %shard_map.77 = (bf16[4,256,128]{2,1,0:T(8,128)(2,1)S(1)}, f32[8,1024]{1,0:T(8,128)S(1)}) custom-call(s32[2]{0:T(128)S(1)} %pad_add_fusion.place_ref, f32[2]{0:T(128)S(1)} %copy-done.4, s32[2]{0:T(128)S(1)} %copy-done.3, s32[2,8]{1,0:T(2,128)S(1)} %copy-done.2, bf16[4,256,128]{2,1,0:T(8,128)(2,1)S(1)} %get-tuple-element.100.full_ref, ...), custom_call_target="tpu_custom_call" | custom-call | flops 1 | bytes 1048576 | tf_op jit(solution)/shard_map/pallas_call | solution.py:349
  32.9 31.3 %conditional.1 = (bf16[1,8,128,128]{3,2,1,0:T(8,128)(2,1)}, f32[16,16]{1,0:T(8,128)}) conditional(s32[]{:T(128)} %bitcast.12, (s32[]{:T(128)}, f32[8,1024]{1,0:T(8,128)S(1)}, bf16[4,256,128]{2,1,0:T(8,128)(2,1)S(1)}, s32[2]{0:T(128)S(1)}, f32[2]{0:T(128)S(1)}, /*index=5*/s32[2]{0:T(128)S(1)}) %tuple.57, (s32[]{:T(128)}, ...), branch_computations={%region_0.1_spmd, %region_1.2_spmd, %region_2.3_spmd, %region_3.4_... | conditional | flops 548098 | bytes 6737203 | solution.py:458
  32.9 7.1 %collective-permute-start.21 = (f32[1,8,1024]{2,1,0:T(8,128)S(1)}, f32[1,8,1024]{2,1,0:T(8,128)S(1)}, u32[]{:S(2)}, u32[]{:S(2)}) collective-permute-start(f32[1,8,1024]{2,1,0:T(8,128)S(1)} %bitcast.47), channel_id=1, source_target_pairs={{0,4},{1,5},{2,6},{3,7},{4,0},{5,1},{6,2},{7,3},{8,12},{9,13},{10,... | collective-permute-start | bytes 98312 | tf_op jit(solution)/shard_map/cond/branch_3_fun/ppermute | solution.py:424
  40.1 2.0 %collective-permute-done.21 = f32[1,8,1024]{2,1,0:T(8,128)S(1)} collective-permute-done((f32[1,8,1024]{2,1,0:T(8,128)S(1)}, f32[1,8,1024]{2,1,0:T(8,128)S(1)}, u32[]{:S(2)}, u32[]{:S(2)}) %collective-permute-start.21) | collective-permute-done | bytes 32800 | tf_op jit(solution)/shard_map/cond/branch_3_fun/ppermute | solution.py:424
  42.1 1.8 %collective-permute-start.22 = (f32[2,8,1024]{2,1,0:T(8,128)S(1)}, f32[2,8,1024]{2,1,0:T(8,128)S(1)}, u32[]{:S(2)}, u32[]{:S(2)}) collective-permute-start(f32[2,8,1024]{2,1,0:T(8,128)S(1)} %pad_maximum_fusion.14), channel_id=1, source_target_pairs={{0,2},{1,3},{2,0},{3,1},{4,6},{5,7},{6,4},{7,5},{8,10},{9,11},{10,... | collective-permute-start | bytes 196616 | tf_op jit(solution)/shard_map/cond/branch_3_fun/ppermute | solution.py:424
  43.9 2.9 %collective-permute-start.24 = (bf16[4,256,128]{2,1,0:T(8,128)(2,1)S(1)}, bf16[4,256,128]{2,1,0:T(8,128)(2,1)S(1)}, u32[]{:S(2)}, u32[]{:S(2)}) collective-permute-start(bf16[4,256,128]{2,1,0:T(8,128)(2,1)S(1)} %get-tuple-element.86.adj_ref), channel_id=1, source_target_pairs={{0,4},{4,0},{1,5},{5,1},{2,6},{6,2},{3,7},{7,3},{8,12},{12,8},{9,1... | collective-permute-start | bytes 786440 | tf_op jit(solution)/shard_map/cond/branch_3_fun/ppermute | solution.py:420
  46.8 0.0 collective-permute-done.22
  46.8 0.3 collective-permute-start.23
  47.1 4.8 %collective-permute-done.23 = f32[4,8,1024]{2,1,0:T(8,128)S(1)} collective-permute-done((f32[4,8,1024]{2,1,0:T(8,128)S(1)}, f32[4,8,1024]{2,1,0:T(8,128)S(1)}, u32[]{:S(2)}, u32[]{:S(2)}) %collective-permute-start.23) | collective-permute-done | bytes 131104 | tf_op jit(solution)/shard_map/cond/branch_3_fun/ppermute | solution.py:424
  51.9 3.0 %collective-permute-done.24.refs_0_ = bf16[4,256,128]{2,1,0:T(8,128)(2,1)S(1)} collective-permute-done((bf16[4,256,128]{2,1,0:T(8,128)(2,1)S(1)}, bf16[4,256,128]{2,1,0:T(8,128)(2,1)S(1)}, u32[]{:S(2)}, u32[]{:S(2)}) %collective-permute-start.24) | collective-permute-done | bytes 262176 | tf_op jit(solution)/shard_map/cond/branch_3_fun/ppermute | solution.py:420
  54.9 1.9 %branch_3_fun.1 = (bf16[4,128,128]{2,1,0:T(8,128)(2,1)S(1)}, bf16[4,128,128]{2,1,0:T(8,128)(2,1)S(1)}) custom-call(s32[2]{0:T(128)S(1)} %get-tuple-element.83.place_ref, f32[2]{0:T(128)S(1)} %get-tuple-element.84.corr_ref, s32[2]{0:T(128)S(1)} %get-tuple-element.85.taper_ref, bf16[4,256,128]{2,1,0:T(8,128)(2,1)S(1)} %get-tuple-element.86.adj_ref, ...), custom_call_target="tpu_custom_call" | custom-call | flops 1 | bytes 1048576 | tf_op jit(solution)/shard_map/cond/branch_3_fun/pallas_call | solution.py:349
  56.9 1.6 %collective-permute-start.26 = (f32[4,16]{1,0:T(4,128)S(1)}, f32[4,16]{1,0:T(4,128)S(1)}, u32[]{:S(2)}, u32[]{:S(2)}) collective-permute-start(f32[4,16]{1,0:T(4,128)S(1)} %slice.131), channel_id=1, source_target_pairs={{0,8},{8,0},{1,9},{9,1},{2,10},{10,2},{3,11},{11,3},{4,12},{12,4},... | collective-permute-start | bytes 776 | tf_op jit(solution)/shard_map/cond/branch_3_fun/ppermute | solution.py:369
  58.5 0.5 collective-permute-start.25
  59.0 1.6 %collective-permute-done.26 = f32[4,16]{1,0:T(4,128)S(1)} collective-permute-done((f32[4,16]{1,0:T(4,128)S(1)}, f32[4,16]{1,0:T(4,128)S(1)}, u32[]{:S(2)}, u32[]{:S(2)}) %collective-permute-start.26) | collective-permute-done | bytes 288 | tf_op jit(solution)/shard_map/cond/branch_3_fun/ppermute | solution.py:369
  60.6 1.8 %all_gather.11 = f32[16,16]{1,0:T(8,128)S(1)} all-gather(f32[8,16]{1,0:T(8,128)S(1)} %pad_maximum_fusion.15), channel_id=1, replica_groups=mesh['sect'=2,'row'=2,'col'=8] {'sect'}, dimensions={0}, use_global_device_ids=true | all-gather | bytes 1536 | tf_op jit(solution)/shard_map/cond/branch_3_fun/all_gather | solution.py:454
  62.4 0.7 %copy.19 = f32[16,16]{1,0:T(8,128)} copy(f32[16,16]{0,1:T(8,128)S(1)} %bitcast.58) | data formatting | bytes 2048 | tf_op jit(solution)/shard_map/cond | solution.py:458
  63.0 0.4 collective-permute-done.25
  63.5 0.7 %maximum_bitcast_fusion.3 = bf16[1,8,128,128]{3,2,1,0:T(8,128)(2,1)} fusion(bf16[4,128,128]{2,1,0:T(8,128)(2,1)S(1)} %get-tuple-element.124, bf16[4,128,128]{2,1,0:T(8,128)(2,1)S(1)} %get-tuple-element.123), kind=kLoop, calls=%fused_computation.34 | loop fusion | flops 131072 | bytes 524288 | tf_op jit(solution)/shard_map/cond/branch_3_fun/broadcast_in_dim | solution.py:455
  (11 shorter events, 0.2 us)
Async XLA Ops:
  0.6 8.9 %copy-start = (bf16[1,8,128,128]{3,2,1,0:T(8,128)(2,1)S(1)}, bf16[1,8,128,128]{3,2,1,0:T(8,128)(2,1)}, u32[]{:S(2)}) copy-start(bf16[1,8,128,128]{3,2,1,0:T(8,128)(2,1)} %param.13) | copy-start | bytes 786436
  1.6 7.9 %collective-permute-start.27 = (bf16[4,128,128]{2,1,0:T(8,128)(2,1)S(1)}, bf16[4,128,128]{2,1,0:T(8,128)(2,1)S(1)}, u32[]{:S(2)}, u32[]{:S(2)}) collective-permute-start(bf16[4,128,128]{2,1,0:T(8,128)(2,1)S(1)} %dynamic-slice_bitcast_fusion), channel_id=1, source_target_pairs={{0,8},{8,0},{1,9},{9,1},{2,10},{10,2},{3,11},{11,3},{4,12},{12,4},... | collective-permute-start | bytes 393224 | tf_op jit(solution)/shard_map/ppermute | solution.py:369
  4.7 4.9 %collective-permute-start.28 = (f32[128,128]{1,0:T(8,128)}, f32[128,128]{1,0:T(8,128)S(1)}, u32[]{:S(2)}, u32[]{:S(2)}) collective-permute-start(f32[128,128]{1,0:T(8,128)} %refs_2_.1), channel_id=1, source_target_pairs={{0,8},{8,0},{1,9},{9,1},{2,10},{10,2},{3,11},{11,3},{4,12},{12,4},... | collective-permute-start | bytes 196616 | tf_op jit(solution)/shard_map/ppermute | solution.py:369
  9.6 0.8 %copy-start.1 = (f32[128,128]{1,0:T(8,128)S(1)}, f32[128,128]{1,0:T(8,128)}, u32[]{:S(2)}) copy-start(f32[128,128]{1,0:T(8,128)} %refs_2_.1) | copy-start | bytes 196612
  11.4 2.5 %copy-start.3 = (s32[2]{0:T(128)S(1)}, s32[2]{0:T(128)}, u32[]{:S(2)}) copy-start(s32[2]{0:T(128)} %taper_ref.1) | copy-start | bytes 28
  11.4 5.0 %collective-permute-start.29 = (bf16[256,256]{1,0:T(8,128)(2,1)S(1)}, bf16[256,256]{1,0:T(8,128)(2,1)S(1)}, u32[]{:S(2)}, u32[]{:S(2)}) collective-permute-start(bf16[256,256]{1,0:T(8,128)(2,1)S(1)} %get-tuple-element.102), channel_id=1, source_target_pairs={{0,1},{1,0},{2,3},{3,2},{4,5},{5,4},{6,7},{7,6},{8,9},{9,8},{10,11... | collective-permute-start | bytes 393224 | tf_op jit(solution)/shard_map/ppermute | solution.py:398
  13.1 3.3 %collective-permute-start.30 = (bf16[256,256]{1,0:T(8,128)(2,1)S(1)}, bf16[256,256]{1,0:T(8,128)(2,1)S(1)}, u32[]{:S(2)}, u32[]{:S(2)}) collective-permute-start(bf16[256,256]{1,0:T(8,128)(2,1)S(1)} %get-tuple-element.103), channel_id=1, source_target_pairs={{1,2},{2,1},{3,4},{4,3},{5,6},{6,5},{9,10},{10,9},{11,12},{12,11},... | collective-permute-start | bytes 393224 | tf_op jit(solution)/shard_map/ppermute | solution.py:399
  16.4 0.7 %copy-start.2 = (s32[2,8]{1,0:T(2,128)S(1)}, s32[2,8]{1,0:T(2,128)}, u32[]{:S(2)}) copy-start(s32[2,8]{1,0:T(2,128)} %cells_ref.1) | copy-start | bytes 196
  16.4 0.7 %copy-start.4 = (f32[2]{0:T(128)S(1)}, f32[2]{0:T(128)}, u32[]{:S(2)}) copy-start(f32[2]{0:T(128)} %corr_ref.1) | copy-start | bytes 28
  32.9 9.1 %collective-permute-start.21 = (f32[1,8,1024]{2,1,0:T(8,128)S(1)}, f32[1,8,1024]{2,1,0:T(8,128)S(1)}, u32[]{:S(2)}, u32[]{:S(2)}) collective-permute-start(f32[1,8,1024]{2,1,0:T(8,128)S(1)} %bitcast.47), channel_id=1, source_target_pairs={{0,4},{1,5},{2,6},{3,7},{4,0},{5,1},{6,2},{7,3},{8,12},{9,13},{10,... | collective-permute-start | bytes 98312 | tf_op jit(solution)/shard_map/cond/branch_3_fun/ppermute | solution.py:424
  42.1 4.7 %collective-permute-start.22 = (f32[2,8,1024]{2,1,0:T(8,128)S(1)}, f32[2,8,1024]{2,1,0:T(8,128)S(1)}, u32[]{:S(2)}, u32[]{:S(2)}) collective-permute-start(f32[2,8,1024]{2,1,0:T(8,128)S(1)} %pad_maximum_fusion.14), channel_id=1, source_target_pairs={{0,2},{1,3},{2,0},{3,1},{4,6},{5,7},{6,4},{7,5},{8,10},{9,11},{10,... | collective-permute-start | bytes 196616 | tf_op jit(solution)/shard_map/cond/branch_3_fun/ppermute | solution.py:424
  43.9 11.0 %collective-permute-start.24 = (bf16[4,256,128]{2,1,0:T(8,128)(2,1)S(1)}, bf16[4,256,128]{2,1,0:T(8,128)(2,1)S(1)}, u32[]{:S(2)}, u32[]{:S(2)}) collective-permute-start(bf16[4,256,128]{2,1,0:T(8,128)(2,1)S(1)} %get-tuple-element.86.adj_ref), channel_id=1, source_target_pairs={{0,4},{4,0},{1,5},{5,1},{2,6},{6,2},{3,7},{7,3},{8,12},{12,8},{9,1... | collective-permute-start | bytes 786440 | tf_op jit(solution)/shard_map/cond/branch_3_fun/ppermute | solution.py:420
  46.8 5.0 %collective-permute-start.23 = (f32[4,8,1024]{2,1,0:T(8,128)S(1)}, f32[4,8,1024]{2,1,0:T(8,128)S(1)}, u32[]{:S(2)}, u32[]{:S(2)}) collective-permute-start(f32[4,8,1024]{2,1,0:T(8,128)S(1)} %pad_maximum_fusion.13), channel_id=1, source_target_pairs={{0,1},{1,0},{2,3},{3,2},{4,5},{5,4},{6,7},{7,6},{8,9},{9,8},{10,11... | collective-permute-start | bytes 393224 | tf_op jit(solution)/shard_map/cond/branch_3_fun/ppermute | solution.py:424
  56.9 3.7 %collective-permute-start.26 = (f32[4,16]{1,0:T(4,128)S(1)}, f32[4,16]{1,0:T(4,128)S(1)}, u32[]{:S(2)}, u32[]{:S(2)}) collective-permute-start(f32[4,16]{1,0:T(4,128)S(1)} %slice.131), channel_id=1, source_target_pairs={{0,8},{8,0},{1,9},{9,1},{2,10},{10,2},{3,11},{11,3},{4,12},{12,4},... | collective-permute-start | bytes 776 | tf_op jit(solution)/shard_map/cond/branch_3_fun/ppermute | solution.py:369
  58.5 5.0 %collective-permute-start.25 = (bf16[4,128,128]{2,1,0:T(8,128)(2,1)S(1)}, bf16[4,128,128]{2,1,0:T(8,128)(2,1)S(1)}, u32[]{:S(2)}, u32[]{:S(2)}) collective-permute-start(bf16[4,128,128]{2,1,0:T(8,128)(2,1)S(1)} %get-tuple-element.90), channel_id=1, source_target_pairs={{0,8},{8,0},{1,9},{9,1},{2,10},{10,2},{3,11},{11,3},{4,12},{12,4},... | collective-permute-start | bytes 393224 | tf_op jit(solution)/shard_map/cond/branch_3_fun/ppermute | solution.py:369

commit v3 on v0

v3 whole, which is shorter than its diff:
```python
import functools

import jax
import jax.numpy as jnp
from jax import lax
from jax.experimental import pallas as pl
from jax.experimental.pallas import tpu as pltpu
from jax.sharding import PartitionSpec as P

BLOCK = 128
TAPER = 4
SWEEPS = 24
HALO = 24
LANES = 128
STRIP = 32
PACK = LANES // STRIP
CHUNKS = 1
UNROLL = 16

leakage = 0.05
F32, BF16 = jnp.float32, jnp.bfloat16


def iota(shape, dim):
    return lax.broadcasted_iota(jnp.int32, shape, dim)


def one_hot(mask):
    return jnp.where(mask, 1.0, 0.0).astype(BF16)


def dot(a, b):
    return jnp.dot(a, b, preferred_element_type=F32)


def harmonic(a, b):
    return 2.0 * a * b / (a + b)


def factor(offset, scale, reach):
    distance = jnp.abs(offset).astype(F32)
    return jnp.exp(-distance / scale) * jnp.maximum(1.0 - distance / reach, 0.0)


def scales(corr_ref, taper_ref, total_rows):
    row_scale = corr_ref[0] * (total_rows / 4.0)
    row_reach = (taper_ref[0] + TAPER).astype(F32) * (total_rows / (2.0 * TAPER)) + 1.0
    col_scale = corr_ref[1] * BLOCK
    col_reach = (taper_ref[1] * BLOCK + 1).astype(F32)
    return row_scale, row_reach, col_scale, col_reach


def split3(value):
    pieces = []
    for _ in range(3):
        piece = value.astype(BF16)
        pieces.append(piece)
        value = value - piece.astype(F32)
    return pieces


def strip_slot(lane, wells):
    slot, k = lane // HALO, lane % HALO
    return jnp.where(slot <= wells, slot, -1), k


def strips(place_ref, fields, logs):
    even = lax.rem(place_ref[1], 2) == 0
    tail = LANES - HALO
    start_a = jnp.where(even, tail, 0)
    rows = fields[0].shape[0]
    values = jnp.concatenate(fields + [logs[0]], axis=1)
    shape = (values.shape[1], 2 * LANES)
    src, dst = iota(shape, 0), iota(shape, 1)
    slot, k = strip_slot(dst % LANES, len(fields))
    start = jnp.where(dst < LANES, start_a, tail - start_a)
    first = dot(values, one_hot((slot == src // LANES) & (src % LANES == k + start)))
    shape = (LANES, 2 * LANES)
    src, dst = iota(shape, 0), iota(shape, 1)
    start = jnp.where(dst < LANES, start_a, tail - start_a)
    k = dst % STRIP
    wide = dot(logs[1], one_hot((src == k + start) & (k < HALO)))
    block = rows // PACK
    lane = iota((block, 2 * LANES), 1) % LANES // STRIP
    second = jnp.zeros((block, 2 * LANES), F32)
    for q in range(PACK):
        second = jnp.where(lane == q, wide[q * block : (q + 1) * block], second)
    return [
        (first[:, at : at + LANES].astype(BF16), second[:, at : at + LANES].astype(BF16))
        for at in (0, LANES)
    ]


def split_kernel(place_ref, obs_ref, lt_ref, sent_ref, kept_ref, planes_ref, logs_ref, sems):
    wells = sent_ref.shape[0]
    mine = place_ref[0] * wells
    copies = [
        pltpu.make_async_copy(lt_ref, logs_ref, sems.at[0]),
        pltpu.make_async_copy(obs_ref.at[pl.ds(wells - mine, wells)], sent_ref, sems.at[1]),
        pltpu.make_async_copy(obs_ref.at[pl.ds(mine, wells)], kept_ref, sems.at[2]),
    ]
    for copy in copies:
        copy.start()
    copies[0].wait()
    for i, piece in enumerate(split3(logs_ref[...])):
        planes_ref[i] = piece
    copies[1].wait()
    copies[2].wait()


def row_parts(swapped, place_ref, refs, rows):
    if not swapped:
        obs_ref, lt_ref = refs
        return [(pl.ds(0, rows), [obs_ref[w] for w in range(obs_ref.shape[0])], split3(lt_ref[...]))]
    kept_ref, planes_ref, recv_ref, lt_ref = refs
    half = rows // 2
    mine = pl.multiple_of(place_ref[0] * half, half)
    other = pl.multiple_of(half - mine, half)
    wells = kept_ref.shape[0]
    return [
        (pl.ds(mine, half), [kept_ref[w] for w in range(wells)], [planes_ref[i] for i in range(3)]),
        (pl.ds(other, half), [recv_ref[w] for w in range(wells)], split3(lt_ref[...])),
    ]


def pack_kernel(swapped, place_ref, *refs):
    out_refs = refs[-2:]
    rows = out_refs[0].shape[0] * PACK // (PACK + 1)
    for where, fields, logs in row_parts(swapped, place_ref, refs[:-2], rows):
        block = where.size // PACK
        after = pl.multiple_of(rows + lax.div(where.start, PACK), 8)
        for ref, (first, second) in zip(out_refs, strips(place_ref, fields, logs)):
            ref[where, :] = first
            ref[pl.ds(after, block), :] = second


def layout(wells):
    width = LANES // wells
    return width, -(-(LANES + 2 * HALO) // width)


def fold_rows(rows, transposed=False):
    at, row = iota((rows, rows), int(transposed)), iota((rows, rows), 1 - int(transposed))
    seg = rows // 8
    t, g = at // 8, at % 8
    return one_hot(row == jnp.where(g % 2 == 0, g * seg + t, (g + 1) * seg - 1 - t))


def window_column(wells, shape, dim):
    width, parts = layout(wells)
    lane = iota(shape, dim)
    return parts * (lane % width) + lane // LANES, (lane % LANES) // width


def own_kernel(swapped, wells, total_cols, place_ref, corr_ref, taper_ref, cells_ref, *refs):
    field_ref, log_ref, basis_ref, rw_ref, cw_ref, all_ref = refs[-6:]
    rows = field_ref.shape[0]
    parts = layout(wells)[1]
    for where, fields, logs in row_parts(swapped, place_ref, refs[:-6], rows):
        for i, value in enumerate(fields + logs):
            all_ref[where, i * LANES : (i + 1) * LANES] = value
    folded = dot(fold_rows(rows), all_ref[...]).astype(BF16)
    edge = wells * LANES
    shape = (edge, parts * LANES)
    column, well = window_column(wells, shape, 1)
    src = iota(shape, 0)
    pick = one_hot((column == src % LANES + HALO) & (well == src // LANES))
    field_ref[...] = dot(folded[:, :edge], pick)
    shape = (3 * LANES, parts * LANES)
    column, _ = window_column(wells, shape, 1)
    pick = one_hot(column == iota(shape, 0) % LANES + HALO)
    log_ref[...] = dot(folded[:, edge:], pick)
    col = place_ref[1]
    row_scale, row_reach, col_scale, col_reach = scales(corr_ref, taper_ref, rows)
    kind, c = iota((8, LANES), 0), iota((8, LANES), 1)
    reach = jnp.where(kind % 4 < 2, LANES - c, c + 1).astype(F32)
    basis = jnp.exp(-reach / col_scale) * jnp.where(kind % 2 == 0, 1.0, reach / LANES)
    high = basis.astype(BF16)
    basis_ref[...] = jnp.where(kind < 4, high.astype(F32), basis - high.astype(F32)).astype(BF16)
    m_lane = iota((1, LANES), 1)
    cell = jnp.full((1, LANES), -1, jnp.int32)
    batches, per_batch = cells_ref.shape
    for b in range(batches):
        for n in range(per_batch):
            cell = jnp.where(m_lane == b * per_batch + n, cells_ref[b, n], cell)
    cell_row, cell_col = lax.div(cell, total_cols), lax.rem(cell, total_cols)
    row_weight = factor(cell_row - iota((rows, LANES), 0), row_scale, row_reach)
    rw_ref[...] = row_weight.astype(BF16).astype(F32)
    cw_ref[...] = factor(
        cell_col - (col * LANES + iota((LANES, LANES), 0)), col_scale, col_reach
    ).astype(BF16)


def seam(value, outer):
    group = iota(value.shape, 0)
    up = pltpu.roll(value, 1, 0)
    down = pltpu.roll(value, 7, 0)
    return jnp.where((group % 2 == 0) == (not outer), down, up)


def sweep_kernel(wells, tile_rows, total_cols, place_ref, field_ref, log_ref, basis_ref, rw_ref,
                 cw_ref, a_ref, b_ref, *refs):
    adj_refs = refs[:-5]
    mom_ref, xa_ref, xb_ref, s_ref, c_ref = refs[-5:]
    rows = field_ref.shape[0]
    seg = rows // 8
    width, parts = layout(wells)
    col = place_ref[1]
    even = lax.rem(col, 2) == 0
    a, b = a_ref[...], b_ref[...]
    sides = []
    for side in (jnp.where(even, b, a), jnp.where(even, a, b)):
        block = tile_rows // PACK
        blank = jnp.zeros((block, LANES), BF16)
        quarter = iota((block, LANES), 1) // STRIP
        second = [
            jnp.where(quarter == q, side[rows + p * block : rows + (p + 1) * block], blank)
            for p in range(rows // tile_rows) for q in range(PACK)
        ]
        sides.append((side[:rows], jnp.concatenate(second, axis=0)))
    strip = jnp.concatenate([sides[0][0], sides[1][0], sides[0][1], sides[1][1]], axis=1)
    folded = dot(fold_rows(rows), strip).astype(BF16)
    shape = (2 * LANES, parts * LANES)
    column, well = window_column(wells, shape, 1)
    src = iota(shape, 0)
    base = jnp.where(src < LANES, 0, LANES + HALO)
    slot, k = strip_slot(src % LANES, wells)
    hit = column == k + base
    k = src % STRIP
    again = (k < HALO) & (column == k + base)
    fields = field_ref[...] + dot(folded[:, : 2 * LANES], one_hot(hit & (slot == well)))
    logs = log_ref[...] + dot(folded[:, : 2 * LANES], one_hot(hit & (slot == wells)))
    logs = logs + dot(folded[:, 2 * LANES :], one_hot(again))

    cond = jnp.exp(logs)
    cond = [cond[:, i * LANES : (i + 1) * LANES] for i in range(parts)]
    lane = iota((1, LANES), 1)
    group = iota((8, LANES), 0)
    border = (group == 0) | (group == 7)
    east = [harmonic(cond[i], cond[i + 1]) for i in range(parts - 1)]
    east.append(harmonic(cond[-1], pltpu.roll(cond[0], LANES - 1, 1)))
    west = [pltpu.roll(east[-1], 1, 1)] + east[:-1]
    for i in range(parts):
        place = parts * (lane % width) + i
        column = col * LANES - HALO + place
        inside = (column >= 0) & (column < total_cols) & (place < LANES + 2 * HALO)
        here = cond[i]
        inner = harmonic(here, jnp.concatenate([here[8:], seam(here[-8:], False)], axis=0))
        first = harmonic(here[:8], seam(here[:8], True))
        outer = jnp.concatenate([jnp.where(border, here[:8], first), inner[:-8]], axis=0)
        fe = jnp.where(column < total_cols - 1, east[i], here)
        fw = jnp.where(column > 0, west[i], here)
        inverse = jnp.where(inside, 1.0 / (fe + fw + outer + inner + leakage), 0.0)
        values = [fe * inverse, fw * inverse, outer * inverse, inner * inverse]
        source = fields[:, i * LANES : (i + 1) * LANES] * inverse
        for t in range(seg):
            s_ref[(t * parts + i) * 8 : (t * parts + i + 1) * 8, :] = source[8 * t : 8 * t + 8]
            for d in range(4):
                at = ((t * parts + i) * 4 + d) * 8
                value = values[d][8 * t : 8 * t + 8]
                if t == 0 and d == 2:
                    value = jnp.where(border, 0.0, value)
                c_ref[at : at + 8, :] = value

    def load(ref, t, count=parts):
        at = t * (count * 8)
        at = at if isinstance(at, int) else pl.multiple_of(at, 8)
        return [ref[pl.ds(at + 8 * i, 8), :] for i in range(count)]

    def save(ref, t, value):
        at = t * (parts * 8)
        at = at if isinstance(at, int) else pl.multiple_of(at, 8)
        for i in range(parts):
            ref[pl.ds(at + 8 * i, 8), :] = value[i]

    def update(previous, current, following, coefs, source):
        easts = current[1:] + [pltpu.roll(current[0], LANES - 1, 1)]
        wests = [pltpu.roll(current[-1], 1, 1)] + current[:-1]
        result = []
        for i in range(parts):
            ce, cw, co, ci = coefs[4 * i : 4 * i + 4]
            result.append(
                ((source[i] + co * previous[i]) + ci * following[i])
                + (ce * easts[i] + cw * wests[i])
            )
        return result

    unroll = min(UNROLL, seg)

    def march(from_ref, to_ref):
        x1 = load(from_ref, 0)
        x0 = [seam(v, True) for v in x1]
        save(from_ref, seg, [seam(v, False) for v in load(from_ref, seg - 1)])

        def rows_of(block, carry):
            x0, x1 = carry
            for i in range(unroll):
                t = block * unroll + i
                x2 = load(from_ref, t + 1)
                save(to_ref, t, update(x0, x1, x2, load(c_ref, t, 4 * parts), load(s_ref, t)))
                x0, x1 = x1, x2
            return x0, x1

        if seg == unroll:
            rows_of(0, (x0, x1))
        else:
            lax.fori_loop(0, seg // unroll, rows_of, (x0, x1))

    march(s_ref, xa_ref)

    def more(_, carry):
        march(xa_ref, xb_ref)
        march(xb_ref, xa_ref)
        return carry

    lax.fori_loop(0, SWEEPS // 2 - 1, more, 0)

    state = jnp.concatenate(
        [
            jnp.concatenate(
                [xa_ref[(t * parts + i) * 8 : (t * parts + i + 1) * 8, :] for t in range(seg)], axis=0
            ).astype(BF16)
            for i in range(parts)
        ],
        axis=1,
    )
    shape = (parts * LANES, wells * LANES)
    column, well = window_column(wells, shape, 0)
    dst = iota(shape, 1)
    order = one_hot((column == dst % LANES + HALO) & (well == dst // LANES))
    adjoints = dot(fold_rows(rows, True), dot(state, order).astype(BF16)).astype(BF16)
    mom_ref[...] = jnp.zeros(mom_ref.shape, F32)
    span = wells * rows // 2
    both = []
    for w in range(wells):
        adjoint = adjoints[:, w * LANES : (w + 1) * LANES]
        adj_refs[w // adj_refs[0].shape[0]][w % adj_refs[0].shape[0]] = adjoint
        both.append(lax.dot_general(
            basis_ref[...], adjoint, (((1,), (1,)), ((), ())), preferred_element_type=F32
        ))
        sampled = dot(adjoint, cw_ref[...]) * rw_ref[...]
        mom_ref[w : w + 1, span : span + LANES] = jnp.sum(sampled, axis=0, keepdims=True)
    both = jnp.concatenate(both, axis=1)
    both = both[0:4] + both[4:8]
    for h in range(2):
        mom_ref[4 * h : 4 * h + 4, :span] = both[:, h * span : (h + 1) * span]


def moment(mom_ref, index, which):
    span = mom_ref.shape[2] - LANES
    return jnp.concatenate(
        [mom_ref[index, which + 4 * h : which + 4 * h + 1, :span] for h in range(2)], axis=1
    )


def factor_kernel(place_ref, corr_ref, taper_ref, mats_ref, row_ref, spread_ref):
    rows = row_ref.shape[0]
    col, taper = place_ref[1], taper_ref[1]
    row_scale, row_reach, col_scale, col_reach = scales(corr_ref, taper_ref, rows)
    kind, c = iota((16, LANES), 0), iota((16, LANES), 1)
    near = jnp.where(kind % 4 < 2, c, LANES - 1 - c).astype(F32)
    spread = jnp.exp(-near / col_scale) * jnp.where(
        kind % 2 == 0, 1.0 - near / col_reach, -LANES / col_reach
    )
    high = spread.astype(BF16).astype(F32)
    spread = jnp.where(kind < 8, high, jnp.where(kind < 12, spread - high, 0.0))
    spread_ref[...] = spread.astype(BF16)
    src, dst = iota((LANES, LANES), 0), iota((LANES, LANES), 1)
    even = lax.rem(lax.div(col, taper), 2) == 0
    shift = jnp.where(even, taper, -taper) * LANES
    for i, away in enumerate((0, shift, -shift)):
        mats_ref[i] = factor(dst - src - away, col_scale, col_reach).astype(BF16)
    offset = iota((rows, rows), 0) - iota((rows, rows), 1)
    row_ref[...] = factor(offset, row_scale, row_reach).astype(BF16)


def moment_kernel(offsets, place_ref, corr_ref, taper_ref, mom_ref, mats_ref, spread_ref, *refs):
    half = len(refs) // 2
    adj_refs, out_refs = refs[:half], refs[half:]
    col, taper = place_ref[1], taper_ref[1]
    col_scale = corr_ref[1] * BLOCK
    scale_v = jnp.ones((1, LANES), F32) * col_scale
    per, rows, _ = adj_refs[0].shape
    span = half * per * rows
    sums = [jnp.zeros((1, span), F32) for _ in range(4)]
    for index, offset in enumerate(offsets):
        if offset == 0:
            continue
        away = lax.bitwise_xor(col, offset) - col
        for side, k in ((0, -away), (1, away)):
            live = (k >= 1) & (k < taper)
            gap = jnp.maximum(k - 1, 0).astype(F32)
            gain = jnp.where(live, 1.0, 0.0) * jnp.exp(-gap * LANES / scale_v)
            gain = gain[:, :1]
            zero = moment(mom_ref, index, 2 * side)
            one = moment(mom_ref, index, 2 * side + 1)
            sums[2 * side] = sums[2 * side] + gain * zero
            sums[2 * side + 1] = sums[2 * side + 1] + gain * (gap * zero + one)
    stacked = jnp.concatenate(sums * 4, axis=0)
    kind = iota((16, span), 0)
    high = stacked.astype(BF16).astype(F32)
    stacked = jnp.where((kind >= 4) & (kind < 8), stacked - high, high).astype(BF16)
    for w in range(half * per):
        base = lax.dot_general(
            stacked[:, w * rows : (w + 1) * rows], spread_ref[...],
            (((0,), (0,)), ((), ())), preferred_element_type=F32,
        )
        out_refs[w // per][w % per] = base + dot(adj_refs[w // per][w % per], mats_ref[0])


def mix_kernel(swapped, tiles, place_ref, base_ref, mats_ref, row_ref, *refs):
    out_refs = refs[tiles:]
    wells, rows, _ = base_ref.shape
    for w in range(wells):
        mixed = base_ref[w]
        for i in range(tiles):
            mixed = mixed + dot(refs[i][w], mats_ref[1 + i])
        field = dot(row_ref[...], mixed.astype(BF16)).astype(BF16)
        if swapped:
            half = rows // 2
            keep = place_ref[0] == 0
            out_refs[0][w] = jnp.where(keep, field[:half], field[half:])
            out_refs[1][w] = jnp.where(keep, field[half:], field[:half])
        else:
            out_refs[0][w] = field


VMEM = pl.BlockSpec(memory_space=pltpu.VMEM)
SMEM = pl.BlockSpec(memory_space=pltpu.SMEM)


def call(kernel, smem, vmem, outs, scratch=(), flops=1, whole=VMEM, limit=48 * 2**20):
    return pl.pallas_call(
        kernel,
        in_specs=[SMEM] * len(smem) + [whole] * len(vmem),
        out_specs=[VMEM] * len(outs),
        out_shape=[jax.ShapeDtypeStruct(shape, dtype) for shape, dtype in outs],
        scratch_shapes=list(scratch),
        compiler_params=pltpu.CompilerParams(vmem_limit_bytes=limit),
        cost_estimate=pl.CostEstimate(flops=flops, bytes_accessed=2**20, transcendentals=0),
    )(*smem, *vmem)


def pairs_at(count, distance, odd):
    pairs = []
    for i in range(count - distance):
        if (i // distance) % 2 == odd:
            pairs += [(i, i + distance), (i + distance, i)]
    return pairs


def exchanged(value, axis):
    return lax.ppermute(value, axis, [(0, 1), (1, 0)])


def local(log_trans, corr_len, taper_width, well_cells, obs_weight):
    tile_rows, tile_cols = log_trans.shape
    row_count, col_count = lax.axis_size("row"), lax.axis_size("col")
    total_rows, total_cols = tile_rows * row_count, tile_cols * col_count
    well_count = well_cells.shape[1]
    wells = well_count // row_count
    row, col = lax.axis_index("row"), lax.axis_index("col")
    place = jnp.stack([row, col]).astype(jnp.int32)
    own = obs_weight[0]
    swapped = row_count == 2
    tile = (wells, total_rows, tile_cols)

    if swapped:
        half = ((wells, tile_rows, tile_cols), BF16)
        sent, kept, planes = call(
            split_kernel, (place,), (own, log_trans),
            [half, half, ((3, tile_rows, tile_cols), BF16)],
            [pltpu.VMEM((tile_rows, tile_cols), F32), pltpu.SemaphoreType.DMA((3,))],
            whole=pl.BlockSpec(memory_space=pl.ANY),
        )
        operands = (kept, planes, exchanged(sent, "row"), exchanged(log_trans, "row"))
    else:
        operands = (
            lax.all_to_all(own, "row", 0, 1, tiled=True),
            lax.all_gather(log_trans, "row", axis=0, tiled=True),
        )
    packed = call(
        functools.partial(pack_kernel, swapped), (place,), operands,
        [((total_rows + total_rows // PACK, LANES), BF16)] * 2,
    )
    received = [
        lax.ppermute(value, "col", pairs_at(col_count, 1, odd)) for odd, value in enumerate(packed)
    ]
    parts = layout(wells)[1]
    placed = ((total_rows, parts * LANES), F32)
    prepared = call(
        functools.partial(own_kernel, swapped, wells, total_cols),
        (place, corr_len, taper_width, well_cells), operands,
        [placed, placed, ((8, LANES), BF16), ((total_rows, LANES), F32), ((LANES, LANES), BF16)],
        [pltpu.VMEM((total_rows, (wells + 3) * LANES), BF16)],
    )
    seg = total_rows // 8
    chunks = min(CHUNKS, wells)
    piece = (wells // chunks,) + tile[1:]
    *adjoints, moments = call(
        functools.partial(sweep_kernel, wells, tile_rows if swapped else total_rows, total_cols),
        (place,), (*prepared, *received),
        [(piece, BF16)] * chunks + [((8, wells * total_rows // 2 + LANES), F32)],
        [
            pltpu.VMEM(((seg + 1) * parts * 8, LANES), F32),
            pltpu.VMEM(((seg + 1) * parts * 8, LANES), F32),
            pltpu.VMEM(((seg + 1) * parts * 8, LANES), F32),
            pltpu.VMEM((seg * parts * 32, LANES), F32),
        ],
    )

    def finish(distance, moments, *adjoints):
        borders = [pairs_at(col_count, distance, odd) for odd in range(2)]
        borders = [pairs for pairs in borders if pairs]
        tiles = [[lax.ppermute(part, "col", pairs) for pairs in borders] for part in adjoints]
        mats, row_mix, spread = call(
            factor_kernel, (place, corr_len, taper_width), (),
            [((3, LANES, LANES), BF16), ((total_rows, total_rows), BF16), ((16, LANES), BF16)],
        )
        gathered, offsets = moments[None], [0]
        step = col_count // 2
        while step:
            moved = lax.ppermute(gathered, "col", [(i, i ^ step) for i in range(col_count)])
            gathered = jnp.concatenate([gathered, moved], axis=0)
            offsets = offsets + [offset ^ step for offset in offsets]
            step //= 2
        samples = [gathered[i, :wells, -LANES:] for i in range(col_count)]
        while len(samples) > 1:
            samples = [a + b for a, b in zip(samples[::2], samples[1::2])]
        samples = samples[0][:, : 2 * well_count]
        bases = call(
            functools.partial(moment_kernel, tuple(offsets)), (place, corr_len, taper_width),
            (gathered, mats, spread, *adjoints), [(piece, F32)] * chunks,
        )
        low, front = row == 0, lax.axis_index("sect") == 0
        if swapped:
            theirs = exchanged(samples, "row")
            samples = jnp.concatenate(
                [jnp.where(low, samples, theirs), jnp.where(low, theirs, samples)], axis=0
            )
        else:
            samples = lax.all_gather(samples, "row", axis=0, tiled=True)
        theirs = exchanged(samples, "sect")
        samples = jnp.concatenate(
            [jnp.where(front, samples, theirs), jnp.where(front, theirs, samples)], axis=0
        ).T
        half = (piece[0], tile_rows, tile_cols)
        kept, others = [], []
        for base, received in zip(bases, tiles):
            fields = call(
                functools.partial(mix_kernel, swapped, len(borders)), (place,),
                (base, mats, row_mix, *received),
                [(half, BF16)] * 2 if swapped else [(piece, BF16)],
            )
            kept.append(fields[0])
            if swapped:
                others.append(exchanged(fields[1], "row"))
        if swapped:
            qh_fields = jnp.concatenate(
                [jnp.where(low, a, b) for a, b in zip(kept, others)]
                + [jnp.where(low, b, a) for a, b in zip(kept, others)], axis=0
            )
        else:
            qh_fields = lax.all_to_all(jnp.concatenate(kept), "row", 1, 0, tiled=True)
        return qh_fields[None], samples

    branches = [functools.partial(finish, distance) for distance in range(1, TAPER + 1)]
    return lax.switch(taper_width[1] - 1, branches, moments, *adjoints)


def solution(mesh):
    placed = (P("row", "col"), P(), P(), P(), P("sect", None, "row", "col"))
    return jax.shard_map(
        local,
        mesh=mesh,
        in_specs=placed,
        out_specs=(P("sect", None, "row", "col"), P()),
        check_vma=False,
    )
```

time: 822 us -> 60 us (0.07)
  starting transfers between devices: 332 us -> 19 us
  waiting for transfers between devices: 203 us -> 16.9 us
  local copies, waits for them, and re-layouts: 181 us -> 3.71 us
  blocking collectives: 45.8 us -> 0 us
  other arithmetic: 44.6 us -> 0.89 us
  Pallas kernels: 0 us -> 17.8 us
    ppermute x108 -> x12, starting transfers between devices: 332 us -> 19 us  [the longest x3 9.19 us: finish(): lax.ppermute(gathered, 'col', [(i, i ^ step) for i in range(col_count)])]
    ppermute x108 -> x12, waiting for transfers between devices: 203 us -> 16.9 us  [the longest x5 8.84 us: exchanged(): return lax.ppermute(value, axis, [(0, 1), (1, 0)])]
    slice x174 -> x1, local copies, waits for them, and re-layouts: 148 us -> 0.58 us  [local(): return lax.switch(taper_width[1] - 1, branches, moments, *adjoints)]
    select_n x25 -> x3, other arithmetic: 38.2 us -> 0.03 us  [the longest x1 0.02 us: finish(): jnp.where(low, a, b)]
    psum x1 -> x0, blocking collectives: 36.6 us -> none  [local(): joined = lax.psum(sampled, ('row', 'col'))]
    while x96 -> x0, local copies, waits for them, and re-layouts: 28.1 us -> none
    pallas_call x0 -> x7, Pallas kernels: none -> 17.8 us  [call(): pl.pallas_call(kernel, in_specs=[SMEM] * len(smem) + [whole] * len(vmem),...]
    all_gather x2 -> x0, blocking collectives: 9.29 us -> none  [the longest x1 7.5 us: local(): segment = lax.all_gather(mixed, 'row', axis=1, tiled=True)]
  transfers between devices with their start and end apart: 108 -> 12, of which waited for: 53 -> 7; matrix products, arithmetic and copies ran while one was open for 18% -> 2% of each run, Pallas kernels for 0% -> 7%
where the time goes in v3:
time: 60 us; the launch traced here: 59.7 us
  starting transfers between devices  19 us (32%)
  Pallas kernels  17.8 us (30%)
  waiting for transfers between devices  16.9 us (28%)
  local copies, waits for them, and re-layouts  3.71 us (6%)
  between operations  1.37 us (2%)
  other arithmetic  0.89 us (1%)
    pallas_call x7, Pallas kernels, call(): pl.pallas_call(kernel, in_specs=[SMEM] * len(smem) + [whole] * len(vmem),...  17.8 us
    ppermute x3, starting transfers between devices, finish(): lax.ppermute(gathered, 'col', [(i, i ^ step) for i in range(col_count)])  9.19 us
    ppermute x5, waiting for transfers between devices, exchanged(): return lax.ppermute(value, axis, [(0, 1), (1, 0)])  8.84 us
    ppermute x3, waiting for transfers between devices, finish(): lax.ppermute(gathered, 'col', [(i, i ^ step) for i in range(col_count)])  7.06 us
    ppermute x5, starting transfers between devices, exchanged(): return lax.ppermute(value, axis, [(0, 1), (1, 0)])  6.28 us
    unnamed x10, local copies, waits for them, and re-layouts  2.46 us
    ppermute x2, starting transfers between devices, local(): lax.ppermute(value, 'col', pairs_at(col_count, 1, odd))  2.43 us
  transfers between devices with their start and end apart: 12, of which 7 were waited for; matrix products, arithmetic and copies ran while one was open for 2% of the time, Pallas kernels for 7%

profile of v3, /device:TPU:0, one launch (start us, length us, event | category | flops | bytes accessed | tf_op | source)
XLA Modules:
  0.0 59.7 jit_solution(17777692072917194734)
XLA Ops:
  0.6 0.1 pad_add_fusion.place_ref
  0.7 0.0 copy-start
  0.7 0.9 %copy-done = bf16[1,8,128,128]{3,2,1,0:T(8,128)(2,1)S(1)} copy-done((bf16[1,8,128,128]{3,2,1,0:T(8,128)(2,1)S(1)}, bf16[1,8,128,128]{3,2,1,0:T(8,128)(2,1)}, u32[]{:S(2)}) %copy-start) | copy-done | bytes 262168
  1.7 0.0 copy-start.1
  1.7 0.8 %copy-done.1 = f32[128,128]{1,0:T(8,128)S(1)} copy-done((f32[128,128]{1,0:T(8,128)S(1)}, f32[128,128]{1,0:T(8,128)}, u32[]{:S(2)}) %copy-start.1) | copy-done | bytes 65560
  2.5 1.0 %shard_map.76 = (bf16[4,128,128]{2,1,0:T(8,128)(2,1)S(1)}, bf16[4,128,128]{2,1,0:T(8,128)(2,1)S(1)}, bf16[3,128,128]{2,1,0:T(8,128)(2,1)S(1)}) custom-call(s32[2]{0:T(128)S(1)} %pad_add_fusion.place_ref, bf16[8,128,128]{2,1,0:T(8,128)(2,1)S(1)} %bitcast.36, f32[128,128]{1,0:T(8,128)S(1)} %copy-done.1), custom_call_target="tpu_custom_call" | custom-call | flops 1 | bytes 1048576 | tf_op jit(solution)/shard_map/pallas_call | solution.py:433
  3.5 3.0 %collective-permute-start.31 = (bf16[4,128,128]{2,1,0:T(8,128)(2,1)S(1)}, bf16[4,128,128]{2,1,0:T(8,128)(2,1)S(1)}, u32[]{:S(2)}, u32[]{:S(2)}) collective-permute-start(bf16[4,128,128]{2,1,0:T(8,128)(2,1)S(1)} %get-tuple-element.108), channel_id=1, source_target_pairs={{0,8},{8,0},{1,9},{9,1},{2,10},{10,2},{3,11},{11,3},{4,12},{12,4},... | collective-permute-start | bytes 393224 | tf_op jit(solution)/shard_map/ppermute | solution.py:453
  6.6 0.1 collective-permute-start.32
  6.6 4.8 %collective-permute-done.32.refs_3_ = f32[128,128]{1,0:T(8,128)S(1)} collective-permute-done((f32[128,128]{1,0:T(8,128)S(1)}, f32[128,128]{1,0:T(8,128)S(1)}, u32[]{:S(2)}, u32[]{:S(2)}) %collective-permute-start.32) | collective-permute-done | bytes 65568 | tf_op jit(solution)/shard_map/ppermute | solution.py:453
  11.5 0.0 collective-permute-done.31.refs_2_
  11.5 0.9 %shard_map.78 = (bf16[320,128]{1,0:T(8,128)(2,1)S(1)}, bf16[320,128]{1,0:T(8,128)(2,1)S(1)}) custom-call(s32[2]{0:T(128)S(1)} %pad_add_fusion.place_ref, bf16[4,128,128]{2,1,0:T(8,128)(2,1)S(1)} %get-tuple-element.106.refs_0_, bf16[3,128,128]{2,1,0:T(8,128)(2,1)S(1)} %get-tuple-element.107.refs_1_, bf16[4,128,128]{2,1,0:T(8,128)(2,1)S(1)} %collective-permute-done.31.refs_2_, ...), custom_call_target="tpu_custom_call" | custom-call | flops 1 | bytes 1048576 | tf_op jit(solution)/shard_map/pallas_call | solution.py:433
  12.3 0.0 copy-start.3
  12.3 1.8 %collective-permute-start.33 = (bf16[320,128]{1,0:T(8,128)(2,1)S(1)}, bf16[320,128]{1,0:T(8,128)(2,1)S(1)}, u32[]{:S(2)}, u32[]{:S(2)}) collective-permute-start(bf16[320,128]{1,0:T(8,128)(2,1)S(1)} %get-tuple-element.114), channel_id=1, source_target_pairs={{0,1},{1,0},{2,3},{3,2},{4,5},{5,4},{6,7},{7,6},{8,9},{9,8},{10,11... | collective-permute-start | bytes 245768 | tf_op jit(solution)/shard_map/ppermute | solution.py:487
  14.1 0.7 %collective-permute-start.34 = (bf16[320,128]{1,0:T(8,128)(2,1)S(1)}, bf16[320,128]{1,0:T(8,128)(2,1)S(1)}, u32[]{:S(2)}, u32[]{:S(2)}) collective-permute-start(bf16[320,128]{1,0:T(8,128)(2,1)S(1)} %get-tuple-element.115), channel_id=1, source_target_pairs={{1,2},{2,1},{3,4},{4,3},{5,6},{6,5},{9,10},{10,9},{11,12},{12,11},... | collective-permute-start | bytes 245768 | tf_op jit(solution)/shard_map/ppermute | solution.py:487
  14.8 0.0 copy-done.3
  14.8 0.6 slice.111
  16.0 0.0 copy-start.2
  16.0 0.0 copy-start.4
  16.0 0.7 %copy-done.2 = s32[2,8]{1,0:T(2,128)S(1)} copy-done((s32[2,8]{1,0:T(2,128)S(1)}, s32[2,8]{1,0:T(2,128)}, u32[]{:S(2)}) %copy-start.2) | copy-done | bytes 88
  16.7 0.0 copy-done.4
  16.7 1.6 %shard_map.77 = (f32[256,768]{1,0:T(8,128)S(1)}, f32[256,768]{1,0:T(8,128)S(1)}, bf16[8,128]{1,0:T(8,128)(2,1)S(1)}, f32[256,128]{1,0:T(8,128)S(1)}, bf16[128,128]{1,0:T(8,128)(2,1)S(1)}) custom-call(s32[2]{0:T(128)S(1)} %pad_add_fusion.place_ref, f32[2]{0:T(128)S(1)} %copy-done.4, s32[2]{0:T(128)S(1)} %copy-done.3, s32[2,8]{1,0:T(2,128)S(1)} %copy-done.2, ...), custom_call_target="tpu_custom_call" | custom-call | flops 1 | bytes 1048576 | tf_op jit(solution)/shard_map/pallas_call | solution.py:433
  18.3 0.0 collective-permute-done.33.a_ref
  18.3 0.0 collective-permute-done.34.b_ref
  18.3 11.5 %shard_map.79 = (bf16[4,256,128]{2,1,0:T(8,128)(2,1)S(1)}, f32[8,640]{1,0:T(8,128)S(1)}) custom-call(s32[2]{0:T(128)S(1)} %pad_add_fusion.place_ref, f32[256,768]{1,0:T(8,128)S(1)} %get-tuple-element.109.field_ref, f32[256,768]{1,0:T(8,128)S(1)} %get-tuple-element.110.log_ref, bf16[8,128]{1,0:T(8,128)(2,1)S(1)} %get-tuple-element.111.basis_ref, ...), custom_call_target="tpu_custom_call" | custom-call | flops 1 | bytes 1048576 | tf_op jit(solution)/shard_map/pallas_call | solution.py:433
  29.8 29.9 %conditional.1 = (bf16[1,8,128,128]{3,2,1,0:T(8,128)(2,1)}, f32[16,16]{1,0:T(8,128)}) conditional(s32[]{:T(128)} %bitcast.16, (s32[]{:T(128)}, f32[8,640]{1,0:T(8,128)S(1)}, s32[2]{0:T(128)S(1)}, f32[2]{0:T(128)S(1)}, s32[2]{0:T(128)S(1)}, /*index=5*/bf16[4,256,128]{2,1,0:T(8,128)(2,1)S(1)}) %tuple.57, (s32[]{:T(128)}, ...), branch_computations={%region_0.1_spmd, %region_1.2_spmd, %region_2.3_spmd, %region_3.4_... | conditional | flops 440712 | bytes 7992709 | solution.py:568
  29.8 5.7 %collective-permute-start = (f32[1,8,640]{2,1,0:T(8,128)S(1)}, f32[1,8,640]{2,1,0:T(8,128)S(1)}, u32[]{:S(2)}, u32[]{:S(2)}) collective-permute-start(f32[1,8,640]{2,1,0:T(8,128)S(1)} %bitcast.37), channel_id=1, source_target_pairs={{0,4},{1,5},{2,6},{3,7},{4,0},{5,1},{6,2},{7,3},{8,12},{9,13},{10,... | collective-permute-start | bytes 61448 | tf_op jit(solution)/shard_map/cond/branch_0_fun/ppermute | solution.py:523
  35.5 1.8 %collective-permute-done = f32[1,8,640]{2,1,0:T(8,128)S(1)} collective-permute-done((f32[1,8,640]{2,1,0:T(8,128)S(1)}, f32[1,8,640]{2,1,0:T(8,128)S(1)}, u32[]{:S(2)}, u32[]{:S(2)}) %collective-permute-start) | collective-permute-done | bytes 20512 | tf_op jit(solution)/shard_map/cond/branch_0_fun/ppermute | solution.py:523
  37.3 1.9 %collective-permute-start.1 = (f32[2,8,640]{2,1,0:T(8,128)S(1)}, f32[2,8,640]{2,1,0:T(8,128)S(1)}, u32[]{:S(2)}, u32[]{:S(2)}) collective-permute-start(f32[2,8,640]{2,1,0:T(8,128)S(1)} %pad_maximum_fusion.2), channel_id=1, source_target_pairs={{0,2},{1,3},{2,0},{3,1},{4,6},{5,7},{6,4},{7,5},{8,10},{9,11},{10,... | collective-permute-start | bytes 122888 | tf_op jit(solution)/shard_map/cond/branch_0_fun/ppermute | solution.py:523
  39.2 2.1 %collective-permute-done.1 = f32[2,8,640]{2,1,0:T(8,128)S(1)} collective-permute-done((f32[2,8,640]{2,1,0:T(8,128)S(1)}, f32[2,8,640]{2,1,0:T(8,128)S(1)}, u32[]{:S(2)}, u32[]{:S(2)}) %collective-permute-start.1) | collective-permute-done | bytes 40992 | tf_op jit(solution)/shard_map/cond/branch_0_fun/ppermute | solution.py:523
  41.3 1.6 %collective-permute-start.2 = (f32[4,8,640]{2,1,0:T(8,128)S(1)}, f32[4,8,640]{2,1,0:T(8,128)S(1)}, u32[]{:S(2)}, u32[]{:S(2)}) collective-permute-start(f32[4,8,640]{2,1,0:T(8,128)S(1)} %pad_maximum_fusion.1), channel_id=1, source_target_pairs={{0,1},{1,0},{2,3},{3,2},{4,5},{5,4},{6,7},{7,6},{8,9},{9,8},{10,11... | collective-permute-start | bytes 245768 | tf_op jit(solution)/shard_map/cond/branch_0_fun/ppermute | solution.py:523
  42.9 0.4 collective-permute-start.3
  43.3 0.7 %collective-permute-start.4 = (bf16[4,256,128]{2,1,0:T(8,128)(2,1)S(1)}, bf16[4,256,128]{2,1,0:T(8,128)(2,1)S(1)}, u32[]{:S(2)}, u32[]{:S(2)}) collective-permute-start(bf16[4,256,128]{2,1,0:T(8,128)(2,1)S(1)} %get-tuple-element.55.refs_0_), channel_id=1, source_target_pairs={{1,2},{2,1},{3,4},{4,3},{5,6},{6,5},{9,10},{10,9},{11,12},{12,11},... | collective-permute-start | bytes 786440 | tf_op jit(solution)/shard_map/cond/branch_0_fun/ppermute | solution.py:515
  44.0 3.2 %collective-permute-done.2 = f32[4,8,640]{2,1,0:T(8,128)S(1)} collective-permute-done((f32[4,8,640]{2,1,0:T(8,128)S(1)}, f32[4,8,640]{2,1,0:T(8,128)S(1)}, u32[]{:S(2)}, u32[]{:S(2)}) %collective-permute-start.2) | collective-permute-done | bytes 81952 | tf_op jit(solution)/shard_map/cond/branch_0_fun/ppermute | solution.py:523
  47.2 1.5 %collective-permute-start.6 = (f32[4,16]{1,0:T(4,128)S(1)}, f32[4,16]{1,0:T(4,128)S(1)}, u32[]{:S(2)}, u32[]{:S(2)}) collective-permute-start(f32[4,16]{1,0:T(4,128)S(1)} %bitcast.57), channel_id=1, source_target_pairs={{0,8},{8,0},{1,9},{9,1},{2,10},{10,2},{3,11},{11,3},{4,12},{12,4},... | collective-permute-start | bytes 776 | tf_op jit(solution)/shard_map/cond/branch_0_fun/ppermute | solution.py:453
  48.7 0.8 %branch_0_fun.3 = (bf16[3,128,128]{2,1,0:T(8,128)(2,1)S(1)}, bf16[256,256]{1,0:T(8,128)(2,1)S(1)}, bf16[16,128]{1,0:T(8,128)(2,1)S(1)}) custom-call(s32[2]{0:T(128)S(1)} %get-tuple-element.49.place_ref, f32[2]{0:T(128)S(1)} %get-tuple-element.50.corr_ref, s32[2]{0:T(128)S(1)} %get-tuple-element.51.taper_ref), custom_call_target="tpu_custom_call" | custom-call | flops 1 | bytes 1048576 | tf_op jit(solution)/shard_map/cond/branch_0_fun/pallas_call | solution.py:433
  49.5 1.3 %collective-permute-done.6 = f32[4,16]{1,0:T(4,128)S(1)} collective-permute-done((f32[4,16]{1,0:T(4,128)S(1)}, f32[4,16]{1,0:T(4,128)S(1)}, u32[]{:S(2)}, u32[]{:S(2)}) %collective-permute-start.6) | collective-permute-done | bytes 288 | tf_op jit(solution)/shard_map/cond/branch_0_fun/ppermute | solution.py:453
  50.8 0.1 collective-permute-start.7
  50.9 0.9 %branch_0_fun.4.base_ref = f32[4,256,128]{2,1,0:T(8,128)S(1)} custom-call(s32[2]{0:T(128)S(1)} %get-tuple-element.49.place_ref, f32[2]{0:T(128)S(1)} %get-tuple-element.50.corr_ref, s32[2]{0:T(128)S(1)} %get-tuple-element.51.taper_ref, f32[8,8,640]{2,1,0:T(8,128)S(1)} %pad_maximum_fusion.mom_ref, bf16[3,128,128]{2,1,0:T(8,128)(2,1)S(1)} %get-tuple-element.53.mats_ref, ...), custom_call_target="tpu_custom_call" | custom-call | flops 1 | bytes 1048576 | tf_op jit(solution)/shard_map/cond/branch_0_fun/pallas_call | solution.py:433
  51.8 1.0 %collective-permute-done.3.refs_0_ = bf16[4,256,128]{2,1,0:T(8,128)(2,1)S(1)} collective-permute-done((bf16[4,256,128]{2,1,0:T(8,128)(2,1)S(1)}, bf16[4,256,128]{2,1,0:T(8,128)(2,1)S(1)}, u32[]{:S(2)}, u32[]{:S(2)}) %collective-permute-start.3) | collective-permute-done | bytes 262176 | tf_op jit(solution)/shard_map/cond/branch_0_fun/ppermute | solution.py:515
  52.8 0.0 collective-permute-done.4.refs_1_
  52.8 1.1 %branch_0_fun.5 = (bf16[4,128,128]{2,1,0:T(8,128)(2,1)S(1)}, bf16[4,128,128]{2,1,0:T(8,128)(2,1)S(1)}) custom-call(s32[2]{0:T(128)S(1)} %get-tuple-element.49.place_ref, f32[4,256,128]{2,1,0:T(8,128)S(1)} %branch_0_fun.4.base_ref, bf16[3,128,128]{2,1,0:T(8,128)(2,1)S(1)} %get-tuple-element.53.mats_ref, bf16[256,256]{1,0:T(8,128)(2,1)S(1)} %get-tuple-element.56.row_ref, ...), custom_call_target="tpu_custom_call" | custom-call | flops 1 | bytes 1048576 | tf_op jit(solution)/shard_map/cond/branch_0_fun/pallas_call | solution.py:433
  53.9 1.6 %collective-permute-start.5 = (bf16[4,128,128]{2,1,0:T(8,128)(2,1)S(1)}, bf16[4,128,128]{2,1,0:T(8,128)(2,1)S(1)}, u32[]{:S(2)}, u32[]{:S(2)}) collective-permute-start(bf16[4,128,128]{2,1,0:T(8,128)(2,1)S(1)} %get-tuple-element.58), channel_id=1, source_target_pairs={{0,8},{8,0},{1,9},{9,1},{2,10},{10,2},{3,11},{11,3},{4,12},{12,4},... | collective-permute-start | bytes 393224 | tf_op jit(solution)/shard_map/cond/branch_0_fun/ppermute | solution.py:453
  55.5 0.0 collective-permute-done.7
  55.5 0.7 %copy.16 = f32[16,16]{1,0:T(8,128)} copy(f32[16,16]{0,1:T(8,128)S(1)} %maximum_bitcast_fusion.1) | data formatting | bytes 2048 | tf_op jit(solution)/shard_map/cond | solution.py:568
  56.2 2.8 %collective-permute-done.5 = bf16[4,128,128]{2,1,0:T(8,128)(2,1)S(1)} collective-permute-done((bf16[4,128,128]{2,1,0:T(8,128)(2,1)S(1)}, bf16[4,128,128]{2,1,0:T(8,128)(2,1)S(1)}, u32[]{:S(2)}, u32[]{:S(2)}) %collective-permute-start.5) | collective-permute-done | bytes 131104 | tf_op jit(solution)/shard_map/cond/branch_0_fun/ppermute | solution.py:453
  59.0 0.7 %maximum_bitcast_fusion = bf16[1,8,128,128]{3,2,1,0:T(8,128)(2,1)} fusion(bf16[4,128,128]{2,1,0:T(8,128)(2,1)S(1)} %get-tuple-element.124, bf16[4,128,128]{2,1,0:T(8,128)(2,1)S(1)} %get-tuple-element.123), kind=kLoop, calls=%fused_computation | loop fusion | flops 131072 | bytes 524288 | tf_op jit(solution)/shard_map/cond/branch_0_fun/broadcast_in_dim | solution.py:565
  (9 shorter events, 0.1 us)
Async XLA Ops:
  0.7 1.0 %copy-start = (bf16[1,8,128,128]{3,2,1,0:T(8,128)(2,1)S(1)}, bf16[1,8,128,128]{3,2,1,0:T(8,128)(2,1)}, u32[]{:S(2)}) copy-start(bf16[1,8,128,128]{3,2,1,0:T(8,128)(2,1)} %param.13) | copy-start | bytes 786436
  1.7 0.8 %copy-start.1 = (f32[128,128]{1,0:T(8,128)S(1)}, f32[128,128]{1,0:T(8,128)}, u32[]{:S(2)}) copy-start(f32[128,128]{1,0:T(8,128)} %lt_ref.1) | copy-start | bytes 196612
  3.5 7.9 %collective-permute-start.31 = (bf16[4,128,128]{2,1,0:T(8,128)(2,1)S(1)}, bf16[4,128,128]{2,1,0:T(8,128)(2,1)S(1)}, u32[]{:S(2)}, u32[]{:S(2)}) collective-permute-start(bf16[4,128,128]{2,1,0:T(8,128)(2,1)S(1)} %get-tuple-element.108), channel_id=1, source_target_pairs={{0,8},{8,0},{1,9},{9,1},{2,10},{10,2},{3,11},{11,3},{4,12},{12,4},... | collective-permute-start | bytes 393224 | tf_op jit(solution)/shard_map/ppermute | solution.py:453
  6.6 4.9 %collective-permute-start.32 = (f32[128,128]{1,0:T(8,128)S(1)}, f32[128,128]{1,0:T(8,128)S(1)}, u32[]{:S(2)}, u32[]{:S(2)}) collective-permute-start(f32[128,128]{1,0:T(8,128)S(1)} %copy-done.1), channel_id=1, source_target_pairs={{0,8},{8,0},{1,9},{9,1},{2,10},{10,2},{3,11},{11,3},{4,12},{12,4},... | collective-permute-start | bytes 196616 | tf_op jit(solution)/shard_map/ppermute | solution.py:453
  12.3 2.5 %copy-start.3 = (s32[2]{0:T(128)S(1)}, s32[2]{0:T(128)}, u32[]{:S(2)}) copy-start(s32[2]{0:T(128)} %taper_ref.1) | copy-start | bytes 28
  12.3 6.0 %collective-permute-start.33 = (bf16[320,128]{1,0:T(8,128)(2,1)S(1)}, bf16[320,128]{1,0:T(8,128)(2,1)S(1)}, u32[]{:S(2)}, u32[]{:S(2)}) collective-permute-start(bf16[320,128]{1,0:T(8,128)(2,1)S(1)} %get-tuple-element.114), channel_id=1, source_target_pairs={{0,1},{1,0},{2,3},{3,2},{4,5},{5,4},{6,7},{7,6},{8,9},{9,8},{10,11... | collective-permute-start | bytes 245768 | tf_op jit(solution)/shard_map/ppermute | solution.py:487
  14.1 4.2 %collective-permute-start.34 = (bf16[320,128]{1,0:T(8,128)(2,1)S(1)}, bf16[320,128]{1,0:T(8,128)(2,1)S(1)}, u32[]{:S(2)}, u32[]{:S(2)}) collective-permute-start(bf16[320,128]{1,0:T(8,128)(2,1)S(1)} %get-tuple-element.115), channel_id=1, source_target_pairs={{1,2},{2,1},{3,4},{4,3},{5,6},{6,5},{9,10},{10,9},{11,12},{12,11},... | collective-permute-start | bytes 245768 | tf_op jit(solution)/shard_map/ppermute | solution.py:487
  16.0 0.7 %copy-start.2 = (s32[2,8]{1,0:T(2,128)S(1)}, s32[2,8]{1,0:T(2,128)}, u32[]{:S(2)}) copy-start(s32[2,8]{1,0:T(2,128)} %cells_ref.1) | copy-start | bytes 196
  16.0 0.7 %copy-start.4 = (f32[2]{0:T(128)S(1)}, f32[2]{0:T(128)}, u32[]{:S(2)}) copy-start(f32[2]{0:T(128)} %corr_ref.1) | copy-start | bytes 28
  29.8 7.4 %collective-permute-start = (f32[1,8,640]{2,1,0:T(8,128)S(1)}, f32[1,8,640]{2,1,0:T(8,128)S(1)}, u32[]{:S(2)}, u32[]{:S(2)}) collective-permute-start(f32[1,8,640]{2,1,0:T(8,128)S(1)} %bitcast.37), channel_id=1, source_target_pairs={{0,4},{1,5},{2,6},{3,7},{4,0},{5,1},{6,2},{7,3},{8,12},{9,13},{10,... | collective-permute-start | bytes 61448 | tf_op jit(solution)/shard_map/cond/branch_0_fun/ppermute | solution.py:523
  37.3 4.0 %collective-permute-start.1 = (f32[2,8,640]{2,1,0:T(8,128)S(1)}, f32[2,8,640]{2,1,0:T(8,128)S(1)}, u32[]{:S(2)}, u32[]{:S(2)}) collective-permute-start(f32[2,8,640]{2,1,0:T(8,128)S(1)} %pad_maximum_fusion.2), channel_id=1, source_target_pairs={{0,2},{1,3},{2,0},{3,1},{4,6},{5,7},{6,4},{7,5},{8,10},{9,11},{10,... | collective-permute-start | bytes 122888 | tf_op jit(solution)/shard_map/cond/branch_0_fun/ppermute | solution.py:523
  41.3 5.9 %collective-permute-start.2 = (f32[4,8,640]{2,1,0:T(8,128)S(1)}, f32[4,8,640]{2,1,0:T(8,128)S(1)}, u32[]{:S(2)}, u32[]{:S(2)}) collective-permute-start(f32[4,8,640]{2,1,0:T(8,128)S(1)} %pad_maximum_fusion.1), channel_id=1, source_target_pairs={{0,1},{1,0},{2,3},{3,2},{4,5},{5,4},{6,7},{7,6},{8,9},{9,8},{10,11... | collective-permute-start | bytes 245768 | tf_op jit(solution)/shard_map/cond/branch_0_fun/ppermute | solution.py:523
  42.9 9.9 %collective-permute-start.3 = (bf16[4,256,128]{2,1,0:T(8,128)(2,1)S(1)}, bf16[4,256,128]{2,1,0:T(8,128)(2,1)S(1)}, u32[]{:S(2)}, u32[]{:S(2)}) collective-permute-start(bf16[4,256,128]{2,1,0:T(8,128)(2,1)S(1)} %get-tuple-element.55.refs_0_), channel_id=1, source_target_pairs={{0,1},{1,0},{2,3},{3,2},{4,5},{5,4},{6,7},{7,6},{8,9},{9,8},{10,11... | collective-permute-start | bytes 786440 | tf_op jit(solution)/shard_map/cond/branch_0_fun/ppermute | solution.py:515
  43.3 9.5 %collective-permute-start.4 = (bf16[4,256,128]{2,1,0:T(8,128)(2,1)S(1)}, bf16[4,256,128]{2,1,0:T(8,128)(2,1)S(1)}, u32[]{:S(2)}, u32[]{:S(2)}) collective-permute-start(bf16[4,256,128]{2,1,0:T(8,128)(2,1)S(1)} %get-tuple-element.55.refs_0_), channel_id=1, source_target_pairs={{1,2},{2,1},{3,4},{4,3},{5,6},{6,5},{9,10},{10,9},{11,12},{12,11},... | collective-permute-start | bytes 786440 | tf_op jit(solution)/shard_map/cond/branch_0_fun/ppermute | solution.py:515
  47.2 3.6 %collective-permute-start.6 = (f32[4,16]{1,0:T(4,128)S(1)}, f32[4,16]{1,0:T(4,128)S(1)}, u32[]{:S(2)}, u32[]{:S(2)}) collective-permute-start(f32[4,16]{1,0:T(4,128)S(1)} %bitcast.57), channel_id=1, source_target_pairs={{0,8},{8,0},{1,9},{9,1},{2,10},{10,2},{3,11},{11,3},{4,12},{12,4},... | collective-permute-start | bytes 776 | tf_op jit(solution)/shard_map/cond/branch_0_fun/ppermute | solution.py:453
  50.8 4.7 %collective-permute-start.7 = (f32[8,16]{1,0:T(8,128)S(1)}, f32[8,16]{1,0:T(8,128)S(1)}, u32[]{:S(2)}, u32[]{:S(2)}) collective-permute-start(f32[8,16]{1,0:T(8,128)S(1)} %pad_maximum_fusion.3), channel_id=1, source_target_pairs={{0,16},{16,0},{1,17},{17,1},{2,18},{18,2},{3,19},{19,3},{4,20},{20... | collective-permute-start | bytes 1544 | tf_op jit(solution)/shard_map/cond/branch_0_fun/ppermute | solution.py:453
  53.9 5.0 %collective-permute-start.5 = (bf16[4,128,128]{2,1,0:T(8,128)(2,1)S(1)}, bf16[4,128,128]{2,1,0:T(8,128)(2,1)S(1)}, u32[]{:S(2)}, u32[]{:S(2)}) collective-permute-start(bf16[4,128,128]{2,1,0:T(8,128)(2,1)S(1)} %get-tuple-element.58), channel_id=1, source_target_pairs={{0,8},{8,0},{1,9},{9,1},{2,10},{10,2},{3,11},{11,3},{4,12},{12,4},... | collective-permute-start | bytes 393224 | tf_op jit(solution)/shard_map/cond/branch_0_fun/ppermute | solution.py:453

commit v4 on v3

--- a/solution.py
+++ b/solution.py
@@ -15,7 +15,7 @@
 STRIP = 32
 PACK = LANES // STRIP
 CHUNKS = 1
-UNROLL = 16
+UNROLL = 32
 
 leakage = 0.05
 F32, BF16 = jnp.float32, jnp.bfloat16
@@ -91,21 +91,9 @@
     ]
 
 
-def split_kernel(place_ref, obs_ref, lt_ref, sent_ref, kept_ref, planes_ref, logs_ref, sems):
-    wells = sent_ref.shape[0]
-    mine = place_ref[0] * wells
-    copies = [
-        pltpu.make_async_copy(lt_ref, logs_ref, sems.at[0]),
-        pltpu.make_async_copy(obs_ref.at[pl.ds(wells - mine, wells)], sent_ref, sems.at[1]),
-        pltpu.make_async_copy(obs_ref.at[pl.ds(mine, wells)], kept_ref, sems.at[2]),
-    ]
-    for copy in copies:
-        copy.start()
-    copies[0].wait()
-    for i, piece in enumerate(split3(logs_ref[...])):
+def split_kernel(lt_ref, planes_ref):
+    for i, piece in enumerate(split3(lt_ref[...])):
         planes_ref[i] = piece
-    copies[1].wait()
-    copies[2].wait()
 
 
 def row_parts(swapped, place_ref, refs, rows):
@@ -466,12 +454,11 @@
     tile = (wells, total_rows, tile_cols)
 
     if swapped:
-        half = ((wells, tile_rows, tile_cols), BF16)
-        sent, kept, planes = call(
-            split_kernel, (place,), (own, log_trans),
-            [half, half, ((3, tile_rows, tile_cols), BF16)],
-            [pltpu.VMEM((tile_rows, tile_cols), F32), pltpu.SemaphoreType.DMA((3,))],
-            whole=pl.BlockSpec(memory_space=pl.ANY),
+        sent, kept = [
+            lax.dynamic_slice_in_dim(own, first * wells, wells, axis=0) for first in (1 - row, row)
+        ]
+        (planes,) = call(
+            split_kernel, (), (log_trans,), [((3, tile_rows, tile_cols), BF16)]
         )
         operands = (kept, planes, exchanged(sent, "row"), exchanged(log_trans, "row"))
     else:

time: 60 us -> 56.8 us (0.947)
  Pallas kernels: 17.8 us -> 14.4 us
  starting transfers between devices: 19 us -> 21.1 us
  waiting for transfers between devices: 16.9 us -> 15.8 us
  local copies, waits for them, and re-layouts: 3.71 us -> 2.95 us
    pallas_call x7, Pallas kernels: 17.8 us -> 14.4 us  [call(): pl.pallas_call(kernel, in_specs=[SMEM] * len(smem) + [whole] * len(vmem),...]
    ppermute x3, waiting for transfers between devices: 7.06 us -> 4.18 us  [finish(): lax.ppermute(gathered, 'col', [(i, i ^ step) for i in range(col_count)])]
    ppermute x2 -> x1, waiting for transfers between devices: 0.97 us -> 2.89 us  [finish(): lax.ppermute(part, 'col', pairs)]
    unnamed x10 -> x8, local copies, waits for them, and re-layouts: 2.46 us -> 0.68 us
    ppermute x3, starting transfers between devices: 9.19 us -> 10.3 us  [finish(): lax.ppermute(gathered, 'col', [(i, i ^ step) for i in range(col_count)])]
    ppermute x2 -> x1, starting transfers between devices: 1.07 us -> 2.09 us  [finish(): lax.ppermute(part, 'col', pairs)]
    dynamic_slice x0 -> x1, local copies, waits for them, and re-layouts: none -> 1.02 us  [local(): lax.dynamic_slice_in_dim(own, first * wells, wells, axis=0)]
  transfers between devices with their start and end apart: 12 -> 11, of which waited for: 7 -> 7; matrix products, arithmetic and copies ran while one was open for 2% -> 2% of each run, Pallas kernels for 7% -> 8%
where the time goes in v4:
time: 56.8 us; the launch traced here: 56.6 us
  starting transfers between devices  21.1 us (37%)
  waiting for transfers between devices  15.8 us (28%)
  Pallas kernels  14.4 us (25%)
  local copies, waits for them, and re-layouts  2.95 us (5%)
  between operations  1.39 us (2%)
  other arithmetic  0.89 us (2%)
    pallas_call x7, Pallas kernels, call(): pl.pallas_call(kernel, in_specs=[SMEM] * len(smem) + [whole] * len(vmem),...  14.4 us
    ppermute x3, starting transfers between devices, finish(): lax.ppermute(gathered, 'col', [(i, i ^ step) for i in range(col_count)])  10.3 us
    ppermute x5, waiting for transfers between devices, exchanged(): return lax.ppermute(value, axis, [(0, 1), (1, 0)])  8.73 us
    ppermute x5, starting transfers between devices, exchanged(): return lax.ppermute(value, axis, [(0, 1), (1, 0)])  6.29 us
    ppermute x3, waiting for transfers between devices, finish(): lax.ppermute(gathered, 'col', [(i, i ^ step) for i in range(col_count)])  4.18 us
    ppermute x1, waiting for transfers between devices, finish(): lax.ppermute(part, 'col', pairs)  2.89 us
    ppermute x2, starting transfers between devices, local(): lax.ppermute(value, 'col', pairs_at(col_count, 1, odd))  2.43 us
    ppermute x1, starting transfers between devices, finish(): lax.ppermute(part, 'col', pairs)  2.09 us
  transfers between devices with their start and end apart: 11, of which 7 were waited for; matrix products, arithmetic and copies ran while one was open for 2% of the time, Pallas kernels for 8%

profile of v4, /device:TPU:0, one launch (start us, length us, event | category | flops | bytes accessed | tf_op | source)
XLA Modules:
  0.0 56.6 jit_solution(4285138834233199135)
XLA Ops:
  0.6 0.0 copy-start
  0.6 1.0 %dynamic-slice_bitcast_fusion = (bf16[4,128,128]{2,1,0:T(8,128)(2,1)S(1)}, bf16[4,128,128]{2,1,0:T(8,128)(2,1)S(1)}) fusion(bf16[1,8,128,128]{3,2,1,0:T(8,128)(2,1)} %param.13, s32[]{:T(128)S(6)} %select_n.133, s32[]{:T(128)S(6)} %select_n.132), kind=kLoop, calls=%fused_computation.80 | loop fusion | bytes 524296 | tf_op jit(solution)/shard_map/dynamic_slice | solution.py:458
  1.7 3.0 %collective-permute-start.31 = (bf16[4,128,128]{2,1,0:T(8,128)(2,1)S(1)}, bf16[4,128,128]{2,1,0:T(8,128)(2,1)S(1)}, u32[]{:S(2)}, u32[]{:S(2)}) collective-permute-start(bf16[4,128,128]{2,1,0:T(8,128)(2,1)S(1)} %get-tuple-element.141), channel_id=1, source_target_pairs={{0,8},{8,0},{1,9},{9,1},{2,10},{10,2},{3,11},{11,3},{4,12},{12,4},... | collective-permute-start | bytes 393224 | tf_op jit(solution)/shard_map/ppermute | solution.py:441
  4.7 0.0 copy-done
  4.7 0.1 collective-permute-start.32
  4.8 0.1 pad_add_fusion.place_ref
  4.9 4.7 %collective-permute-done.32.refs_3_ = f32[128,128]{1,0:T(8,128)S(1)} collective-permute-done((f32[128,128]{1,0:T(8,128)S(1)}, f32[128,128]{1,0:T(8,128)S(1)}, u32[]{:S(2)}, u32[]{:S(2)}) %collective-permute-start.32) | collective-permute-done | bytes 65568 | tf_op jit(solution)/shard_map/ppermute | solution.py:441
  9.6 0.0 collective-permute-done.31.refs_2_
  9.6 0.9 %shard_map.78 = (bf16[320,128]{1,0:T(8,128)(2,1)S(1)}, bf16[320,128]{1,0:T(8,128)(2,1)S(1)}) custom-call(s32[2]{0:T(128)S(1)} %pad_add_fusion.place_ref, bf16[4,128,128]{2,1,0:T(8,128)(2,1)S(1)} %get-tuple-element.142.refs_0_, bf16[3,128,128]{2,1,0:T(8,128)(2,1)S(1)} %shard_map.76.refs_1_, bf16[4,128,128]{2,1,0:T(8,128)(2,1)S(1)} %collective-permute-done.31.refs_2_, ...), custom_call_target="tpu_custom_call" | custom-call | flops 1 | bytes 1048576 | tf_op jit(solution)/shard_map/pallas_call | solution.py:421
  10.5 0.0 copy-start.2
  10.5 1.8 %collective-permute-start.33 = (bf16[320,128]{1,0:T(8,128)(2,1)S(1)}, bf16[320,128]{1,0:T(8,128)(2,1)S(1)}, u32[]{:S(2)}, u32[]{:S(2)}) collective-permute-start(bf16[320,128]{1,0:T(8,128)(2,1)S(1)} %get-tuple-element.108), channel_id=1, source_target_pairs={{0,1},{1,0},{2,3},{3,2},{4,5},{5,4},{6,7},{7,6},{8,9},{9,8},{10,11... | collective-permute-start | bytes 245768 | tf_op jit(solution)/shard_map/ppermute | solution.py:474
  12.3 0.7 %collective-permute-start.34 = (bf16[320,128]{1,0:T(8,128)(2,1)S(1)}, bf16[320,128]{1,0:T(8,128)(2,1)S(1)}, u32[]{:S(2)}, u32[]{:S(2)}) collective-permute-start(bf16[320,128]{1,0:T(8,128)(2,1)S(1)} %get-tuple-element.109), channel_id=1, source_target_pairs={{1,2},{2,1},{3,4},{4,3},{5,6},{6,5},{9,10},{10,9},{11,12},{12,11},... | collective-permute-start | bytes 245768 | tf_op jit(solution)/shard_map/ppermute | solution.py:474
  12.9 0.0 copy-done.2
  12.9 0.6 %slice.111 = s32[1]{0:T(128)} slice(s32[2]{0:T(128)S(1)} %copy-done.2), slice={[1:2]} | slice | bytes 8 | tf_op jit(solution)/shard_map/slice | solution.py:555
  14.2 0.0 copy-start.1
  14.2 0.0 copy-start.3
  14.2 0.7 %copy-done.1 = s32[2,8]{1,0:T(2,128)S(1)} copy-done((s32[2,8]{1,0:T(2,128)S(1)}, s32[2,8]{1,0:T(2,128)}, u32[]{:S(2)}) %copy-start.1) | copy-done | bytes 88
  14.9 0.0 copy-done.3
  14.9 1.6 %shard_map.77 = (f32[256,768]{1,0:T(8,128)S(1)}, f32[256,768]{1,0:T(8,128)S(1)}, bf16[8,128]{1,0:T(8,128)(2,1)S(1)}, f32[256,128]{1,0:T(8,128)S(1)}, bf16[128,128]{1,0:T(8,128)(2,1)S(1)}) custom-call(s32[2]{0:T(128)S(1)} %pad_add_fusion.place_ref, f32[2]{0:T(128)S(1)} %copy-done.3, s32[2]{0:T(128)S(1)} %copy-done.2, s32[2,8]{1,0:T(2,128)S(1)} %copy-done.1, ...), custom_call_target="tpu_custom_call" | custom-call | flops 1 | bytes 1048576 | tf_op jit(solution)/shard_map/pallas_call | solution.py:421
  16.5 0.0 collective-permute-done.33.a_ref
  16.5 0.0 collective-permute-done.34.b_ref
  16.5 9.0 %shard_map.79 = (bf16[4,256,128]{2,1,0:T(8,128)(2,1)S(1)}, f32[8,640]{1,0:T(8,128)S(1)}) custom-call(s32[2]{0:T(128)S(1)} %pad_add_fusion.place_ref, f32[256,768]{1,0:T(8,128)S(1)} %get-tuple-element.103.field_ref, f32[256,768]{1,0:T(8,128)S(1)} %get-tuple-element.104.log_ref, bf16[8,128]{1,0:T(8,128)(2,1)S(1)} %get-tuple-element.105.basis_ref, ...), custom_call_target="tpu_custom_call" | custom-call | flops 1 | bytes 1048576 | tf_op jit(solution)/shard_map/pallas_call | solution.py:421
  25.5 31.1 %conditional.1 = (bf16[1,8,128,128]{3,2,1,0:T(8,128)(2,1)}, f32[16,16]{1,0:T(8,128)}) conditional(s32[]{:T(128)} %bitcast.16, (s32[]{:T(128)}, f32[8,640]{1,0:T(8,128)S(1)}, s32[2]{0:T(128)S(1)}, f32[2]{0:T(128)S(1)}, s32[2]{0:T(128)S(1)}, /*index=5*/bf16[4,256,128]{2,1,0:T(8,128)(2,1)S(1)}) %tuple.58, (s32[]{:T(128)}, ...), branch_computations={%region_0.1_spmd, %region_1.2_spmd, %region_2.3_spmd, %region_3.4_... | conditional | flops 440712 | bytes 7992709 | solution.py:555
  25.5 5.7 %collective-permute-start.24 = (f32[1,8,640]{2,1,0:T(8,128)S(1)}, f32[1,8,640]{2,1,0:T(8,128)S(1)}, u32[]{:S(2)}, u32[]{:S(2)}) collective-permute-start(f32[1,8,640]{2,1,0:T(8,128)S(1)} %bitcast.54), channel_id=1, source_target_pairs={{0,4},{1,5},{2,6},{3,7},{4,0},{5,1},{6,2},{7,3},{8,12},{9,13},{10,... | collective-permute-start | bytes 61448 | tf_op jit(solution)/shard_map/cond/branch_3_fun/ppermute | solution.py:510
  31.2 1.8 %collective-permute-done.24 = f32[1,8,640]{2,1,0:T(8,128)S(1)} collective-permute-done((f32[1,8,640]{2,1,0:T(8,128)S(1)}, f32[1,8,640]{2,1,0:T(8,128)S(1)}, u32[]{:S(2)}, u32[]{:S(2)}) %collective-permute-start.24) | collective-permute-done | bytes 20512 | tf_op jit(solution)/shard_map/cond/branch_3_fun/ppermute | solution.py:510
  32.9 1.9 %collective-permute-start.25 = (f32[2,8,640]{2,1,0:T(8,128)S(1)}, f32[2,8,640]{2,1,0:T(8,128)S(1)}, u32[]{:S(2)}, u32[]{:S(2)}) collective-permute-start(f32[2,8,640]{2,1,0:T(8,128)S(1)} %pad_maximum_fusion.14), channel_id=1, source_target_pairs={{0,2},{1,3},{2,0},{3,1},{4,6},{5,7},{6,4},{7,5},{8,10},{9,11},{10,... | collective-permute-start | bytes 122888 | tf_op jit(solution)/shard_map/cond/branch_3_fun/ppermute | solution.py:510
  34.8 2.1 %collective-permute-done.25 = f32[2,8,640]{2,1,0:T(8,128)S(1)} collective-permute-done((f32[2,8,640]{2,1,0:T(8,128)S(1)}, f32[2,8,640]{2,1,0:T(8,128)S(1)}, u32[]{:S(2)}, u32[]{:S(2)}) %collective-permute-start.25) | collective-permute-done | bytes 40992 | tf_op jit(solution)/shard_map/cond/branch_3_fun/ppermute | solution.py:510
  36.9 2.7 %collective-permute-start.26 = (f32[4,8,640]{2,1,0:T(8,128)S(1)}, f32[4,8,640]{2,1,0:T(8,128)S(1)}, u32[]{:S(2)}, u32[]{:S(2)}) collective-permute-start(f32[4,8,640]{2,1,0:T(8,128)S(1)} %pad_maximum_fusion.13), channel_id=1, source_target_pairs={{0,1},{1,0},{2,3},{3,2},{4,5},{5,4},{6,7},{7,6},{8,9},{9,8},{10,11... | collective-permute-start | bytes 245768 | tf_op jit(solution)/shard_map/cond/branch_3_fun/ppermute | solution.py:510
  39.7 2.1 %collective-permute-start.27 = (bf16[4,256,128]{2,1,0:T(8,128)(2,1)S(1)}, bf16[4,256,128]{2,1,0:T(8,128)(2,1)S(1)}, u32[]{:S(2)}, u32[]{:S(2)}) collective-permute-start(bf16[4,256,128]{2,1,0:T(8,128)(2,1)S(1)} %get-tuple-element.88.refs_0_), channel_id=1, source_target_pairs={{0,4},{4,0},{1,5},{5,1},{2,6},{6,2},{3,7},{7,3},{8,12},{12,8},{9,1... | collective-permute-start | bytes 786440 | tf_op jit(solution)/shard_map/cond/branch_3_fun/ppermute | solution.py:502
  41.8 0.3 collective-permute-done.26
  42.1 1.5 %collective-permute-start.29 = (f32[4,16]{1,0:T(4,128)S(1)}, f32[4,16]{1,0:T(4,128)S(1)}, u32[]{:S(2)}, u32[]{:S(2)}) collective-permute-start(f32[4,16]{1,0:T(4,128)S(1)} %bitcast.62), channel_id=1, source_target_pairs={{0,8},{8,0},{1,9},{9,1},{2,10},{10,2},{3,11},{11,3},{4,12},{12,4},... | collective-permute-start | bytes 776 | tf_op jit(solution)/shard_map/cond/branch_3_fun/ppermute | solution.py:441
  43.6 0.8 %branch_3_fun.3 = (bf16[3,128,128]{2,1,0:T(8,128)(2,1)S(1)}, bf16[256,256]{1,0:T(8,128)(2,1)S(1)}, bf16[16,128]{1,0:T(8,128)(2,1)S(1)}) custom-call(s32[2]{0:T(128)S(1)} %get-tuple-element.82.place_ref, f32[2]{0:T(128)S(1)} %get-tuple-element.83.corr_ref, s32[2]{0:T(128)S(1)} %get-tuple-element.84.taper_ref), custom_call_target="tpu_custom_call" | custom-call | flops 1 | bytes 1048576 | tf_op jit(solution)/shard_map/cond/branch_3_fun/pallas_call | solution.py:421
  44.4 1.3 %collective-permute-done.29 = f32[4,16]{1,0:T(4,128)S(1)} collective-permute-done((f32[4,16]{1,0:T(4,128)S(1)}, f32[4,16]{1,0:T(4,128)S(1)}, u32[]{:S(2)}, u32[]{:S(2)}) %collective-permute-start.29) | collective-permute-done | bytes 288 | tf_op jit(solution)/shard_map/cond/branch_3_fun/ppermute | solution.py:441
  45.7 0.1 collective-permute-start.30
  45.8 0.9 %branch_3_fun.4.base_ref = f32[4,256,128]{2,1,0:T(8,128)S(1)} custom-call(s32[2]{0:T(128)S(1)} %get-tuple-element.82.place_ref, f32[2]{0:T(128)S(1)} %get-tuple-element.83.corr_ref, s32[2]{0:T(128)S(1)} %get-tuple-element.84.taper_ref, f32[8,8,640]{2,1,0:T(8,128)S(1)} %pad_maximum_fusion.12.mom_ref, bf16[3,128,128]{2,1,0:T(8,128)(2,1)S(1)} %get-tuple-element.86.mats_ref, ...), custom_call_target="tpu_custom_call" | custom-call | flops 1 | bytes 1048576 | tf_op jit(solution)/shard_map/cond/branch_3_fun/pallas_call | solution.py:421
  46.8 2.9 %collective-permute-done.27.refs_0_ = bf16[4,256,128]{2,1,0:T(8,128)(2,1)S(1)} collective-permute-done((bf16[4,256,128]{2,1,0:T(8,128)(2,1)S(1)}, bf16[4,256,128]{2,1,0:T(8,128)(2,1)S(1)}, u32[]{:S(2)}, u32[]{:S(2)}) %collective-permute-start.27) | collective-permute-done | bytes 262176 | tf_op jit(solution)/shard_map/cond/branch_3_fun/ppermute | solution.py:502
  49.6 1.1 %branch_3_fun.5 = (bf16[4,128,128]{2,1,0:T(8,128)(2,1)S(1)}, bf16[4,128,128]{2,1,0:T(8,128)(2,1)S(1)}) custom-call(s32[2]{0:T(128)S(1)} %get-tuple-element.82.place_ref, f32[4,256,128]{2,1,0:T(8,128)S(1)} %branch_3_fun.4.base_ref, bf16[3,128,128]{2,1,0:T(8,128)(2,1)S(1)} %get-tuple-element.86.mats_ref, bf16[256,256]{1,0:T(8,128)(2,1)S(1)} %get-tuple-element.89.row_ref, ...), custom_call_target="tpu_custom_call" | custom-call | flops 1 | bytes 1048576 | tf_op jit(solution)/shard_map/cond/branch_3_fun/pallas_call | solution.py:421
  50.8 1.6 %collective-permute-start.28 = (bf16[4,128,128]{2,1,0:T(8,128)(2,1)S(1)}, bf16[4,128,128]{2,1,0:T(8,128)(2,1)S(1)}, u32[]{:S(2)}, u32[]{:S(2)}) collective-permute-start(bf16[4,128,128]{2,1,0:T(8,128)(2,1)S(1)} %get-tuple-element.91), channel_id=1, source_target_pairs={{0,8},{8,0},{1,9},{9,1},{2,10},{10,2},{3,11},{11,3},{4,12},{12,4},... | collective-permute-start | bytes 393224 | tf_op jit(solution)/shard_map/cond/branch_3_fun/ppermute | solution.py:441
  52.4 0.0 collective-permute-done.30
  52.4 0.7 %copy.19 = f32[16,16]{1,0:T(8,128)} copy(f32[16,16]{0,1:T(8,128)S(1)} %maximum_bitcast_fusion.7) | data formatting | bytes 2048 | tf_op jit(solution)/shard_map/cond | solution.py:555
  53.1 2.7 %collective-permute-done.28 = bf16[4,128,128]{2,1,0:T(8,128)(2,1)S(1)} collective-permute-done((bf16[4,128,128]{2,1,0:T(8,128)(2,1)S(1)}, bf16[4,128,128]{2,1,0:T(8,128)(2,1)S(1)}, u32[]{:S(2)}, u32[]{:S(2)}) %collective-permute-start.28) | collective-permute-done | bytes 131104 | tf_op jit(solution)/shard_map/cond/branch_3_fun/ppermute | solution.py:441
  55.9 0.7 %maximum_bitcast_fusion.6 = bf16[1,8,128,128]{3,2,1,0:T(8,128)(2,1)} fusion(bf16[4,128,128]{2,1,0:T(8,128)(2,1)S(1)} %get-tuple-element.136, bf16[4,128,128]{2,1,0:T(8,128)(2,1)S(1)} %get-tuple-element.135), kind=kLoop, calls=%fused_computation.60 | loop fusion | flops 131072 | bytes 524288 | tf_op jit(solution)/shard_map/cond/branch_3_fun/broadcast_in_dim | solution.py:552
  (10 shorter events, 0.1 us)
Async XLA Ops:
  0.6 4.1 %copy-start = (f32[128,128]{1,0:T(8,128)S(1)}, f32[128,128]{1,0:T(8,128)}, u32[]{:S(2)}) copy-start(f32[128,128]{1,0:T(8,128)} %lt_ref.1) | copy-start | bytes 196612
  1.7 7.9 %collective-permute-start.31 = (bf16[4,128,128]{2,1,0:T(8,128)(2,1)S(1)}, bf16[4,128,128]{2,1,0:T(8,128)(2,1)S(1)}, u32[]{:S(2)}, u32[]{:S(2)}) collective-permute-start(bf16[4,128,128]{2,1,0:T(8,128)(2,1)S(1)} %get-tuple-element.141), channel_id=1, source_target_pairs={{0,8},{8,0},{1,9},{9,1},{2,10},{10,2},{3,11},{11,3},{4,12},{12,4},... | collective-permute-start | bytes 393224 | tf_op jit(solution)/shard_map/ppermute | solution.py:441
  4.7 4.9 %collective-permute-start.32 = (f32[128,128]{1,0:T(8,128)S(1)}, f32[128,128]{1,0:T(8,128)S(1)}, u32[]{:S(2)}, u32[]{:S(2)}) collective-permute-start(f32[128,128]{1,0:T(8,128)S(1)} %copy-done), channel_id=1, source_target_pairs={{0,8},{8,0},{1,9},{9,1},{2,10},{10,2},{3,11},{11,3},{4,12},{12,4},... | collective-permute-start | bytes 196616 | tf_op jit(solution)/shard_map/ppermute | solution.py:441
  10.5 2.5 %copy-start.2 = (s32[2]{0:T(128)S(1)}, s32[2]{0:T(128)}, u32[]{:S(2)}) copy-start(s32[2]{0:T(128)} %taper_ref.1) | copy-start | bytes 28
  10.5 6.0 %collective-permute-start.33 = (bf16[320,128]{1,0:T(8,128)(2,1)S(1)}, bf16[320,128]{1,0:T(8,128)(2,1)S(1)}, u32[]{:S(2)}, u32[]{:S(2)}) collective-permute-start(bf16[320,128]{1,0:T(8,128)(2,1)S(1)} %get-tuple-element.108), channel_id=1, source_target_pairs={{0,1},{1,0},{2,3},{3,2},{4,5},{5,4},{6,7},{7,6},{8,9},{9,8},{10,11... | collective-permute-start | bytes 245768 | tf_op jit(solution)/shard_map/ppermute | solution.py:474
  12.3 4.2 %collective-permute-start.34 = (bf16[320,128]{1,0:T(8,128)(2,1)S(1)}, bf16[320,128]{1,0:T(8,128)(2,1)S(1)}, u32[]{:S(2)}, u32[]{:S(2)}) collective-permute-start(bf16[320,128]{1,0:T(8,128)(2,1)S(1)} %get-tuple-element.109), channel_id=1, source_target_pairs={{1,2},{2,1},{3,4},{4,3},{5,6},{6,5},{9,10},{10,9},{11,12},{12,11},... | collective-permute-start | bytes 245768 | tf_op jit(solution)/shard_map/ppermute | solution.py:474
  14.2 0.7 %copy-start.1 = (s32[2,8]{1,0:T(2,128)S(1)}, s32[2,8]{1,0:T(2,128)}, u32[]{:S(2)}) copy-start(s32[2,8]{1,0:T(2,128)} %cells_ref.1) | copy-start | bytes 196
  14.2 0.7 %copy-start.3 = (f32[2]{0:T(128)S(1)}, f32[2]{0:T(128)}, u32[]{:S(2)}) copy-start(f32[2]{0:T(128)} %corr_ref.1) | copy-start | bytes 28
  25.5 7.4 %collective-permute-start.24 = (f32[1,8,640]{2,1,0:T(8,128)S(1)}, f32[1,8,640]{2,1,0:T(8,128)S(1)}, u32[]{:S(2)}, u32[]{:S(2)}) collective-permute-start(f32[1,8,640]{2,1,0:T(8,128)S(1)} %bitcast.54), channel_id=1, source_target_pairs={{0,4},{1,5},{2,6},{3,7},{4,0},{5,1},{6,2},{7,3},{8,12},{9,13},{10,... | collective-permute-start | bytes 61448 | tf_op jit(solution)/shard_map/cond/branch_3_fun/ppermute | solution.py:510
  32.9 4.0 %collective-permute-start.25 = (f32[2,8,640]{2,1,0:T(8,128)S(1)}, f32[2,8,640]{2,1,0:T(8,128)S(1)}, u32[]{:S(2)}, u32[]{:S(2)}) collective-permute-start(f32[2,8,640]{2,1,0:T(8,128)S(1)} %pad_maximum_fusion.14), channel_id=1, source_target_pairs={{0,2},{1,3},{2,0},{3,1},{4,6},{5,7},{6,4},{7,5},{8,10},{9,11},{10,... | collective-permute-start | bytes 122888 | tf_op jit(solution)/shard_map/cond/branch_3_fun/ppermute | solution.py:510
  36.9 5.2 %collective-permute-start.26 = (f32[4,8,640]{2,1,0:T(8,128)S(1)}, f32[4,8,640]{2,1,0:T(8,128)S(1)}, u32[]{:S(2)}, u32[]{:S(2)}) collective-permute-start(f32[4,8,640]{2,1,0:T(8,128)S(1)} %pad_maximum_fusion.13), channel_id=1, source_target_pairs={{0,1},{1,0},{2,3},{3,2},{4,5},{5,4},{6,7},{7,6},{8,9},{9,8},{10,11... | collective-permute-start | bytes 245768 | tf_op jit(solution)/shard_map/cond/branch_3_fun/ppermute | solution.py:510
  39.7 10.0 %collective-permute-start.27 = (bf16[4,256,128]{2,1,0:T(8,128)(2,1)S(1)}, bf16[4,256,128]{2,1,0:T(8,128)(2,1)S(1)}, u32[]{:S(2)}, u32[]{:S(2)}) collective-permute-start(bf16[4,256,128]{2,1,0:T(8,128)(2,1)S(1)} %get-tuple-element.88.refs_0_), channel_id=1, source_target_pairs={{0,4},{4,0},{1,5},{5,1},{2,6},{6,2},{3,7},{7,3},{8,12},{12,8},{9,1... | collective-permute-start | bytes 786440 | tf_op jit(solution)/shard_map/cond/branch_3_fun/ppermute | solution.py:502
  42.1 3.6 %collective-permute-start.29 = (f32[4,16]{1,0:T(4,128)S(1)}, f32[4,16]{1,0:T(4,128)S(1)}, u32[]{:S(2)}, u32[]{:S(2)}) collective-permute-start(f32[4,16]{1,0:T(4,128)S(1)} %bitcast.62), channel_id=1, source_target_pairs={{0,8},{8,0},{1,9},{9,1},{2,10},{10,2},{3,11},{11,3},{4,12},{12,4},... | collective-permute-start | bytes 776 | tf_op jit(solution)/shard_map/cond/branch_3_fun/ppermute | solution.py:441
  45.7 6.7 %collective-permute-start.30 = (f32[8,16]{1,0:T(8,128)S(1)}, f32[8,16]{1,0:T(8,128)S(1)}, u32[]{:S(2)}, u32[]{:S(2)}) collective-permute-start(f32[8,16]{1,0:T(8,128)S(1)} %pad_maximum_fusion.15), channel_id=1, source_target_pairs={{0,16},{16,0},{1,17},{17,1},{2,18},{18,2},{3,19},{19,3},{4,20},{20... | collective-permute-start | bytes 1544 | tf_op jit(solution)/shard_map/cond/branch_3_fun/ppermute | solution.py:441
  50.8 5.0 %collective-permute-start.28 = (bf16[4,128,128]{2,1,0:T(8,128)(2,1)S(1)}, bf16[4,128,128]{2,1,0:T(8,128)(2,1)S(1)}, u32[]{:S(2)}, u32[]{:S(2)}) collective-permute-start(bf16[4,128,128]{2,1,0:T(8,128)(2,1)S(1)} %get-tuple-element.91), channel_id=1, source_target_pairs={{0,8},{8,0},{1,9},{9,1},{2,10},{10,2},{3,11},{11,3},{4,12},{12,4},... | collective-permute-start | bytes 393224 | tf_op jit(solution)/shard_map/cond/branch_3_fun/ppermute | solution.py:441

commit v5 on v4

--- a/solution.py
+++ b/solution.py
@@ -505,12 +505,13 @@
             [((3, LANES, LANES), BF16), ((total_rows, total_rows), BF16), ((16, LANES), BF16)],
         )
         gathered, offsets = moments[None], [0]
-        step = col_count // 2
-        while step:
+        steps = [1 << i for i in range(col_count.bit_length() - 1)][::-1]
+        if distance == 3:
+            steps[-2:] = steps[:-3:-1]
+        for step in steps:
             moved = lax.ppermute(gathered, "col", [(i, i ^ step) for i in range(col_count)])
             gathered = jnp.concatenate([gathered, moved], axis=0)
             offsets = offsets + [offset ^ step for offset in offsets]
-            step //= 2
         samples = [gathered[i, :wells, -LANES:] for i in range(col_count)]
         while len(samples) > 1:
             samples = [a + b for a, b in zip(samples[::2], samples[1::2])]

time: 56.8 us -> 56.8 us (level)
  no operation moved by 1% of the time
where the time goes in v5:
time: 56.8 us; the launch traced here: 56.6 us
  starting transfers between devices  21.1 us (37%)
  waiting for transfers between devices  15.8 us (28%)
  Pallas kernels  14.4 us (25%)
  local copies, waits for them, and re-layouts  2.95 us (5%)
  between operations  1.39 us (2%)
  other arithmetic  0.89 us (2%)
    pallas_call x7, Pallas kernels, call(): pl.pallas_call(kernel, in_specs=[SMEM] * len(smem) + [whole] * len(vmem),...  14.4 us
    ppermute x3, starting transfers between devices, finish(): lax.ppermute(gathered, 'col', [(i, i ^ step) for i in range(col_count)])  10.3 us
    ppermute x5, waiting for transfers between devices, exchanged(): return lax.ppermute(value, axis, [(0, 1), (1, 0)])  8.73 us
    ppermute x5, starting transfers between devices, exchanged(): return lax.ppermute(value, axis, [(0, 1), (1, 0)])  6.29 us
    ppermute x3, waiting for transfers between devices, finish(): lax.ppermute(gathered, 'col', [(i, i ^ step) for i in range(col_count)])  4.18 us
    ppermute x1, waiting for transfers between devices, finish(): lax.ppermute(part, 'col', pairs)  2.89 us
    ppermute x2, starting transfers between devices, local(): lax.ppermute(value, 'col', pairs_at(col_count, 1, odd))  2.43 us
    ppermute x1, starting transfers between devices, finish(): lax.ppermute(part, 'col', pairs)  2.09 us
  transfers between devices with their start and end apart: 11, of which 7 were waited for; matrix products, arithmetic and copies ran while one was open for 2% of the time, Pallas kernels for 8%

profile of v5, /device:TPU:0, one launch (start us, length us, event | category | flops | bytes accessed | tf_op | source)
XLA Modules:
  0.0 56.6 jit_solution(17439028248918797587)
XLA Ops:
  0.6 0.0 copy-start
  0.6 1.0 %dynamic-slice_bitcast_fusion = (bf16[4,128,128]{2,1,0:T(8,128)(2,1)S(1)}, bf16[4,128,128]{2,1,0:T(8,128)(2,1)S(1)}) fusion(bf16[1,8,128,128]{3,2,1,0:T(8,128)(2,1)} %param.13, s32[]{:T(128)S(6)} %select_n.133, s32[]{:T(128)S(6)} %select_n.132), kind=kLoop, calls=%fused_computation.80 | loop fusion | bytes 524296 | tf_op jit(solution)/shard_map/dynamic_slice | solution.py:458
  1.7 3.0 %collective-permute-start.31 = (bf16[4,128,128]{2,1,0:T(8,128)(2,1)S(1)}, bf16[4,128,128]{2,1,0:T(8,128)(2,1)S(1)}, u32[]{:S(2)}, u32[]{:S(2)}) collective-permute-start(bf16[4,128,128]{2,1,0:T(8,128)(2,1)S(1)} %get-tuple-element.141), channel_id=1, source_target_pairs={{0,8},{8,0},{1,9},{9,1},{2,10},{10,2},{3,11},{11,3},{4,12},{12,4},... | collective-permute-start | bytes 393224 | tf_op jit(solution)/shard_map/ppermute | solution.py:441
  4.7 0.0 copy-done
  4.7 0.1 collective-permute-start.32
  4.8 0.1 pad_add_fusion.place_ref
  4.9 4.7 %collective-permute-done.32.refs_3_ = f32[128,128]{1,0:T(8,128)S(1)} collective-permute-done((f32[128,128]{1,0:T(8,128)S(1)}, f32[128,128]{1,0:T(8,128)S(1)}, u32[]{:S(2)}, u32[]{:S(2)}) %collective-permute-start.32) | collective-permute-done | bytes 65568 | tf_op jit(solution)/shard_map/ppermute | solution.py:441
  9.6 0.0 collective-permute-done.31.refs_2_
  9.6 0.9 %shard_map.78 = (bf16[320,128]{1,0:T(8,128)(2,1)S(1)}, bf16[320,128]{1,0:T(8,128)(2,1)S(1)}) custom-call(s32[2]{0:T(128)S(1)} %pad_add_fusion.place_ref, bf16[4,128,128]{2,1,0:T(8,128)(2,1)S(1)} %get-tuple-element.142.refs_0_, bf16[3,128,128]{2,1,0:T(8,128)(2,1)S(1)} %shard_map.76.refs_1_, bf16[4,128,128]{2,1,0:T(8,128)(2,1)S(1)} %collective-permute-done.31.refs_2_, ...), custom_call_target="tpu_custom_call" | custom-call | flops 1 | bytes 1048576 | tf_op jit(solution)/shard_map/pallas_call | solution.py:421
  10.5 0.0 copy-start.2
  10.5 1.8 %collective-permute-start.33 = (bf16[320,128]{1,0:T(8,128)(2,1)S(1)}, bf16[320,128]{1,0:T(8,128)(2,1)S(1)}, u32[]{:S(2)}, u32[]{:S(2)}) collective-permute-start(bf16[320,128]{1,0:T(8,128)(2,1)S(1)} %get-tuple-element.108), channel_id=1, source_target_pairs={{0,1},{1,0},{2,3},{3,2},{4,5},{5,4},{6,7},{7,6},{8,9},{9,8},{10,11... | collective-permute-start | bytes 245768 | tf_op jit(solution)/shard_map/ppermute | solution.py:474
  12.3 0.7 %collective-permute-start.34 = (bf16[320,128]{1,0:T(8,128)(2,1)S(1)}, bf16[320,128]{1,0:T(8,128)(2,1)S(1)}, u32[]{:S(2)}, u32[]{:S(2)}) collective-permute-start(bf16[320,128]{1,0:T(8,128)(2,1)S(1)} %get-tuple-element.109), channel_id=1, source_target_pairs={{1,2},{2,1},{3,4},{4,3},{5,6},{6,5},{9,10},{10,9},{11,12},{12,11},... | collective-permute-start | bytes 245768 | tf_op jit(solution)/shard_map/ppermute | solution.py:474
  12.9 0.0 copy-done.2
  12.9 0.6 %slice.111 = s32[1]{0:T(128)} slice(s32[2]{0:T(128)S(1)} %copy-done.2), slice={[1:2]} | slice | bytes 8 | tf_op jit(solution)/shard_map/slice | solution.py:556
  14.2 0.0 copy-start.1
  14.2 0.0 copy-start.3
  14.2 0.7 %copy-done.1 = s32[2,8]{1,0:T(2,128)S(1)} copy-done((s32[2,8]{1,0:T(2,128)S(1)}, s32[2,8]{1,0:T(2,128)}, u32[]{:S(2)}) %copy-start.1) | copy-done | bytes 88
  14.9 0.0 copy-done.3
  14.9 1.6 %shard_map.77 = (f32[256,768]{1,0:T(8,128)S(1)}, f32[256,768]{1,0:T(8,128)S(1)}, bf16[8,128]{1,0:T(8,128)(2,1)S(1)}, f32[256,128]{1,0:T(8,128)S(1)}, bf16[128,128]{1,0:T(8,128)(2,1)S(1)}) custom-call(s32[2]{0:T(128)S(1)} %pad_add_fusion.place_ref, f32[2]{0:T(128)S(1)} %copy-done.3, s32[2]{0:T(128)S(1)} %copy-done.2, s32[2,8]{1,0:T(2,128)S(1)} %copy-done.1, ...), custom_call_target="tpu_custom_call" | custom-call | flops 1 | bytes 1048576 | tf_op jit(solution)/shard_map/pallas_call | solution.py:421
  16.5 0.0 collective-permute-done.33.a_ref
  16.5 0.0 collective-permute-done.34.b_ref
  16.5 9.0 %shard_map.79 = (bf16[4,256,128]{2,1,0:T(8,128)(2,1)S(1)}, f32[8,640]{1,0:T(8,128)S(1)}) custom-call(s32[2]{0:T(128)S(1)} %pad_add_fusion.place_ref, f32[256,768]{1,0:T(8,128)S(1)} %get-tuple-element.103.field_ref, f32[256,768]{1,0:T(8,128)S(1)} %get-tuple-element.104.log_ref, bf16[8,128]{1,0:T(8,128)(2,1)S(1)} %get-tuple-element.105.basis_ref, ...), custom_call_target="tpu_custom_call" | custom-call | flops 1 | bytes 1048576 | tf_op jit(solution)/shard_map/pallas_call | solution.py:421
  25.5 31.1 %conditional.1 = (bf16[1,8,128,128]{3,2,1,0:T(8,128)(2,1)}, f32[16,16]{1,0:T(8,128)}) conditional(s32[]{:T(128)} %bitcast.16, (s32[]{:T(128)}, f32[8,640]{1,0:T(8,128)S(1)}, s32[2]{0:T(128)S(1)}, f32[2]{0:T(128)S(1)}, s32[2]{0:T(128)S(1)}, /*index=5*/bf16[4,256,128]{2,1,0:T(8,128)(2,1)S(1)}) %tuple.58, (s32[]{:T(128)}, ...), branch_computations={%region_0.1_spmd, %region_1.2_spmd, %region_2.3_spmd, %region_3.4_... | conditional | flops 440712 | bytes 7992709 | solution.py:556
  25.5 5.7 %collective-permute-start.24 = (f32[1,8,640]{2,1,0:T(8,128)S(1)}, f32[1,8,640]{2,1,0:T(8,128)S(1)}, u32[]{:S(2)}, u32[]{:S(2)}) collective-permute-start(f32[1,8,640]{2,1,0:T(8,128)S(1)} %bitcast.54), channel_id=1, source_target_pairs={{0,4},{1,5},{2,6},{3,7},{4,0},{5,1},{6,2},{7,3},{8,12},{9,13},{10,... | collective-permute-start | bytes 61448 | tf_op jit(solution)/shard_map/cond/branch_3_fun/ppermute | solution.py:512
  31.2 1.8 %collective-permute-done.24 = f32[1,8,640]{2,1,0:T(8,128)S(1)} collective-permute-done((f32[1,8,640]{2,1,0:T(8,128)S(1)}, f32[1,8,640]{2,1,0:T(8,128)S(1)}, u32[]{:S(2)}, u32[]{:S(2)}) %collective-permute-start.24) | collective-permute-done | bytes 20512 | tf_op jit(solution)/shard_map/cond/branch_3_fun/ppermute | solution.py:512
  32.9 1.9 %collective-permute-start.25 = (f32[2,8,640]{2,1,0:T(8,128)S(1)}, f32[2,8,640]{2,1,0:T(8,128)S(1)}, u32[]{:S(2)}, u32[]{:S(2)}) collective-permute-start(f32[2,8,640]{2,1,0:T(8,128)S(1)} %pad_maximum_fusion.14), channel_id=1, source_target_pairs={{0,2},{1,3},{2,0},{3,1},{4,6},{5,7},{6,4},{7,5},{8,10},{9,11},{10,... | collective-permute-start | bytes 122888 | tf_op jit(solution)/shard_map/cond/branch_3_fun/ppermute | solution.py:512
  34.8 2.1 %collective-permute-done.25 = f32[2,8,640]{2,1,0:T(8,128)S(1)} collective-permute-done((f32[2,8,640]{2,1,0:T(8,128)S(1)}, f32[2,8,640]{2,1,0:T(8,128)S(1)}, u32[]{:S(2)}, u32[]{:S(2)}) %collective-permute-start.25) | collective-permute-done | bytes 40992 | tf_op jit(solution)/shard_map/cond/branch_3_fun/ppermute | solution.py:512
  36.9 2.7 %collective-permute-start.26 = (f32[4,8,640]{2,1,0:T(8,128)S(1)}, f32[4,8,640]{2,1,0:T(8,128)S(1)}, u32[]{:S(2)}, u32[]{:S(2)}) collective-permute-start(f32[4,8,640]{2,1,0:T(8,128)S(1)} %pad_maximum_fusion.13), channel_id=1, source_target_pairs={{0,1},{1,0},{2,3},{3,2},{4,5},{5,4},{6,7},{7,6},{8,9},{9,8},{10,11... | collective-permute-start | bytes 245768 | tf_op jit(solution)/shard_map/cond/branch_3_fun/ppermute | solution.py:512
  39.7 2.1 %collective-permute-start.27 = (bf16[4,256,128]{2,1,0:T(8,128)(2,1)S(1)}, bf16[4,256,128]{2,1,0:T(8,128)(2,1)S(1)}, u32[]{:S(2)}, u32[]{:S(2)}) collective-permute-start(bf16[4,256,128]{2,1,0:T(8,128)(2,1)S(1)} %get-tuple-element.88.refs_0_), channel_id=1, source_target_pairs={{0,4},{4,0},{1,5},{5,1},{2,6},{6,2},{3,7},{7,3},{8,12},{12,8},{9,1... | collective-permute-start | bytes 786440 | tf_op jit(solution)/shard_map/cond/branch_3_fun/ppermute | solution.py:502
  41.8 0.3 collective-permute-done.26
  42.1 1.5 %collective-permute-start.29 = (f32[4,16]{1,0:T(4,128)S(1)}, f32[4,16]{1,0:T(4,128)S(1)}, u32[]{:S(2)}, u32[]{:S(2)}) collective-permute-start(f32[4,16]{1,0:T(4,128)S(1)} %bitcast.62), channel_id=1, source_target_pairs={{0,8},{8,0},{1,9},{9,1},{2,10},{10,2},{3,11},{11,3},{4,12},{12,4},... | collective-permute-start | bytes 776 | tf_op jit(solution)/shard_map/cond/branch_3_fun/ppermute | solution.py:441
  43.6 0.8 %branch_3_fun.3 = (bf16[3,128,128]{2,1,0:T(8,128)(2,1)S(1)}, bf16[256,256]{1,0:T(8,128)(2,1)S(1)}, bf16[16,128]{1,0:T(8,128)(2,1)S(1)}) custom-call(s32[2]{0:T(128)S(1)} %get-tuple-element.82.place_ref, f32[2]{0:T(128)S(1)} %get-tuple-element.83.corr_ref, s32[2]{0:T(128)S(1)} %get-tuple-element.84.taper_ref), custom_call_target="tpu_custom_call" | custom-call | flops 1 | bytes 1048576 | tf_op jit(solution)/shard_map/cond/branch_3_fun/pallas_call | solution.py:421
  44.4 1.3 %collective-permute-done.29 = f32[4,16]{1,0:T(4,128)S(1)} collective-permute-done((f32[4,16]{1,0:T(4,128)S(1)}, f32[4,16]{1,0:T(4,128)S(1)}, u32[]{:S(2)}, u32[]{:S(2)}) %collective-permute-start.29) | collective-permute-done | bytes 288 | tf_op jit(solution)/shard_map/cond/branch_3_fun/ppermute | solution.py:441
  45.7 0.1 collective-permute-start.30
  45.8 0.9 %branch_3_fun.4.base_ref = f32[4,256,128]{2,1,0:T(8,128)S(1)} custom-call(s32[2]{0:T(128)S(1)} %get-tuple-element.82.place_ref, f32[2]{0:T(128)S(1)} %get-tuple-element.83.corr_ref, s32[2]{0:T(128)S(1)} %get-tuple-element.84.taper_ref, f32[8,8,640]{2,1,0:T(8,128)S(1)} %pad_maximum_fusion.12.mom_ref, bf16[3,128,128]{2,1,0:T(8,128)(2,1)S(1)} %get-tuple-element.86.mats_ref, ...), custom_call_target="tpu_custom_call" | custom-call | flops 1 | bytes 1048576 | tf_op jit(solution)/shard_map/cond/branch_3_fun/pallas_call | solution.py:421
  46.8 2.9 %collective-permute-done.27.refs_0_ = bf16[4,256,128]{2,1,0:T(8,128)(2,1)S(1)} collective-permute-done((bf16[4,256,128]{2,1,0:T(8,128)(2,1)S(1)}, bf16[4,256,128]{2,1,0:T(8,128)(2,1)S(1)}, u32[]{:S(2)}, u32[]{:S(2)}) %collective-permute-start.27) | collective-permute-done | bytes 262176 | tf_op jit(solution)/shard_map/cond/branch_3_fun/ppermute | solution.py:502
  49.6 1.1 %branch_3_fun.5 = (bf16[4,128,128]{2,1,0:T(8,128)(2,1)S(1)}, bf16[4,128,128]{2,1,0:T(8,128)(2,1)S(1)}) custom-call(s32[2]{0:T(128)S(1)} %get-tuple-element.82.place_ref, f32[4,256,128]{2,1,0:T(8,128)S(1)} %branch_3_fun.4.base_ref, bf16[3,128,128]{2,1,0:T(8,128)(2,1)S(1)} %get-tuple-element.86.mats_ref, bf16[256,256]{1,0:T(8,128)(2,1)S(1)} %get-tuple-element.89.row_ref, ...), custom_call_target="tpu_custom_call" | custom-call | flops 1 | bytes 1048576 | tf_op jit(solution)/shard_map/cond/branch_3_fun/pallas_call | solution.py:421
  50.8 1.6 %collective-permute-start.28 = (bf16[4,128,128]{2,1,0:T(8,128)(2,1)S(1)}, bf16[4,128,128]{2,1,0:T(8,128)(2,1)S(1)}, u32[]{:S(2)}, u32[]{:S(2)}) collective-permute-start(bf16[4,128,128]{2,1,0:T(8,128)(2,1)S(1)} %get-tuple-element.91), channel_id=1, source_target_pairs={{0,8},{8,0},{1,9},{9,1},{2,10},{10,2},{3,11},{11,3},{4,12},{12,4},... | collective-permute-start | bytes 393224 | tf_op jit(solution)/shard_map/cond/branch_3_fun/ppermute | solution.py:441
  52.4 0.0 collective-permute-done.30
  52.4 0.7 %copy.19 = f32[16,16]{1,0:T(8,128)} copy(f32[16,16]{0,1:T(8,128)S(1)} %maximum_bitcast_fusion.7) | data formatting | bytes 2048 | tf_op jit(solution)/shard_map/cond | solution.py:556
  53.1 2.7 %collective-permute-done.28 = bf16[4,128,128]{2,1,0:T(8,128)(2,1)S(1)} collective-permute-done((bf16[4,128,128]{2,1,0:T(8,128)(2,1)S(1)}, bf16[4,128,128]{2,1,0:T(8,128)(2,1)S(1)}, u32[]{:S(2)}, u32[]{:S(2)}) %collective-permute-start.28) | collective-permute-done | bytes 131104 | tf_op jit(solution)/shard_map/cond/branch_3_fun/ppermute | solution.py:441
  55.9 0.7 %maximum_bitcast_fusion.6 = bf16[1,8,128,128]{3,2,1,0:T(8,128)(2,1)} fusion(bf16[4,128,128]{2,1,0:T(8,128)(2,1)S(1)} %get-tuple-element.136, bf16[4,128,128]{2,1,0:T(8,128)(2,1)S(1)} %get-tuple-element.135), kind=kLoop, calls=%fused_computation.60 | loop fusion | flops 131072 | bytes 524288 | tf_op jit(solution)/shard_map/cond/branch_3_fun/broadcast_in_dim | solution.py:553
  (10 shorter events, 0.1 us)
Async XLA Ops:
  0.6 4.1 %copy-start = (f32[128,128]{1,0:T(8,128)S(1)}, f32[128,128]{1,0:T(8,128)}, u32[]{:S(2)}) copy-start(f32[128,128]{1,0:T(8,128)} %lt_ref.1) | copy-start | bytes 196612
  1.7 7.9 %collective-permute-start.31 = (bf16[4,128,128]{2,1,0:T(8,128)(2,1)S(1)}, bf16[4,128,128]{2,1,0:T(8,128)(2,1)S(1)}, u32[]{:S(2)}, u32[]{:S(2)}) collective-permute-start(bf16[4,128,128]{2,1,0:T(8,128)(2,1)S(1)} %get-tuple-element.141), channel_id=1, source_target_pairs={{0,8},{8,0},{1,9},{9,1},{2,10},{10,2},{3,11},{11,3},{4,12},{12,4},... | collective-permute-start | bytes 393224 | tf_op jit(solution)/shard_map/ppermute | solution.py:441
  4.7 4.9 %collective-permute-start.32 = (f32[128,128]{1,0:T(8,128)S(1)}, f32[128,128]{1,0:T(8,128)S(1)}, u32[]{:S(2)}, u32[]{:S(2)}) collective-permute-start(f32[128,128]{1,0:T(8,128)S(1)} %copy-done), channel_id=1, source_target_pairs={{0,8},{8,0},{1,9},{9,1},{2,10},{10,2},{3,11},{11,3},{4,12},{12,4},... | collective-permute-start | bytes 196616 | tf_op jit(solution)/shard_map/ppermute | solution.py:441
  10.5 2.5 %copy-start.2 = (s32[2]{0:T(128)S(1)}, s32[2]{0:T(128)}, u32[]{:S(2)}) copy-start(s32[2]{0:T(128)} %taper_ref.1) | copy-start | bytes 28
  10.5 6.0 %collective-permute-start.33 = (bf16[320,128]{1,0:T(8,128)(2,1)S(1)}, bf16[320,128]{1,0:T(8,128)(2,1)S(1)}, u32[]{:S(2)}, u32[]{:S(2)}) collective-permute-start(bf16[320,128]{1,0:T(8,128)(2,1)S(1)} %get-tuple-element.108), channel_id=1, source_target_pairs={{0,1},{1,0},{2,3},{3,2},{4,5},{5,4},{6,7},{7,6},{8,9},{9,8},{10,11... | collective-permute-start | bytes 245768 | tf_op jit(solution)/shard_map/ppermute | solution.py:474
  12.3 4.2 %collective-permute-start.34 = (bf16[320,128]{1,0:T(8,128)(2,1)S(1)}, bf16[320,128]{1,0:T(8,128)(2,1)S(1)}, u32[]{:S(2)}, u32[]{:S(2)}) collective-permute-start(bf16[320,128]{1,0:T(8,128)(2,1)S(1)} %get-tuple-element.109), channel_id=1, source_target_pairs={{1,2},{2,1},{3,4},{4,3},{5,6},{6,5},{9,10},{10,9},{11,12},{12,11},... | collective-permute-start | bytes 245768 | tf_op jit(solution)/shard_map/ppermute | solution.py:474
  14.2 0.7 %copy-start.1 = (s32[2,8]{1,0:T(2,128)S(1)}, s32[2,8]{1,0:T(2,128)}, u32[]{:S(2)}) copy-start(s32[2,8]{1,0:T(2,128)} %cells_ref.1) | copy-start | bytes 196
  14.2 0.7 %copy-start.3 = (f32[2]{0:T(128)S(1)}, f32[2]{0:T(128)}, u32[]{:S(2)}) copy-start(f32[2]{0:T(128)} %corr_ref.1) | copy-start | bytes 28
  25.5 7.4 %collective-permute-start.24 = (f32[1,8,640]{2,1,0:T(8,128)S(1)}, f32[1,8,640]{2,1,0:T(8,128)S(1)}, u32[]{:S(2)}, u32[]{:S(2)}) collective-permute-start(f32[1,8,640]{2,1,0:T(8,128)S(1)} %bitcast.54), channel_id=1, source_target_pairs={{0,4},{1,5},{2,6},{3,7},{4,0},{5,1},{6,2},{7,3},{8,12},{9,13},{10,... | collective-permute-start | bytes 61448 | tf_op jit(solution)/shard_map/cond/branch_3_fun/ppermute | solution.py:512
  32.9 4.0 %collective-permute-start.25 = (f32[2,8,640]{2,1,0:T(8,128)S(1)}, f32[2,8,640]{2,1,0:T(8,128)S(1)}, u32[]{:S(2)}, u32[]{:S(2)}) collective-permute-start(f32[2,8,640]{2,1,0:T(8,128)S(1)} %pad_maximum_fusion.14), channel_id=1, source_target_pairs={{0,2},{1,3},{2,0},{3,1},{4,6},{5,7},{6,4},{7,5},{8,10},{9,11},{10,... | collective-permute-start | bytes 122888 | tf_op jit(solution)/shard_map/cond/branch_3_fun/ppermute | solution.py:512
  36.9 5.2 %collective-permute-start.26 = (f32[4,8,640]{2,1,0:T(8,128)S(1)}, f32[4,8,640]{2,1,0:T(8,128)S(1)}, u32[]{:S(2)}, u32[]{:S(2)}) collective-permute-start(f32[4,8,640]{2,1,0:T(8,128)S(1)} %pad_maximum_fusion.13), channel_id=1, source_target_pairs={{0,1},{1,0},{2,3},{3,2},{4,5},{5,4},{6,7},{7,6},{8,9},{9,8},{10,11... | collective-permute-start | bytes 245768 | tf_op jit(solution)/shard_map/cond/branch_3_fun/ppermute | solution.py:512
  39.7 10.0 %collective-permute-start.27 = (bf16[4,256,128]{2,1,0:T(8,128)(2,1)S(1)}, bf16[4,256,128]{2,1,0:T(8,128)(2,1)S(1)}, u32[]{:S(2)}, u32[]{:S(2)}) collective-permute-start(bf16[4,256,128]{2,1,0:T(8,128)(2,1)S(1)} %get-tuple-element.88.refs_0_), channel_id=1, source_target_pairs={{0,4},{4,0},{1,5},{5,1},{2,6},{6,2},{3,7},{7,3},{8,12},{12,8},{9,1... | collective-permute-start | bytes 786440 | tf_op jit(solution)/shard_map/cond/branch_3_fun/ppermute | solution.py:502
  42.1 3.6 %collective-permute-start.29 = (f32[4,16]{1,0:T(4,128)S(1)}, f32[4,16]{1,0:T(4,128)S(1)}, u32[]{:S(2)}, u32[]{:S(2)}) collective-permute-start(f32[4,16]{1,0:T(4,128)S(1)} %bitcast.62), channel_id=1, source_target_pairs={{0,8},{8,0},{1,9},{9,1},{2,10},{10,2},{3,11},{11,3},{4,12},{12,4},... | collective-permute-start | bytes 776 | tf_op jit(solution)/shard_map/cond/branch_3_fun/ppermute | solution.py:441
  45.7 6.7 %collective-permute-start.30 = (f32[8,16]{1,0:T(8,128)S(1)}, f32[8,16]{1,0:T(8,128)S(1)}, u32[]{:S(2)}, u32[]{:S(2)}) collective-permute-start(f32[8,16]{1,0:T(8,128)S(1)} %pad_maximum_fusion.15), channel_id=1, source_target_pairs={{0,16},{16,0},{1,17},{17,1},{2,18},{18,2},{3,19},{19,3},{4,20},{20... | collective-permute-start | bytes 1544 | tf_op jit(solution)/shard_map/cond/branch_3_fun/ppermute | solution.py:441
  50.8 5.0 %collective-permute-start.28 = (bf16[4,128,128]{2,1,0:T(8,128)(2,1)S(1)}, bf16[4,128,128]{2,1,0:T(8,128)(2,1)S(1)}, u32[]{:S(2)}, u32[]{:S(2)}) collective-permute-start(bf16[4,128,128]{2,1,0:T(8,128)(2,1)S(1)} %get-tuple-element.91), channel_id=1, source_target_pairs={{0,8},{8,0},{1,9},{9,1},{2,10},{10,2},{3,11},{11,3},{4,12},{12,4},... | collective-permute-start | bytes 393224 | tf_op jit(solution)/shard_map/cond/branch_3_fun/ppermute | solution.py:441

commit v6 on v5

--- a/solution.py
+++ b/solution.py
@@ -403,14 +403,21 @@
         mixed = base_ref[w]
         for i in range(tiles):
             mixed = mixed + dot(refs[i][w], mats_ref[1 + i])
-        field = dot(row_ref[...], mixed.astype(BF16)).astype(BF16)
+        mixed = mixed.astype(BF16)
         if swapped:
             half = rows // 2
-            keep = place_ref[0] == 0
-            out_refs[0][w] = jnp.where(keep, field[:half], field[half:])
-            out_refs[1][w] = jnp.where(keep, field[half:], field[:half])
+            other = pl.multiple_of((1 - place_ref[0]) * half, half)
+            out_refs[0][w] = dot(row_ref[pl.ds(other, half), :], mixed).astype(BF16)
+            out_refs[1][w] = mixed
         else:
-            out_refs[0][w] = field
+            out_refs[0][w] = dot(row_ref[...], mixed).astype(BF16)
+
+
+def keep_kernel(place_ref, mixed_ref, row_ref, out_ref):
+    half = out_ref.shape[1]
+    mine = pl.multiple_of(place_ref[0] * half, half)
+    for w in range(mixed_ref.shape[0]):
+        out_ref[w] = dot(row_ref[pl.ds(mine, half), :], mixed_ref[w]).astype(BF16)
 
 
 VMEM = pl.BlockSpec(memory_space=pltpu.VMEM)
@@ -538,11 +545,12 @@
             fields = call(
                 functools.partial(mix_kernel, swapped, len(borders)), (place,),
                 (base, mats, row_mix, *received),
-                [(half, BF16)] * 2 if swapped else [(piece, BF16)],
+                [(half, BF16), (piece, BF16)] if swapped else [(piece, BF16)],
             )
+            if swapped:
+                others.append(exchanged(fields[0], "row"))
+                fields = call(keep_kernel, (place,), (fields[1], row_mix), [(half, BF16)])
             kept.append(fields[0])
-            if swapped:
-                others.append(exchanged(fields[1], "row"))
         if swapped:
             qh_fields = jnp.concatenate(
                 [jnp.where(low, a, b) for a, b in zip(kept, others)]

time: 56.8 us -> 56.6 us (level)
  waiting for transfers between devices: 15.8 us -> 15 us
    ppermute x5, waiting for transfers between devices: 8.73 us -> 7.97 us  [exchanged(): return lax.ppermute(value, axis, [(0, 1), (1, 0)])]
    pallas_call x7 -> x8, Pallas kernels: 14.4 us -> 14.9 us  [call(): pl.pallas_call(kernel, in_specs=[SMEM] * len(smem) + [whole] * len(vmem),...]
  transfers between devices with their start and end apart: 11 -> 11, of which waited for: 7 -> 7; matrix products, arithmetic and copies ran while one was open for 2% -> 2% of each run, Pallas kernels for 8% -> 9%
where the time goes in v6:
time: 56.6 us; the launch traced here: 56.4 us
  starting transfers between devices  21.1 us (37%)
  waiting for transfers between devices  15 us (27%)
  Pallas kernels  14.9 us (26%)
  local copies, waits for them, and re-layouts  2.95 us (5%)
  between operations  1.39 us (2%)
  other arithmetic  0.89 us (2%)
    pallas_call x8, Pallas kernels, call(): pl.pallas_call(kernel, in_specs=[SMEM] * len(smem) + [whole] * len(vmem),...  14.9 us
    ppermute x3, starting transfers between devices, finish(): lax.ppermute(gathered, 'col', [(i, i ^ step) for i in range(col_count)])  10.3 us
    ppermute x5, waiting for transfers between devices, exchanged(): return lax.ppermute(value, axis, [(0, 1), (1, 0)])  7.97 us
    ppermute x5, starting transfers between devices, exchanged(): return lax.ppermute(value, axis, [(0, 1), (1, 0)])  6.29 us
    ppermute x3, waiting for transfers between devices, finish(): lax.ppermute(gathered, 'col', [(i, i ^ step) for i in range(col_count)])  4.18 us
    ppermute x1, waiting for transfers between devices, finish(): lax.ppermute(part, 'col', pairs)  2.89 us
    ppermute x2, starting transfers between devices, local(): lax.ppermute(value, 'col', pairs_at(col_count, 1, odd))  2.43 us
    ppermute x1, starting transfers between devices, finish(): lax.ppermute(part, 'col', pairs)  2.09 us
  transfers between devices with their start and end apart: 11, of which 7 were waited for; matrix products, arithmetic and copies ran while one was open for 2% of the time, Pallas kernels for 9%

profile of v6, /device:TPU:0, one launch (start us, length us, event | category | flops | bytes accessed | tf_op | source)
XLA Modules:
  0.0 56.4 jit_solution(2985760641757112632)
XLA Ops:
  0.6 0.0 copy-start
  0.6 1.0 %dynamic-slice_bitcast_fusion = (bf16[4,128,128]{2,1,0:T(8,128)(2,1)S(1)}, bf16[4,128,128]{2,1,0:T(8,128)(2,1)S(1)}) fusion(bf16[1,8,128,128]{3,2,1,0:T(8,128)(2,1)} %param.13, s32[]{:T(128)S(6)} %select_n.133, s32[]{:T(128)S(6)} %select_n.132), kind=kLoop, calls=%fused_computation.80 | loop fusion | bytes 524296 | tf_op jit(solution)/shard_map/dynamic_slice | solution.py:465
  1.7 3.0 %collective-permute-start.31 = (bf16[4,128,128]{2,1,0:T(8,128)(2,1)S(1)}, bf16[4,128,128]{2,1,0:T(8,128)(2,1)S(1)}, u32[]{:S(2)}, u32[]{:S(2)}) collective-permute-start(bf16[4,128,128]{2,1,0:T(8,128)(2,1)S(1)} %get-tuple-element.141), channel_id=1, source_target_pairs={{0,8},{8,0},{1,9},{9,1},{2,10},{10,2},{3,11},{11,3},{4,12},{12,4},... | collective-permute-start | bytes 393224 | tf_op jit(solution)/shard_map/ppermute | solution.py:448
  4.7 0.0 copy-done
  4.7 0.1 collective-permute-start.32
  4.8 0.1 pad_add_fusion.place_ref
  4.9 4.7 %collective-permute-done.32.refs_3_ = f32[128,128]{1,0:T(8,128)S(1)} collective-permute-done((f32[128,128]{1,0:T(8,128)S(1)}, f32[128,128]{1,0:T(8,128)S(1)}, u32[]{:S(2)}, u32[]{:S(2)}) %collective-permute-start.32) | collective-permute-done | bytes 65568 | tf_op jit(solution)/shard_map/ppermute | solution.py:448
  9.6 0.0 collective-permute-done.31.refs_2_
  9.6 0.9 %shard_map.78 = (bf16[320,128]{1,0:T(8,128)(2,1)S(1)}, bf16[320,128]{1,0:T(8,128)(2,1)S(1)}) custom-call(s32[2]{0:T(128)S(1)} %pad_add_fusion.place_ref, bf16[4,128,128]{2,1,0:T(8,128)(2,1)S(1)} %get-tuple-element.142.refs_0_, bf16[3,128,128]{2,1,0:T(8,128)(2,1)S(1)} %shard_map.76.refs_1_, bf16[4,128,128]{2,1,0:T(8,128)(2,1)S(1)} %collective-permute-done.31.refs_2_, ...), custom_call_target="tpu_custom_call" | custom-call | flops 1 | bytes 1048576 | tf_op jit(solution)/shard_map/pallas_call | solution.py:428
  10.5 0.0 copy-start.2
  10.5 1.8 %collective-permute-start.33 = (bf16[320,128]{1,0:T(8,128)(2,1)S(1)}, bf16[320,128]{1,0:T(8,128)(2,1)S(1)}, u32[]{:S(2)}, u32[]{:S(2)}) collective-permute-start(bf16[320,128]{1,0:T(8,128)(2,1)S(1)} %get-tuple-element.108), channel_id=1, source_target_pairs={{0,1},{1,0},{2,3},{3,2},{4,5},{5,4},{6,7},{7,6},{8,9},{9,8},{10,11... | collective-permute-start | bytes 245768 | tf_op jit(solution)/shard_map/ppermute | solution.py:481
  12.3 0.7 %collective-permute-start.34 = (bf16[320,128]{1,0:T(8,128)(2,1)S(1)}, bf16[320,128]{1,0:T(8,128)(2,1)S(1)}, u32[]{:S(2)}, u32[]{:S(2)}) collective-permute-start(bf16[320,128]{1,0:T(8,128)(2,1)S(1)} %get-tuple-element.109), channel_id=1, source_target_pairs={{1,2},{2,1},{3,4},{4,3},{5,6},{6,5},{9,10},{10,9},{11,12},{12,11},... | collective-permute-start | bytes 245768 | tf_op jit(solution)/shard_map/ppermute | solution.py:481
  12.9 0.0 copy-done.2
  12.9 0.6 %slice.111 = s32[1]{0:T(128)} slice(s32[2]{0:T(128)S(1)} %copy-done.2), slice={[1:2]} | slice | bytes 8 | tf_op jit(solution)/shard_map/slice | solution.py:564
  14.2 0.0 copy-start.1
  14.2 0.0 copy-start.3
  14.2 0.7 %copy-done.1 = s32[2,8]{1,0:T(2,128)S(1)} copy-done((s32[2,8]{1,0:T(2,128)S(1)}, s32[2,8]{1,0:T(2,128)}, u32[]{:S(2)}) %copy-start.1) | copy-done | bytes 88
  14.9 0.0 copy-done.3
  14.9 1.6 %shard_map.77 = (f32[256,768]{1,0:T(8,128)S(1)}, f32[256,768]{1,0:T(8,128)S(1)}, bf16[8,128]{1,0:T(8,128)(2,1)S(1)}, f32[256,128]{1,0:T(8,128)S(1)}, bf16[128,128]{1,0:T(8,128)(2,1)S(1)}) custom-call(s32[2]{0:T(128)S(1)} %pad_add_fusion.place_ref, f32[2]{0:T(128)S(1)} %copy-done.3, s32[2]{0:T(128)S(1)} %copy-done.2, s32[2,8]{1,0:T(2,128)S(1)} %copy-done.1, ...), custom_call_target="tpu_custom_call" | custom-call | flops 1 | bytes 1048576 | tf_op jit(solution)/shard_map/pallas_call | solution.py:428
  16.5 0.0 collective-permute-done.33.a_ref
  16.5 0.0 collective-permute-done.34.b_ref
  16.5 9.0 %shard_map.79 = (bf16[4,256,128]{2,1,0:T(8,128)(2,1)S(1)}, f32[8,640]{1,0:T(8,128)S(1)}) custom-call(s32[2]{0:T(128)S(1)} %pad_add_fusion.place_ref, f32[256,768]{1,0:T(8,128)S(1)} %get-tuple-element.103.field_ref, f32[256,768]{1,0:T(8,128)S(1)} %get-tuple-element.104.log_ref, bf16[8,128]{1,0:T(8,128)(2,1)S(1)} %get-tuple-element.105.basis_ref, ...), custom_call_target="tpu_custom_call" | custom-call | flops 1 | bytes 1048576 | tf_op jit(solution)/shard_map/pallas_call | solution.py:428
  25.5 30.9 %conditional.1 = (bf16[1,8,128,128]{3,2,1,0:T(8,128)(2,1)}, f32[16,16]{1,0:T(8,128)}) conditional(s32[]{:T(128)} %bitcast.16, (s32[]{:T(128)}, f32[8,640]{1,0:T(8,128)S(1)}, s32[2]{0:T(128)S(1)}, f32[2]{0:T(128)S(1)}, s32[2]{0:T(128)S(1)}, /*index=5*/bf16[4,256,128]{2,1,0:T(8,128)(2,1)S(1)}) %tuple.58, (s32[]{:T(128)}, ...), branch_computations={%region_0.1_spmd, %region_1.2_spmd, %region_2.3_spmd, %region_3.4_... | conditional | flops 440713 | bytes 9041285 | solution.py:564
  25.5 5.7 %collective-permute-start.24 = (f32[1,8,640]{2,1,0:T(8,128)S(1)}, f32[1,8,640]{2,1,0:T(8,128)S(1)}, u32[]{:S(2)}, u32[]{:S(2)}) collective-permute-start(f32[1,8,640]{2,1,0:T(8,128)S(1)} %bitcast.54), channel_id=1, source_target_pairs={{0,4},{1,5},{2,6},{3,7},{4,0},{5,1},{6,2},{7,3},{8,12},{9,13},{10,... | collective-permute-start | bytes 61448 | tf_op jit(solution)/shard_map/cond/branch_3_fun/ppermute | solution.py:519
  31.2 1.8 %collective-permute-done.24 = f32[1,8,640]{2,1,0:T(8,128)S(1)} collective-permute-done((f32[1,8,640]{2,1,0:T(8,128)S(1)}, f32[1,8,640]{2,1,0:T(8,128)S(1)}, u32[]{:S(2)}, u32[]{:S(2)}) %collective-permute-start.24) | collective-permute-done | bytes 20512 | tf_op jit(solution)/shard_map/cond/branch_3_fun/ppermute | solution.py:519
  32.9 1.9 %collective-permute-start.25 = (f32[2,8,640]{2,1,0:T(8,128)S(1)}, f32[2,8,640]{2,1,0:T(8,128)S(1)}, u32[]{:S(2)}, u32[]{:S(2)}) collective-permute-start(f32[2,8,640]{2,1,0:T(8,128)S(1)} %pad_maximum_fusion.14), channel_id=1, source_target_pairs={{0,2},{1,3},{2,0},{3,1},{4,6},{5,7},{6,4},{7,5},{8,10},{9,11},{10,... | collective-permute-start | bytes 122888 | tf_op jit(solution)/shard_map/cond/branch_3_fun/ppermute | solution.py:519
  34.8 2.1 %collective-permute-done.25 = f32[2,8,640]{2,1,0:T(8,128)S(1)} collective-permute-done((f32[2,8,640]{2,1,0:T(8,128)S(1)}, f32[2,8,640]{2,1,0:T(8,128)S(1)}, u32[]{:S(2)}, u32[]{:S(2)}) %collective-permute-start.25) | collective-permute-done | bytes 40992 | tf_op jit(solution)/shard_map/cond/branch_3_fun/ppermute | solution.py:519
  36.9 2.7 %collective-permute-start.26 = (f32[4,8,640]{2,1,0:T(8,128)S(1)}, f32[4,8,640]{2,1,0:T(8,128)S(1)}, u32[]{:S(2)}, u32[]{:S(2)}) collective-permute-start(f32[4,8,640]{2,1,0:T(8,128)S(1)} %pad_maximum_fusion.13), channel_id=1, source_target_pairs={{0,1},{1,0},{2,3},{3,2},{4,5},{5,4},{6,7},{7,6},{8,9},{9,8},{10,11... | collective-permute-start | bytes 245768 | tf_op jit(solution)/shard_map/cond/branch_3_fun/ppermute | solution.py:519
  39.7 2.1 %collective-permute-start.27 = (bf16[4,256,128]{2,1,0:T(8,128)(2,1)S(1)}, bf16[4,256,128]{2,1,0:T(8,128)(2,1)S(1)}, u32[]{:S(2)}, u32[]{:S(2)}) collective-permute-start(bf16[4,256,128]{2,1,0:T(8,128)(2,1)S(1)} %get-tuple-element.88.refs_0_), channel_id=1, source_target_pairs={{0,4},{4,0},{1,5},{5,1},{2,6},{6,2},{3,7},{7,3},{8,12},{12,8},{9,1... | collective-permute-start | bytes 786440 | tf_op jit(solution)/shard_map/cond/branch_3_fun/ppermute | solution.py:509
  41.8 0.3 collective-permute-done.26
  42.1 1.5 %collective-permute-start.29 = (f32[4,16]{1,0:T(4,128)S(1)}, f32[4,16]{1,0:T(4,128)S(1)}, u32[]{:S(2)}, u32[]{:S(2)}) collective-permute-start(f32[4,16]{1,0:T(4,128)S(1)} %bitcast.62), channel_id=1, source_target_pairs={{0,8},{8,0},{1,9},{9,1},{2,10},{10,2},{3,11},{11,3},{4,12},{12,4},... | collective-permute-start | bytes 776 | tf_op jit(solution)/shard_map/cond/branch_3_fun/ppermute | solution.py:448
  43.6 0.8 %branch_3_fun.4 = (bf16[3,128,128]{2,1,0:T(8,128)(2,1)S(1)}, bf16[256,256]{1,0:T(8,128)(2,1)S(1)}, bf16[16,128]{1,0:T(8,128)(2,1)S(1)}) custom-call(s32[2]{0:T(128)S(1)} %get-tuple-element.82.place_ref, f32[2]{0:T(128)S(1)} %get-tuple-element.83.corr_ref, s32[2]{0:T(128)S(1)} %get-tuple-element.84.taper_ref), custom_call_target="tpu_custom_call" | custom-call | flops 1 | bytes 1048576 | tf_op jit(solution)/shard_map/cond/branch_3_fun/pallas_call | solution.py:428
  44.4 1.3 %collective-permute-done.29 = f32[4,16]{1,0:T(4,128)S(1)} collective-permute-done((f32[4,16]{1,0:T(4,128)S(1)}, f32[4,16]{1,0:T(4,128)S(1)}, u32[]{:S(2)}, u32[]{:S(2)}) %collective-permute-start.29) | collective-permute-done | bytes 288 | tf_op jit(solution)/shard_map/cond/branch_3_fun/ppermute | solution.py:448
  45.7 0.1 collective-permute-start.30
  45.8 0.9 %branch_3_fun.5.base_ref = f32[4,256,128]{2,1,0:T(8,128)S(1)} custom-call(s32[2]{0:T(128)S(1)} %get-tuple-element.82.place_ref, f32[2]{0:T(128)S(1)} %get-tuple-element.83.corr_ref, s32[2]{0:T(128)S(1)} %get-tuple-element.84.taper_ref, f32[8,8,640]{2,1,0:T(8,128)S(1)} %pad_maximum_fusion.12.mom_ref, bf16[3,128,128]{2,1,0:T(8,128)(2,1)S(1)} %get-tuple-element.86.mats_ref, ...), custom_call_target="tpu_custom_call" | custom-call | flops 1 | bytes 1048576 | tf_op jit(solution)/shard_map/cond/branch_3_fun/pallas_call | solution.py:428
  46.8 2.9 %collective-permute-done.27.refs_0_ = bf16[4,256,128]{2,1,0:T(8,128)(2,1)S(1)} collective-permute-done((bf16[4,256,128]{2,1,0:T(8,128)(2,1)S(1)}, bf16[4,256,128]{2,1,0:T(8,128)(2,1)S(1)}, u32[]{:S(2)}, u32[]{:S(2)}) %collective-permute-start.27) | collective-permute-done | bytes 262176 | tf_op jit(solution)/shard_map/cond/branch_3_fun/ppermute | solution.py:509
  49.6 1.0 %branch_3_fun.6 = (bf16[4,128,128]{2,1,0:T(8,128)(2,1)S(1)}, bf16[4,256,128]{2,1,0:T(8,128)(2,1)S(1)}) custom-call(s32[2]{0:T(128)S(1)} %get-tuple-element.82.place_ref, f32[4,256,128]{2,1,0:T(8,128)S(1)} %branch_3_fun.5.base_ref, bf16[3,128,128]{2,1,0:T(8,128)(2,1)S(1)} %get-tuple-element.86.mats_ref, bf16[256,256]{1,0:T(8,128)(2,1)S(1)} %get-tuple-element.89.row_ref, ...), custom_call_target="tpu_custom_call" | custom-call | flops 1 | bytes 1048576 | tf_op jit(solution)/shard_map/cond/branch_3_fun/pallas_call | solution.py:428
  50.6 1.6 %collective-permute-start.28 = (bf16[4,128,128]{2,1,0:T(8,128)(2,1)S(1)}, bf16[4,128,128]{2,1,0:T(8,128)(2,1)S(1)}, u32[]{:S(2)}, u32[]{:S(2)}) collective-permute-start(bf16[4,128,128]{2,1,0:T(8,128)(2,1)S(1)} %get-tuple-element.91), channel_id=1, source_target_pairs={{0,8},{8,0},{1,9},{9,1},{2,10},{10,2},{3,11},{11,3},{4,12},{12,4},... | collective-permute-start | bytes 393224 | tf_op jit(solution)/shard_map/cond/branch_3_fun/ppermute | solution.py:448
  52.2 0.0 collective-permute-done.30
  52.2 0.7 %copy.19 = f32[16,16]{1,0:T(8,128)} copy(f32[16,16]{0,1:T(8,128)S(1)} %maximum_bitcast_fusion.7) | data formatting | bytes 2048 | tf_op jit(solution)/shard_map/cond | solution.py:564
  52.9 0.8 %branch_3_fun.7 = bf16[4,128,128]{2,1,0:T(8,128)(2,1)S(1)} custom-call(s32[2]{0:T(128)S(1)} %get-tuple-element.82.place_ref, bf16[4,256,128]{2,1,0:T(8,128)(2,1)S(1)} %get-tuple-element.90.mixed_ref, bf16[256,256]{1,0:T(8,128)(2,1)S(1)} %get-tuple-element.89.row_ref), custom_call_target="tpu_custom_call" | custom-call | flops 1 | bytes 1048576 | tf_op jit(solution)/shard_map/cond/branch_3_fun/pallas_call | solution.py:428
  53.7 2.0 %collective-permute-done.28 = bf16[4,128,128]{2,1,0:T(8,128)(2,1)S(1)} collective-permute-done((bf16[4,128,128]{2,1,0:T(8,128)(2,1)S(1)}, bf16[4,128,128]{2,1,0:T(8,128)(2,1)S(1)}, u32[]{:S(2)}, u32[]{:S(2)}) %collective-permute-start.28) | collective-permute-done | bytes 131104 | tf_op jit(solution)/shard_map/cond/branch_3_fun/ppermute | solution.py:448
  55.7 0.7 %maximum_bitcast_fusion.6 = bf16[1,8,128,128]{3,2,1,0:T(8,128)(2,1)} fusion(bf16[4,128,128]{2,1,0:T(8,128)(2,1)S(1)} %get-tuple-element.136, bf16[4,128,128]{2,1,0:T(8,128)(2,1)S(1)} %get-tuple-element.135), kind=kLoop, calls=%fused_computation.60 | loop fusion | flops 131072 | bytes 524288 | tf_op jit(solution)/shard_map/cond/branch_3_fun/broadcast_in_dim | solution.py:561
  (10 shorter events, 0.1 us)
Async XLA Ops:
  0.6 4.1 %copy-start = (f32[128,128]{1,0:T(8,128)S(1)}, f32[128,128]{1,0:T(8,128)}, u32[]{:S(2)}) copy-start(f32[128,128]{1,0:T(8,128)} %lt_ref.1) | copy-start | bytes 196612
  1.7 7.9 %collective-permute-start.31 = (bf16[4,128,128]{2,1,0:T(8,128)(2,1)S(1)}, bf16[4,128,128]{2,1,0:T(8,128)(2,1)S(1)}, u32[]{:S(2)}, u32[]{:S(2)}) collective-permute-start(bf16[4,128,128]{2,1,0:T(8,128)(2,1)S(1)} %get-tuple-element.141), channel_id=1, source_target_pairs={{0,8},{8,0},{1,9},{9,1},{2,10},{10,2},{3,11},{11,3},{4,12},{12,4},... | collective-permute-start | bytes 393224 | tf_op jit(solution)/shard_map/ppermute | solution.py:448
  4.7 4.9 %collective-permute-start.32 = (f32[128,128]{1,0:T(8,128)S(1)}, f32[128,128]{1,0:T(8,128)S(1)}, u32[]{:S(2)}, u32[]{:S(2)}) collective-permute-start(f32[128,128]{1,0:T(8,128)S(1)} %copy-done), channel_id=1, source_target_pairs={{0,8},{8,0},{1,9},{9,1},{2,10},{10,2},{3,11},{11,3},{4,12},{12,4},... | collective-permute-start | bytes 196616 | tf_op jit(solution)/shard_map/ppermute | solution.py:448
  10.5 2.5 %copy-start.2 = (s32[2]{0:T(128)S(1)}, s32[2]{0:T(128)}, u32[]{:S(2)}) copy-start(s32[2]{0:T(128)} %taper_ref.1) | copy-start | bytes 28
  10.5 6.0 %collective-permute-start.33 = (bf16[320,128]{1,0:T(8,128)(2,1)S(1)}, bf16[320,128]{1,0:T(8,128)(2,1)S(1)}, u32[]{:S(2)}, u32[]{:S(2)}) collective-permute-start(bf16[320,128]{1,0:T(8,128)(2,1)S(1)} %get-tuple-element.108), channel_id=1, source_target_pairs={{0,1},{1,0},{2,3},{3,2},{4,5},{5,4},{6,7},{7,6},{8,9},{9,8},{10,11... | collective-permute-start | bytes 245768 | tf_op jit(solution)/shard_map/ppermute | solution.py:481
  12.3 4.2 %collective-permute-start.34 = (bf16[320,128]{1,0:T(8,128)(2,1)S(1)}, bf16[320,128]{1,0:T(8,128)(2,1)S(1)}, u32[]{:S(2)}, u32[]{:S(2)}) collective-permute-start(bf16[320,128]{1,0:T(8,128)(2,1)S(1)} %get-tuple-element.109), channel_id=1, source_target_pairs={{1,2},{2,1},{3,4},{4,3},{5,6},{6,5},{9,10},{10,9},{11,12},{12,11},... | collective-permute-start | bytes 245768 | tf_op jit(solution)/shard_map/ppermute | solution.py:481
  14.2 0.7 %copy-start.1 = (s32[2,8]{1,0:T(2,128)S(1)}, s32[2,8]{1,0:T(2,128)}, u32[]{:S(2)}) copy-start(s32[2,8]{1,0:T(2,128)} %cells_ref.1) | copy-start | bytes 196
  14.2 0.7 %copy-start.3 = (f32[2]{0:T(128)S(1)}, f32[2]{0:T(128)}, u32[]{:S(2)}) copy-start(f32[2]{0:T(128)} %corr_ref.1) | copy-start | bytes 28
  25.5 7.4 %collective-permute-start.24 = (f32[1,8,640]{2,1,0:T(8,128)S(1)}, f32[1,8,640]{2,1,0:T(8,128)S(1)}, u32[]{:S(2)}, u32[]{:S(2)}) collective-permute-start(f32[1,8,640]{2,1,0:T(8,128)S(1)} %bitcast.54), channel_id=1, source_target_pairs={{0,4},{1,5},{2,6},{3,7},{4,0},{5,1},{6,2},{7,3},{8,12},{9,13},{10,... | collective-permute-start | bytes 61448 | tf_op jit(solution)/shard_map/cond/branch_3_fun/ppermute | solution.py:519
  32.9 4.0 %collective-permute-start.25 = (f32[2,8,640]{2,1,0:T(8,128)S(1)}, f32[2,8,640]{2,1,0:T(8,128)S(1)}, u32[]{:S(2)}, u32[]{:S(2)}) collective-permute-start(f32[2,8,640]{2,1,0:T(8,128)S(1)} %pad_maximum_fusion.14), channel_id=1, source_target_pairs={{0,2},{1,3},{2,0},{3,1},{4,6},{5,7},{6,4},{7,5},{8,10},{9,11},{10,... | collective-permute-start | bytes 122888 | tf_op jit(solution)/shard_map/cond/branch_3_fun/ppermute | solution.py:519
  36.9 5.2 %collective-permute-start.26 = (f32[4,8,640]{2,1,0:T(8,128)S(1)}, f32[4,8,640]{2,1,0:T(8,128)S(1)}, u32[]{:S(2)}, u32[]{:S(2)}) collective-permute-start(f32[4,8,640]{2,1,0:T(8,128)S(1)} %pad_maximum_fusion.13), channel_id=1, source_target_pairs={{0,1},{1,0},{2,3},{3,2},{4,5},{5,4},{6,7},{7,6},{8,9},{9,8},{10,11... | collective-permute-start | bytes 245768 | tf_op jit(solution)/shard_map/cond/branch_3_fun/ppermute | solution.py:519
  39.7 10.0 %collective-permute-start.27 = (bf16[4,256,128]{2,1,0:T(8,128)(2,1)S(1)}, bf16[4,256,128]{2,1,0:T(8,128)(2,1)S(1)}, u32[]{:S(2)}, u32[]{:S(2)}) collective-permute-start(bf16[4,256,128]{2,1,0:T(8,128)(2,1)S(1)} %get-tuple-element.88.refs_0_), channel_id=1, source_target_pairs={{0,4},{4,0},{1,5},{5,1},{2,6},{6,2},{3,7},{7,3},{8,12},{12,8},{9,1... | collective-permute-start | bytes 786440 | tf_op jit(solution)/shard_map/cond/branch_3_fun/ppermute | solution.py:509
  42.1 3.6 %collective-permute-start.29 = (f32[4,16]{1,0:T(4,128)S(1)}, f32[4,16]{1,0:T(4,128)S(1)}, u32[]{:S(2)}, u32[]{:S(2)}) collective-permute-start(f32[4,16]{1,0:T(4,128)S(1)} %bitcast.62), channel_id=1, source_target_pairs={{0,8},{8,0},{1,9},{9,1},{2,10},{10,2},{3,11},{11,3},{4,12},{12,4},... | collective-permute-start | bytes 776 | tf_op jit(solution)/shard_map/cond/branch_3_fun/ppermute | solution.py:448
  45.7 6.5 %collective-permute-start.30 = (f32[8,16]{1,0:T(8,128)S(1)}, f32[8,16]{1,0:T(8,128)S(1)}, u32[]{:S(2)}, u32[]{:S(2)}) collective-permute-start(f32[8,16]{1,0:T(8,128)S(1)} %pad_maximum_fusion.15), channel_id=1, source_target_pairs={{0,16},{16,0},{1,17},{17,1},{2,18},{18,2},{3,19},{19,3},{4,20},{20... | collective-permute-start | bytes 1544 | tf_op jit(solution)/shard_map/cond/branch_3_fun/ppermute | solution.py:448
  50.6 5.0 %collective-permute-start.28 = (bf16[4,128,128]{2,1,0:T(8,128)(2,1)S(1)}, bf16[4,128,128]{2,1,0:T(8,128)(2,1)S(1)}, u32[]{:S(2)}, u32[]{:S(2)}) collective-permute-start(bf16[4,128,128]{2,1,0:T(8,128)(2,1)S(1)} %get-tuple-element.91), channel_id=1, source_target_pairs={{0,8},{8,0},{1,9},{9,1},{2,10},{10,2},{3,11},{11,3},{4,12},{12,4},... | collective-permute-start | bytes 393224 | tf_op jit(solution)/shard_map/cond/branch_3_fun/ppermute | solution.py:448
